TPU v7x, 32 devices: a whole 2x2x4 slice. The times are simulated.
32 devices in a mesh: chan: 8 (over z, x), src: 4 (over y, core).
Axes of the slice: x: 2, y: 2, z: 4, core: 2. Of those that a mesh axis runs over, the one named last changes fastest.
Arguments:
- records: bfloat16 [1024, 4096], P('chan'), may hold values from -600 to 600
- virtual_sources: int32 [64], P('src'), may hold values from 0 to 1023
- pair_group: int32 [4096, 1], P(('chan', 'src')), may hold values from 0 to 7; in each aligned block of 128 rows (0 to 127, 128 to 255, ...) at most 32 rows name the same one
- pair_receiver: int32 [4096], P(('chan', 'src')), may hold values from 0 to 127
- pair_source: int32 [4096], P(('chan', 'src')), may hold values from 0 to 15
- observed: float32 [4096, 2048], P(('chan', 'src')), may hold values from -6 to 6
Outputs:
- adjoint_source: float32 [1024, 4096], P(('chan', 'src'))
- pair_misfit: float32 [4096], P(('chan', 'src'))
Inputs may be any that keep to these rules, and one draw needn't show every extreme that they name: `pair_group`: among the 128 pairs listed by one device at most 32 name the same channel group, and in every draw some device lists exactly 32 pairs for some group.
All inputs are finite; a program needn't handle non-finite values.
Results may differ from a plain program's by a relative error of at most 0.0021.
Values sent between devices are 32-bit elements; how exact they have to be, the bound alone decides.
No kernel may reach another device: no remote copies, remote signals or barrier semaphores. Data moves between devices by JAX's collectives and lax.ppermute only.
A program may use at most 64 MiB of HBM per device.

v0:
```python
import math

import jax
import jax.numpy as jnp
from jax import lax
from jax.sharding import PartitionSpec as P

K0 = 64


def fourier_basis(offset, length, time_len, bin_count):
    sample_times = offset + jnp.arange(length, dtype=jnp.int32)[:, None]
    band_bins = K0 + jnp.arange(bin_count, dtype=jnp.int32)[None, :]
    phase_index = band_bins * sample_times % (2 * time_len)
    angles = phase_index.astype(jnp.float32) * (math.pi / time_len)
    return jnp.concatenate([jnp.cos(angles), -jnp.sin(angles)], axis=1)


def forward(signal_rows, bin_count):
    time_len = signal_rows.shape[1]
    block_len = min(512, time_len)

    def add_block(block_index, running):
        offset = block_index * block_len
        segment = lax.dynamic_slice_in_dim(signal_rows, offset, block_len, 1)
        fourier_table = fourier_basis(offset, block_len, time_len, bin_count).astype(jnp.bfloat16)
        return running + jnp.dot(segment, fourier_table, preferred_element_type=jnp.float32)

    return lax.fori_loop(
        0,
        time_len // block_len,
        add_block,
        jnp.zeros((signal_rows.shape[0], 2 * bin_count), jnp.float32),
    )


def inverse(spectral, time_len):
    bin_count = spectral.shape[1] // 2
    block_len = min(512, time_len)

    def fill_block(block_index, output):
        offset = block_index * block_len
        fourier_table = fourier_basis(offset, block_len, time_len, bin_count)
        values = lax.dot_general(
            spectral,
            fourier_table,
            (((1,), (1,)), ((), ())),
            precision=lax.Precision.HIGHEST,
            preferred_element_type=jnp.float32,
        ) * (1.0 / math.sqrt(bin_count))
        return lax.dynamic_update_slice_in_dim(output, values, offset, 1)

    return lax.fori_loop(
        0, time_len // block_len, fill_block, jnp.zeros((spectral.shape[0], time_len), jnp.float32)
    )


def whiten(spectra):
    bin_count = spectra.shape[1] // 2
    band_power = jnp.sum(spectra * spectra, axis=1, keepdims=True) / bin_count
    return spectra / jnp.sqrt(band_power + 1e-06)


def band_taper(bin_count):
    band_bins = jnp.arange(bin_count, dtype=jnp.int32).astype(jnp.float32)
    return 0.5 - 0.5 * jnp.cos((band_bins + 0.5) * (2.0 * math.pi / bin_count))


def pair_terms(source_rows, receiver_rows, observed_rows):
    bin_count = observed_rows.shape[-1] // 2
    weights = band_taper(bin_count)
    source_real = source_rows[..., :bin_count]
    source_imag = source_rows[..., bin_count:]
    receiver_real = receiver_rows[..., :bin_count]
    receiver_imag = receiver_rows[..., bin_count:]
    corr_real = source_real * receiver_real + source_imag * receiver_imag
    corr_imag = source_real * receiver_imag - source_imag * receiver_real
    diff_real = corr_real - observed_rows[..., :bin_count]
    diff_imag = corr_imag - observed_rows[..., bin_count:]
    misfit = jnp.sum(weights * (diff_real * diff_real + diff_imag * diff_imag), axis=-1) / (
        2 * bin_count
    )
    resid_real = weights * diff_real
    resid_imag = weights * diff_imag
    term_real = resid_real * source_real - resid_imag * source_imag
    term_imag = resid_real * source_imag + resid_imag * source_real
    return (misfit, jnp.concatenate([term_real, term_imag], axis=-1))


def per_device(records, virtual_sources, pair_group, pair_receiver, pair_source, observed):
    row_count, time_len = records.shape
    pair_count = observed.shape[0]
    bin_count = observed.shape[1] // 2
    groups = lax.axis_size("chan")
    capacity = 2 * pair_count // groups
    slot_total = groups * capacity
    chan_index = lax.axis_index("chan")
    local_rows = virtual_sources - chan_index * row_count
    inside = (local_rows >= 0) & (local_rows < row_count)
    safe_rows = jnp.clip(local_rows, 0, row_count - 1)
    whitened = whiten(forward(records, bin_count))
    picked = jnp.where(inside[:, None], jnp.take(whitened, safe_rows, axis=0), 0.0)
    sources = lax.psum(picked, "chan")
    destination = pair_group[:, 0]
    group_hits = (destination[:, None] == jnp.arange(groups, dtype=jnp.int32)[None, :]).astype(
        jnp.int32
    )
    slot_ranks = jnp.sum((jnp.cumsum(group_hits, axis=0) - 1) * group_hits, axis=1)
    slot_index = destination * capacity + slot_ranks
    send_receiver = (
        jnp.full((slot_total,), -1, jnp.int32)
        .at[slot_index]
        .set(pair_receiver)
        .reshape(groups, capacity)
    )
    send_source = (
        jnp.zeros((slot_total,), jnp.int32)
        .at[slot_index]
        .set(pair_source)
        .reshape(groups, capacity)
    )
    send_labels = jnp.stack([send_receiver, send_source], axis=-1)
    send_observed = (
        jnp.zeros((slot_total, 2 * bin_count), jnp.float32)
        .at[slot_index]
        .set(observed)
        .reshape(groups, capacity, 2 * bin_count)
    )
    observed_slots = lax.all_to_all(send_observed, "chan", split_axis=0, concat_axis=0, tiled=True)
    label_slots = lax.all_to_all(send_labels, "chan", split_axis=0, concat_axis=0, tiled=True)
    receiver_slots = label_slots[..., 0]
    source_slots = label_slots[..., 1]
    occupied = receiver_slots >= 0
    receiver_rows = jnp.take(whitened, jnp.clip(receiver_slots, 0, row_count - 1), axis=0)
    source_rows = jnp.take(sources, jnp.clip(source_slots, 0, sources.shape[0] - 1), axis=0)
    misfit, adjoint_term = pair_terms(source_rows, receiver_rows, observed_slots)
    adjoint_term = jnp.where(occupied[..., None], adjoint_term, 0.0)
    returned = lax.all_to_all(misfit, "chan", split_axis=0, concat_axis=0, tiled=True)
    arrived_terms, receivers, returned = (adjoint_term, receiver_slots, returned)
    pair_misfit = returned.reshape(slot_total)[slot_index]
    flat_terms = arrived_terms.reshape(slot_total, 2 * bin_count)
    flat_receivers = receivers.reshape(slot_total)
    selector = (jnp.arange(row_count, dtype=jnp.int32)[:, None] == flat_receivers[None, :]).astype(
        jnp.float32
    )
    adjoint_spectra = jnp.dot(
        selector, flat_terms, precision=lax.Precision.HIGHEST, preferred_element_type=jnp.float32
    )
    adjoint_source = lax.psum_scatter(
        inverse(adjoint_spectra, time_len), "src", scatter_dimension=0, tiled=True
    )
    return (adjoint_source, pair_misfit)


def solution(mesh):
    return jax.shard_map(
        per_device,
        mesh=mesh,
        in_specs=(
            P("chan", None),
            P("src"),
            P(("chan", "src"), None),
            P(("chan", "src")),
            P(("chan", "src")),
            P(("chan", "src"), None),
        ),
        out_specs=(P(("chan", "src"), None), P(("chan", "src"))),
        check_vma=False,
    )
```

profile of v0, /device:TPU:0, one launch (start us, length us, event | category | flops | bytes accessed | tf_op | source)
XLA Modules:
  0.0 358.6 jit_solution(7600043194722808114)
XLA Ops:
  12.6 7.3 %all-to-all-start = ((s32[8,32,2]{1,2,0:T(2,128)}), s32[8,32,2]{1,2,0:T(2,128)S(1)}, u32[]{:S(2)}, u32[]{:S(2)}) async-start(s32[8,32,2]{1,2,0:T(2,128)} %pad_add_fusion), calls=%async_computation | async-start | bytes 16384 | tf_op jit(solution)/shard_map/all_to_all | solution.py:130
  19.9 84.7 %while.32 = (s32[]{:T(128)}, f32[128,2048]{1,0:T(8,128)S(1)}, bf16[128,4096]{1,0:T(8,128)(2,1)}, s32[]{:T(128)}, s32[]{:T(128)}, /*index=5*/s32[]{:T(128)}, s32[]{:T(128)}) while((s32[]{:T(128)}, f32[128,2048]{1,0:T(8,128)S(1)}, bf16[128,4096]{1,0:T(8,128)(2,1)}, s32[]{:T(128)}, s32[]{:T(128)}, /*index=5*/s32[]{:T(128)}, ...), condition=%wide.region_5.6_spmd.clone, body=%wide.region_4.5_spmd.clone.sunk | while | flops 282068480 | bytes 6434957 | solution.py:29
  19.9 9.0 %cosine_convert_fusion.2 = (bf16[512,1024]{1,0:T(8,128)(2,1)S(1)}, bf16[512,1024]{1,0:T(8,128)(2,1)S(1)}) fusion(s32[512]{0:T(512)S(1)} %iota_add_fusion.10, s32[1024]{0:T(1024)S(1)} %iota_add_fusion.11), kind=kLoop, calls=%fused_computation.40.clone.1 | loop fusion | flops 8912896 | bytes 2103296 | tf_op jit(solution)/shard_map/convert
  30.5 9.0 %cosine_convert_fusion.2 = (bf16[512,1024]{1,0:T(8,128)(2,1)S(1)}, bf16[512,1024]{1,0:T(8,128)(2,1)S(1)}) fusion(s32[512]{0:T(512)S(1)} %iota_add_fusion.10, s32[1024]{0:T(1024)S(1)} %iota_add_fusion.11), kind=kLoop, calls=%fused_computation.40.clone.1 | loop fusion | flops 8912896 | bytes 2103296 | tf_op jit(solution)/shard_map/convert
  41.1 9.0 %cosine_convert_fusion.2 = (bf16[512,1024]{1,0:T(8,128)(2,1)S(1)}, bf16[512,1024]{1,0:T(8,128)(2,1)S(1)}) fusion(s32[512]{0:T(512)S(1)} %iota_add_fusion.10, s32[1024]{0:T(1024)S(1)} %iota_add_fusion.11), kind=kLoop, calls=%fused_computation.40.clone.1 | loop fusion | flops 8912896 | bytes 2103296 | tf_op jit(solution)/shard_map/convert
  51.7 9.0 %cosine_convert_fusion.2 = (bf16[512,1024]{1,0:T(8,128)(2,1)S(1)}, bf16[512,1024]{1,0:T(8,128)(2,1)S(1)}) fusion(s32[512]{0:T(512)S(1)} %iota_add_fusion.10, s32[1024]{0:T(1024)S(1)} %iota_add_fusion.11), kind=kLoop, calls=%fused_computation.40.clone.1 | loop fusion | flops 8912896 | bytes 2103296 | tf_op jit(solution)/shard_map/convert
  62.2 9.0 %cosine_convert_fusion.2 = (bf16[512,1024]{1,0:T(8,128)(2,1)S(1)}, bf16[512,1024]{1,0:T(8,128)(2,1)S(1)}) fusion(s32[512]{0:T(512)S(1)} %iota_add_fusion.10, s32[1024]{0:T(1024)S(1)} %iota_add_fusion.11), kind=kLoop, calls=%fused_computation.40.clone.1 | loop fusion | flops 8912896 | bytes 2103296 | tf_op jit(solution)/shard_map/convert
  72.8 9.0 %cosine_convert_fusion.2 = (bf16[512,1024]{1,0:T(8,128)(2,1)S(1)}, bf16[512,1024]{1,0:T(8,128)(2,1)S(1)}) fusion(s32[512]{0:T(512)S(1)} %iota_add_fusion.10, s32[1024]{0:T(1024)S(1)} %iota_add_fusion.11), kind=kLoop, calls=%fused_computation.40.clone.1 | loop fusion | flops 8912896 | bytes 2103296 | tf_op jit(solution)/shard_map/convert
  83.4 9.0 %cosine_convert_fusion.2 = (bf16[512,1024]{1,0:T(8,128)(2,1)S(1)}, bf16[512,1024]{1,0:T(8,128)(2,1)S(1)}) fusion(s32[512]{0:T(512)S(1)} %iota_add_fusion.10, s32[1024]{0:T(1024)S(1)} %iota_add_fusion.11), kind=kLoop, calls=%fused_computation.40.clone.1 | loop fusion | flops 8912896 | bytes 2103296 | tf_op jit(solution)/shard_map/convert
  94.0 9.0 %cosine_convert_fusion.2 = (bf16[512,1024]{1,0:T(8,128)(2,1)S(1)}, bf16[512,1024]{1,0:T(8,128)(2,1)S(1)}) fusion(s32[512]{0:T(512)S(1)} %iota_add_fusion.10, s32[1024]{0:T(1024)S(1)} %iota_add_fusion.11), kind=kLoop, calls=%fused_computation.40.clone.1 | loop fusion | flops 8912896 | bytes 2103296 | tf_op jit(solution)/shard_map/convert
  107.9 6.1 %all-to-all-start.1 = ((f32[8,32,2048]{2,1,0:T(8,128)}), f32[8,32,2048]{2,1,0:T(8,128)}, u32[]{:S(2)}, u32[]{:S(2)}) async-start(f32[8,32,2048]{2,1,0:T(8,128)} %bitcast.8), calls=%async_computation.1 | async-start | bytes 4194304 | tf_op jit(solution)/shard_map/all_to_all | solution.py:129
  119.0 87.0 %all-reduce.2.cloned.1.call-done = f32[16,2048]{1,0:T(8,128)} async-done(((f32[16,2048]{1,0:T(8,128)}), f32[16,2048]{1,0:T(8,128)}) %all-reduce.2.cloned.1.call-update) | async-done | bytes 131088 | tf_op jit(solution)/shard_map/psum | solution.py:103
  206.0 4.6 %gather_fusion.1 = f32[256,2048]{1,0:T(8,128)} fusion(f32[16,2048]{1,0:T(8,128)} %all-reduce.2.cloned.1.call-done, s32[1024]{0:T(1024)S(1)} %pad_clamp_fusion.2), kind=kCustom, calls=%fused_computation.1 | custom fusion | bytes 4195328 | tf_op jit(solution)/shard_map/jit(_take)/gather | solution.py:135
  210.5 3.9 %broadcast_select_fusion = (f32[8,32,2048]{2,1,0:T(8,128)}, f32[8,32,2048]{2,1,0:T(8,128)S(1)}) fusion(f32[8,32,2048]{2,1,0:T(8,128)} %bitcast.34, pred[8,32]{1,0:T(8,128)(4,1)S(1)} %get-tuple-element.220, f32[8,32,2048]{2,1,0:T(8,128)} %bitcast.35, pred[8,32]{1,0:T(8,128)(4,1)S(1)} %and_bitcast_fusion.1), kind=kLoop, calls=%fused_computation.58 | loop fusion | flops 1048576 | bytes 8389120 | tf_op jit(solution)/shard_map/jit(_take)/select_n | solution.py:134
  220.2 101.1 %while.31 = (s32[]{:T(128)}, f32[128,4096]{1,0:T(8,128)}, f32[128,2048]{1,0:T(8,128)S(1)}, s32[]{:T(128)}, s32[]{:T(128)}, /*index=5*/s32[]{:T(128)}, s32[]{:T(128)}) while((s32[]{:T(128)}, f32[128,4096]{1,0:T(8,128)}, f32[128,2048]{1,0:T(8,128)S(1)}, s32[]{:T(128)}, s32[]{:T(128)}, /*index=5*/s32[]{:T(128)}, s32[]{:T(128)}) %tuple.92), condition=%wide.region_10.11_spmd, body=%wide.region_9.10_spmd.sunk | while | flops 1619592704 | bytes 10760323 | solution.py:53
  220.2 8.3 %fusion.50 = (f32[512,1024]{1,0:T(8,128)S(1)}, f32[512,1024]{1,0:T(8,128)S(1)}) fusion(s32[512]{0:T(512)S(1)} %iota_add_fusion.8, s32[1024]{0:T(1024)S(1)} %iota_add_fusion.9), kind=kLoop, calls=%fused_computation.22.clone.1 | loop fusion | flops 7864320 | bytes 4200448 | tf_op jit(solution)/shard_map/while/body/eval_jaxpr/cos | solution.py:16
  228.5 3.4 fusion.51
  232.9 8.3 %fusion.50 = (f32[512,1024]{1,0:T(8,128)S(1)}, f32[512,1024]{1,0:T(8,128)S(1)}) fusion(s32[512]{0:T(512)S(1)} %iota_add_fusion.8, s32[1024]{0:T(1024)S(1)} %iota_add_fusion.9), kind=kLoop, calls=%fused_computation.22.clone.1 | loop fusion | flops 7864320 | bytes 4200448 | tf_op jit(solution)/shard_map/while/body/eval_jaxpr/cos | solution.py:16
  241.2 3.4 fusion.51
  245.5 8.3 %fusion.50 = (f32[512,1024]{1,0:T(8,128)S(1)}, f32[512,1024]{1,0:T(8,128)S(1)}) fusion(s32[512]{0:T(512)S(1)} %iota_add_fusion.8, s32[1024]{0:T(1024)S(1)} %iota_add_fusion.9), kind=kLoop, calls=%fused_computation.22.clone.1 | loop fusion | flops 7864320 | bytes 4200448 | tf_op jit(solution)/shard_map/while/body/eval_jaxpr/cos | solution.py:16
  253.8 3.4 fusion.51
  258.2 8.3 %fusion.50 = (f32[512,1024]{1,0:T(8,128)S(1)}, f32[512,1024]{1,0:T(8,128)S(1)}) fusion(s32[512]{0:T(512)S(1)} %iota_add_fusion.8, s32[1024]{0:T(1024)S(1)} %iota_add_fusion.9), kind=kLoop, calls=%fused_computation.22.clone.1 | loop fusion | flops 7864320 | bytes 4200448 | tf_op jit(solution)/shard_map/while/body/eval_jaxpr/cos | solution.py:16
  266.5 3.4 fusion.51
  270.8 8.3 %fusion.50 = (f32[512,1024]{1,0:T(8,128)S(1)}, f32[512,1024]{1,0:T(8,128)S(1)}) fusion(s32[512]{0:T(512)S(1)} %iota_add_fusion.8, s32[1024]{0:T(1024)S(1)} %iota_add_fusion.9), kind=kLoop, calls=%fused_computation.22.clone.1 | loop fusion | flops 7864320 | bytes 4200448 | tf_op jit(solution)/shard_map/while/body/eval_jaxpr/cos | solution.py:16
  279.1 3.4 fusion.51
  283.4 8.3 %fusion.50 = (f32[512,1024]{1,0:T(8,128)S(1)}, f32[512,1024]{1,0:T(8,128)S(1)}) fusion(s32[512]{0:T(512)S(1)} %iota_add_fusion.8, s32[1024]{0:T(1024)S(1)} %iota_add_fusion.9), kind=kLoop, calls=%fused_computation.22.clone.1 | loop fusion | flops 7864320 | bytes 4200448 | tf_op jit(solution)/shard_map/while/body/eval_jaxpr/cos | solution.py:16
  296.1 8.3 %fusion.50 = (f32[512,1024]{1,0:T(8,128)S(1)}, f32[512,1024]{1,0:T(8,128)S(1)}) fusion(s32[512]{0:T(512)S(1)} %iota_add_fusion.8, s32[1024]{0:T(1024)S(1)} %iota_add_fusion.9), kind=kLoop, calls=%fused_computation.22.clone.1 | loop fusion | flops 7864320 | bytes 4200448 | tf_op jit(solution)/shard_map/while/body/eval_jaxpr/cos | solution.py:16
  308.7 8.3 %fusion.50 = (f32[512,1024]{1,0:T(8,128)S(1)}, f32[512,1024]{1,0:T(8,128)S(1)}) fusion(s32[512]{0:T(512)S(1)} %iota_add_fusion.8, s32[1024]{0:T(1024)S(1)} %iota_add_fusion.9), kind=kLoop, calls=%fused_computation.22.clone.1 | loop fusion | flops 7864320 | bytes 4200448 | tf_op jit(solution)/shard_map/while/body/eval_jaxpr/cos | solution.py:16
  317.0 3.4 fusion.51
  321.9 3.7 %all-to-all-start.2 = ((f32[8,1,32]{2,1,0:T(1,128)}), f32[8,1,32]{2,1,0:T(1,128)S(1)}, u32[]{:S(2)}, u32[]{:S(2)}) async-start(f32[8,1,32]{2,1,0:T(1,128)} %bitcast.11), calls=%async_computation.3 | async-start | bytes 8192 | tf_op jit(solution)/shard_map/all_to_all | solution.py:138
  325.7 6.5 %all-to-all-done.2 = f32[8,1,32]{2,1,0:T(1,128)S(1)} async-done(((f32[8,1,32]{2,1,0:T(1,128)}), f32[8,1,32]{2,1,0:T(1,128)S(1)}, u32[]{:S(2)}, u32[]{:S(2)}) %all-to-all-start.2) | async-done | bytes 1056 | tf_op jit(solution)/shard_map/all_to_all | solution.py:138
  335.2 16.6 %reduce-scatter.2.cloned.1.call-done = f32[32,4096]{1,0:T(8,128)} async-done(((f32[128,4096]{1,0:T(8,128)}), f32[32,4096]{1,0:T(8,128)}) %reduce-scatter.2.cloned.1.call-update) | async-done | bytes 524304 | tf_op jit(solution)/shard_map/reduce_scatter | solution.py:149
  (107 shorter events, 49.0 us)
Async XLA Ops:
  12.6 95.3 %all-to-all-start = ((s32[8,32,2]{1,2,0:T(2,128)}), s32[8,32,2]{1,2,0:T(2,128)S(1)}, u32[]{:S(2)}, u32[]{:S(2)}) async-start(s32[8,32,2]{1,2,0:T(2,128)} %pad_add_fusion), calls=%async_computation | async-start | bytes 16384 | tf_op jit(solution)/shard_map/all_to_all | solution.py:130
  107.9 6.2 %copy-start = (s32[16]{0:T(128)S(1)}, s32[16]{0:T(128)}, u32[]{:S(2)}) copy-start(s32[16]{0:T(128)} %param.11) | copy-start | bytes 196
  107.9 106.6 %all-to-all-start.1 = ((f32[8,32,2048]{2,1,0:T(8,128)}), f32[8,32,2048]{2,1,0:T(8,128)}, u32[]{:S(2)}, u32[]{:S(2)}) async-start(f32[8,32,2048]{2,1,0:T(8,128)} %bitcast.8), calls=%async_computation.1 | async-start | bytes 4194304 | tf_op jit(solution)/shard_map/all_to_all | solution.py:129
  114.0 92.0 %all-reduce.2.cloned.1.call-start = ((), (), s32[]{:S(2)}) async-start(), calls=%async_computation.4 | async-start | bytes 262144 | tf_op jit(solution)/shard_map/psum | solution.py:103
  115.8 236.0 %reduce-scatter.2.cloned.1.call-start = ((), (), s32[]{:S(2)}) async-start(), calls=%async_computation.5 | async-start | bytes 2621440 | tf_op jit(solution)/shard_map/reduce_scatter | solution.py:149
  321.9 10.2 %all-to-all-start.2 = ((f32[8,1,32]{2,1,0:T(1,128)}), f32[8,1,32]{2,1,0:T(1,128)S(1)}, u32[]{:S(2)}, u32[]{:S(2)}) async-start(f32[8,1,32]{2,1,0:T(1,128)} %bitcast.11), calls=%async_computation.3 | async-start | bytes 8192 | tf_op jit(solution)/shard_map/all_to_all | solution.py:138
Sparse Core Ops, SparseCore 0:
  118.7 87.2 all-reduce.1
  321.5 30.2 reduce-scatter.1
where the time goes:
time: 359 us
  other arithmetic  151 us (42%)
  waiting for transfers between devices  110 us (31%)
  matrix products  40.4 us (11%)
  local copies, waits for them, and re-layouts  24.9 us (7%)
  starting transfers between devices  17.2 us (5%)
  between operations  14.2 us (4%)
    psum x1, waiting for transfers between devices, per_device(): sources = lax.psum(picked, 'chan')  87 us
    another operation x8, other arithmetic  72.2 us
    cos x8, other arithmetic, fourier_basis(): return jnp.concatenate([jnp.cos(angles), -jnp.sin(angles)], axis=1)  66.4 us
    dot_general x8, matrix products, fill_block(): lax.dot_general(spectral, fourier_table, (((1,), (1,)), ((), ())), precis...  27.4 us
    reduce_scatter x1, waiting for transfers between devices, per_device(): lax.psum_scatter(inverse(adjoint_spectra, time_len), 'src', scatter_dimen...  16.6 us
    dot_general x8, matrix products, add_block(): jnp.dot(segment, fourier_table, preferred_element_type=jnp.float32)  12 us
    all_to_all x1, starting transfers between devices, per_device(): lax.all_to_all(send_labels, 'chan', split_axis=0, concat_axis=0, tiled=True)  7.28 us
  transfers between devices with their start and end apart: 5, of which 3 were waited for; matrix products, arithmetic and copies ran while one was open for 29% of the time, Pallas kernels for 0%

commit v1 on v0

v1 whole, which is shorter than its diff:
```python
import functools
import math

import jax
import jax.numpy as jnp
import numpy as np
from jax import lax
from jax.experimental import pallas as pl
from jax.experimental.pallas import tpu as pltpu
from jax.sharding import PartitionSpec as P


K0 = 64
LANES = 128
CUT = 5
FIRST = (6, 7, 2, 3, 1)
MIDDLE = 4
LAST = 5
BASE = 64
F32 = jnp.float32
BF16 = jnp.bfloat16
VMEM = pl.BlockSpec(memory_space=pltpu.VMEM)
NT_DIMS = (((1,), (1,)), ((), ()))


def mm(a, b):
    return jnp.dot(a, b, preferred_element_type=F32)


def split2(x):
    hi = x.astype(BF16)
    return hi, (x - hi.astype(F32)).astype(BF16)


def split3(x):
    hi = x.astype(BF16)
    rest = x - hi.astype(F32)
    mid = rest.astype(BF16)
    return hi, mid, (rest - mid.astype(F32)).astype(BF16)


def phases(products, period):
    angles = (products % period) * (2.0 * math.pi / period)
    return np.cos(angles), np.sin(angles)


def pack_kernel(parts, groups, tag_ref, group_ref, receiver_ref, source_ref, observed_ref, *outs):
    pairs = observed_ref.shape[0]
    bins = observed_ref.shape[1] // 2
    capacity = 2 * pairs // groups
    group_row = group_ref[...]
    hits = (
        lax.broadcasted_iota(jnp.int32, (max(groups, 8), pairs), 0) == group_row
    ).astype(F32)
    earlier = (
        lax.broadcasted_iota(jnp.int32, (pairs, pairs), 0)
        < lax.broadcasted_iota(jnp.int32, (pairs, pairs), 1)
    ).astype(F32)
    counts = mm(hits.astype(BF16), earlier.astype(BF16))
    rank = jnp.sum(hits * counts, axis=0, keepdims=True).astype(jnp.int32)

    def chosen(slot_row, start, stop):
        index = start + lax.broadcasted_iota(jnp.int32, (stop - start, pairs), 0)
        return (index == slot_row).astype(F32).astype(BF16)

    if len(outs) > len(parts):
        code_ref, slot_ref = outs[-2:]
        slot_row = group_row * capacity + rank
        slot_ref[...] = slot_row
        labels = jnp.concatenate(
            [receiver_ref[...] + 1, source_ref[...]] + [jnp.zeros((6, pairs), jnp.int32)], axis=0
        ).astype(F32).astype(BF16)
        sent = lax.dot_general(
            labels, chosen(slot_row, 0, groups * capacity), NT_DIMS, preferred_element_type=F32
        )
        code_ref[...] = sent[0:1] * 256.0 + sent[1:2]
    slot_row = tag_ref[...] * capacity + rank
    for ((low_tag, high_tag), (first, last)), out_ref in zip(parts, outs):
        rows = chosen(slot_row, low_tag * capacity, high_tag * capacity)
        width = last - first
        for half in range(2):
            hi, mid, low = split3(observed_ref[:, half * bins + first : half * bins + last])
            out_ref[:, half * width : (half + 1) * width] = mm(rows, hi) + mm(rows, mid) + mm(rows, low)


def forward_kernel(
    steps, records_ref, cos_a_ref, sin_a_ref, cos_b_ref, sin_b_ref, rows_ref,
    white_ref, picked_ref, table, total,
):
    step = pl.program_id(0)
    bins = cos_b_ref.shape[1]
    parts = table.shape[0] // BASE

    @pl.when(step == 0)
    def _():
        total[...] = jnp.zeros_like(total)

    for part in range(parts):
        row = step * parts + part
        cos_a = cos_a_ref[pl.ds(row, 1), :]
        sin_a = sin_a_ref[pl.ds(row, 1), :]
        cos_b = cos_b_ref[...]
        sin_b = sin_b_ref[...]
        rows = slice(part * BASE, (part + 1) * BASE)
        table[rows, :bins] = (cos_a * cos_b - sin_a * sin_b).astype(BF16)
        table[rows, bins:] = (sin_a * cos_b + cos_a * sin_b).astype(BF16)
    total[...] += mm(records_ref[...], table[...])

    @pl.when(step == steps - 1)
    def _():
        spectra = total[...]
        power = jnp.sum(spectra * spectra, axis=1, keepdims=True) / bins
        white = spectra / jnp.sqrt(power + 1e-06)
        white_ref[...] = white
        chosen = (
            lax.broadcasted_iota(jnp.int32, (rows_ref.shape[0], white.shape[0]), 1) == rows_ref[...]
        ).astype(F32).astype(BF16)
        hi, mid, low = split3(white)
        picked_ref[...] = mm(chosen, hi) + mm(chosen, mid) + mm(chosen, low)


def pair_kernel(bins, spans, starts, count, code_ref, white_ref, sources_ref, *refs):
    blocks, begun, outs, misfit_ref = (
        refs[:count], refs[count : count + starts], refs[count + starts : -1], refs[-1],
    )
    begin = spans[0][0]
    total = spans[-1][1] - begin
    slots = code_ref.shape[1]
    rows, owners = white_ref.shape[0], sources_ref.shape[0]
    code = code_ref[...]
    receiver = code // 256 - 1
    source = code % 256
    scatter = (lax.broadcasted_iota(jnp.int32, (rows, slots), 0) == receiver).astype(F32)
    source_hits = (
        (lax.broadcasted_iota(jnp.int32, (LANES, slots), 0) == source) & (receiver >= 0)
    ).astype(F32)
    gather = scatter.T.astype(BF16)
    gather2 = jnp.concatenate([gather, gather], axis=1)
    scatter = scatter.astype(BF16)
    scatter2 = jnp.concatenate([scatter, scatter], axis=1)
    pick = source_hits.T[:, :owners].astype(BF16)

    def rows_of(left):
        hi, low = split2(white_ref[:, left : left + LANES])
        return mm(gather2, jnp.concatenate([hi, low], axis=0))

    def sources_of(left):
        hi, low = split2(sources_ref[:, left : left + LANES])
        return mm(pick, hi) + mm(pick, low)

    def summed(terms):
        hi, low = split2(terms)
        return mm(scatter2, jnp.concatenate([hi, low], axis=0))

    def seen(left):
        return jnp.concatenate([block[:, left : left + LANES] for block in blocks], axis=0)

    misfit = jnp.zeros((slots, LANES), F32)
    for number, (first, last) in enumerate(spans):
        width = last - first
        for at in range(0, width, LANES):
            lo = first + at
            index = lo + lax.broadcasted_iota(jnp.int32, (1, LANES), 1)
            weights = 0.5 - 0.5 * jnp.cos((index.astype(F32) + 0.5) * (2.0 * math.pi / bins))
            receiver_real, receiver_imag = rows_of(lo), rows_of(bins + lo)
            source_real, source_imag = sources_of(lo), sources_of(bins + lo)
            diff_real = source_real * receiver_real + source_imag * receiver_imag - seen(lo - begin)
            diff_imag = source_real * receiver_imag - source_imag * receiver_real - seen(total + lo - begin)
            residual_real = weights * diff_real
            residual_imag = weights * diff_imag
            misfit = misfit + (residual_real * diff_real + residual_imag * diff_imag)
            real = summed(residual_real * source_real - residual_imag * source_imag)
            imag = summed(residual_real * source_imag + residual_imag * source_real)
            if starts:
                real = real + begun[number][:, at : at + LANES]
                imag = imag + begun[number][:, width + at : width + at + LANES]
            outs[number][:, at : at + LANES] = real
            outs[number][:, width + at : width + at + LANES] = imag
    misfit_ref[...] = jnp.sum(misfit, axis=1, keepdims=True) / (2 * bins)


def inverse_kernel(scale, mix_ref, turn_cos_ref, turn_sin_ref, last_ref, *refs):
    chunks, (out_ref, held, wide) = refs[:-3], refs[-3:]
    count = out_ref.shape[0]
    blocks = held.shape[1] // 2
    steps = mix_ref.shape[0] // 2
    turns = turn_cos_ref.shape[0]
    at = 0
    for chunk in chunks:
        width = chunk.shape[1] // 2
        for block in range(width // LANES):
            for half in range(2):
                left = half * width + block * LANES
                held[:, half * blocks + at, :] = chunk[:, left : left + LANES]
            at += 1
    mix = mix_ref[...]
    last = last_ref[...]
    turn_cos = turn_cos_ref[...]
    turn_sin = turn_sin_ref[...]
    for row in range(count):
        hi, low = split2(held[row])
        mixed = mm(mix, jnp.concatenate([hi, low, hi], axis=0))
        real = jnp.concatenate([mixed[:steps]] * (turns // steps), axis=0)
        imag = jnp.concatenate([mixed[steps:]] * (turns // steps), axis=0)
        turned = jnp.concatenate(
            [real * turn_cos - imag * turn_sin, real * turn_sin + imag * turn_cos], axis=1
        )
        hi, low = split2(turned)
        wide[row] = lax.dot_general(
            last, jnp.concatenate([hi, low, hi], axis=1), NT_DIMS, preferred_element_type=F32
        )
    for block in range(wide.shape[1]):
        out_ref[:, block * LANES : (block + 1) * LANES] = wide[:, block, :] * scale


def bf16_parts(values):
    hi = values.astype(jnp.bfloat16)
    return hi, (values - hi.astype(np.float64)).astype(jnp.bfloat16)


def inverse(chunks, time_len, bins):
    period = 2 * time_len
    blocks = bins // LANES
    steps = period // LANES
    turns = LANES
    outer = time_len // turns
    cos, sin = phases(np.arange(steps)[:, None] * np.arange(blocks)[None, :] * LANES, period)
    mix = np.concatenate(
        [np.concatenate([cos, -sin], axis=1), np.concatenate([sin, cos], axis=1)], axis=0
    )
    hi, low = bf16_parts(mix)
    mix = np.concatenate([hi, hi, low], axis=1)
    r = np.arange(LANES)[None, :]
    turn_cos, turn_sin = phases((K0 + r) * np.arange(turns)[:, None], period)
    cos, sin = phases((K0 + r) * np.arange(outer)[:, None] * turns, period)
    hi, low = bf16_parts(np.concatenate([cos, -sin], axis=1))
    last = np.concatenate([hi, hi, low], axis=1)
    count = chunks[0].shape[0]
    return pl.pallas_call(
        functools.partial(inverse_kernel, 1.0 / math.sqrt(bins)),
        out_shape=jax.ShapeDtypeStruct((count, time_len), F32),
        in_specs=[VMEM] * (4 + len(chunks)),
        out_specs=VMEM,
        scratch_shapes=[
            pltpu.VMEM((count, 2 * blocks, LANES), F32),
            pltpu.VMEM((count, outer, LANES), F32),
        ],
        cost_estimate=pl.CostEstimate(flops=1_000_000_000, bytes_accessed=2_000_000, transcendentals=0),
        name="inverse",
    )(jnp.asarray(mix), jnp.asarray(turn_cos, F32), jnp.asarray(turn_sin, F32), jnp.asarray(last), *chunks)


def exchange(value, axis):
    return lax.all_to_all(value, axis, split_axis=0, concat_axis=0, tiled=True)


def scatter_sum(value, axis):
    size = lax.axis_size(axis)
    index = lax.axis_index(axis)
    rows, width = value.shape
    value = value.reshape(size, rows // size, width)
    bit = 1
    while bit < size:
        pairs = [(i, i ^ bit) for i in range(size)]
        blocks = value.shape[0]
        value = value.reshape(blocks // 2, 2, rows // size, width)
        side = (index // bit) % 2
        kept = lax.dynamic_index_in_dim(value, side, 1, keepdims=False)
        sent = lax.dynamic_index_in_dim(value, 1 - side, 1, keepdims=False)
        moved = lax.ppermute(sent, axis, pairs)
        value = kept + moved
        bit *= 2
    return value.reshape(rows // size, width)


def per_device(records, virtual_sources, pair_group, pair_receiver, pair_source, observed):
    row_count, time_len = records.shape
    pair_count = observed.shape[0]
    bins = observed.shape[1] // 2
    groups = lax.axis_size("chan")
    capacity = 2 * pair_count // groups
    slots = groups * capacity
    owners = virtual_sources.shape[0]
    chan_index = lax.axis_index("chan")
    routed = groups == 8
    cut = bins * CUT // 8
    spans = [(0, cut), (cut, bins)]
    full = (0, bins)
    group_row = pair_group.reshape(1, pair_count)
    lists = (
        group_row ^ chan_index if routed else group_row,
        group_row,
        pair_receiver.reshape(1, pair_count),
        pair_source.reshape(1, pair_count),
    )

    def pack(parts, labelled):
        shapes = [
            jax.ShapeDtypeStruct(((high - low) * capacity, 2 * (last - first)), F32)
            for (low, high), (first, last) in parts
        ]
        if labelled:
            shapes.append(jax.ShapeDtypeStruct((1, slots), F32))
            shapes.append(jax.ShapeDtypeStruct((1, pair_count), jnp.int32))
        return pl.pallas_call(
            functools.partial(pack_kernel, parts, groups),
            out_shape=shapes,
            in_specs=[VMEM] * 5,
            out_specs=[VMEM] * len(shapes),
            cost_estimate=pl.CostEstimate(flops=400_000_000, bytes_accessed=3_000_000, transcendentals=0),
            name="pack",
        )(*lists, observed)

    def move(value, tag):
        return lax.ppermute(value, "chan", [(i, i ^ tag) for i in range(groups)])

    early = {}
    if routed:
        *sent, code, slot = pack([((tag, tag + 1), full) for tag in FIRST], True)
        for tag, value in zip(FIRST, sent):
            early[tag] = move(value, tag)
        own, middle, last_a, last_b = pack(
            [((0, 1), full), ((MIDDLE, MIDDLE + 1), full)]
            + [((LAST, LAST + 1), span) for span in spans],
            False,
        )
    else:
        own, code, slot = pack([((0, groups), full)], True)

    period = 2 * time_len
    k = K0 + np.arange(bins)[None, :]
    cos_a, sin_a = phases(k * BASE * np.arange(time_len // BASE)[:, None], period)
    cos_b, sin_b = phases(k * np.arange(BASE)[:, None], period)
    steps = 8
    block = time_len // steps
    whole = lambda shape: pl.BlockSpec(shape, lambda i: (0, 0))
    whitened, picked = pl.pallas_call(
        functools.partial(forward_kernel, steps),
        grid=(steps,),
        out_shape=[
            jax.ShapeDtypeStruct((row_count, 2 * bins), F32),
            jax.ShapeDtypeStruct((owners, 2 * bins), F32),
        ],
        in_specs=[
            pl.BlockSpec((row_count, block), lambda i: (0, i)),
            whole(cos_a.shape), whole(cos_a.shape), whole(cos_b.shape), whole(cos_b.shape),
            whole((owners, 1)),
        ],
        out_specs=[whole((row_count, 2 * bins)), whole((owners, 2 * bins))],
        scratch_shapes=[pltpu.VMEM((block, 2 * bins), BF16), pltpu.VMEM((row_count, 2 * bins), F32)],
        cost_estimate=pl.CostEstimate(flops=8_000_000_000, bytes_accessed=4_000_000, transcendentals=0),
        name="forward",
    )(
        records, jnp.asarray(cos_a, F32), jnp.asarray(-sin_a, F32), jnp.asarray(cos_b, F32),
        jnp.asarray(-sin_b, F32), (virtual_sources - chan_index * row_count).reshape(owners, 1),
    )

    part = 2 * bins // groups
    spread = picked.reshape(owners, groups, part).transpose(1, 0, 2)
    label = jnp.pad(code.reshape(groups, 1, capacity), ((0, 0), (0, 7), (0, part - capacity)))
    arrived = exchange(jnp.concatenate([spread, label], axis=1), "chan")
    order = chan_index ^ jnp.arange(groups, dtype=jnp.int32) if routed else None
    codes = arrived[:, owners, :capacity].astype(jnp.int32)
    codes = jnp.take(codes, order, axis=0) if routed else codes
    summed = jnp.sum(arrived[:, :owners], axis=0)
    sources = exchange(jnp.broadcast_to(summed[None], (groups, owners, part)), "chan")
    sources = sources.transpose(1, 0, 2).reshape(owners, 2 * bins)

    def terms(blocks, which, some, begun):
        chosen = codes.reshape(1, slots)
        if routed:
            chosen = jnp.concatenate([codes[tag] for tag in which]).reshape(1, -1)
        count = chosen.shape[1]
        *sums, misfit = pl.pallas_call(
            functools.partial(pair_kernel, bins, some, len(begun), len(blocks)),
            out_shape=[jax.ShapeDtypeStruct((row_count, 2 * (last - first)), F32) for first, last in some]
            + [jax.ShapeDtypeStruct((count, 1), F32)],
            in_specs=[VMEM] * (3 + len(blocks) + len(begun)),
            out_specs=[VMEM] * (len(some) + 1),
            cost_estimate=pl.CostEstimate(flops=2_000_000_000, bytes_accessed=5_000_000, transcendentals=0),
            name="pairs",
        )(chosen, whitened, sources, *blocks, *begun)
        return sums, misfit.reshape(-1, capacity)

    if routed:
        middle = move(middle, MIDDLE)
        last_a = move(last_a, LAST)
        last_b = move(last_b, LAST)
        tags = [0, *FIRST, MIDDLE]
        sums, misfit = terms([own, *early.values(), middle], tags, spans, [])
        (sum_a,), misfit_a = terms([last_a], [LAST], spans[:1], sums[:1])
        spectra = [scatter_sum(sum_a, "src")]
        (sum_b,), misfit_b = terms([last_b], [LAST], spans[1:], sums[1:])
        spectra.append(scatter_sum(sum_b, "src"))
        misfit = jnp.concatenate([misfit, misfit_a + misfit_b], axis=0)
        place = np.argsort(np.array([*tags, LAST]))
        misfit = jnp.take(misfit, jnp.asarray(place)[order], axis=0)
    else:
        sums, misfit = terms([exchange(own.reshape(groups, capacity, -1), "chan").reshape(slots, -1)], [], spans, [])
        spectra = [scatter_sum(value, "src") for value in sums]

    returned = exchange(misfit, "chan").reshape(slots, 1)
    hits = lax.broadcasted_iota(jnp.int32, (slots, pair_count), 0) == slot
    pair_misfit = jnp.sum(jnp.where(hits, returned, 0.0), axis=0)
    result = inverse(spectra, time_len, bins)
    return (result, pair_misfit)


def solution(mesh):
    return jax.shard_map(
        per_device,
        mesh=mesh,
        in_specs=(
            P("chan", None),
            P("src"),
            P(("chan", "src"), None),
            P(("chan", "src")),
            P(("chan", "src")),
            P(("chan", "src"), None),
        ),
        out_specs=(P(("chan", "src"), None), P(("chan", "src"))),
        check_vma=False,
    )
```

time: 359 us -> 126 us (0.35)
  other arithmetic: 151 us -> 6.37 us
  waiting for transfers between devices: 110 us -> 37.4 us
  matrix products: 40.4 us -> 0 us
  Pallas kernels: 0 us -> 35.7 us
  starting transfers between devices: 17.2 us -> 32.7 us
  between operations: 14.2 us -> 0.89 us
  local copies, waits for them, and re-layouts: 24.9 us -> 12.2 us
    psum x1 -> x0, waiting for transfers between devices: 87 us -> none  [per_device(): sources = lax.psum(picked, 'chan')]
    another operation x10 -> x0, other arithmetic: 73 us -> none
    cos x8 -> x0, other arithmetic: 66.4 us -> none  [fourier_basis(): return jnp.concatenate([jnp.cos(angles), -jnp.sin(angles)], axis=1)]
    dot_general x17 -> x0, matrix products: 40.4 us -> none  [the longest x8 27.4 us: fill_block(): lax.dot_general(spectral, fourier_table, (((1,), (1,)), ((), ())), precis...]
    pallas_call x0 -> x7, Pallas kernels: none -> 35.7 us  [the longest x3 12.2 us: terms(): pl.pallas_call(functools.partial(pair_kernel, bins, some, len(begun), len...]
    all_to_all x3, waiting for transfers between devices: 6.49 us -> 25.7 us  [exchange(): return lax.all_to_all(value, axis, split_axis=0, concat_axis=0, tiled=True)]
    ppermute x0 -> x12, starting transfers between devices: none -> 18.4 us  [the longest x8 15.6 us: move(): return lax.ppermute(value, 'chan', [(i, i ^ tag) for i in range(groups)])]
    reduce_scatter x1 -> x0, waiting for transfers between devices: 16.6 us -> none  [per_device(): lax.psum_scatter(inverse(adjoint_spectra, time_len), 'src', scatter_dimen...]
  transfers between devices with their start and end apart: 5 -> 15, of which waited for: 3 -> 6; matrix products, arithmetic and copies ran while one was open for 29% -> 8% of each run, Pallas kernels for 0% -> 12%
where the time goes in v1:
time: 126 us; the launch traced here: 125 us
  waiting for transfers between devices  37.4 us (30%)
  Pallas kernels  35.7 us (28%)
  starting transfers between devices  32.7 us (26%)
  local copies, waits for them, and re-layouts  12.2 us (10%)
  other arithmetic  6.37 us (5%)
    all_to_all x3, waiting for transfers between devices, exchange(): return lax.all_to_all(value, axis, split_axis=0, concat_axis=0, tiled=True)  25.7 us
    ppermute x8, starting transfers between devices, move(): return lax.ppermute(value, 'chan', [(i, i ^ tag) for i in range(groups)])  15.6 us
    all_to_all x3, starting transfers between devices, exchange(): return lax.all_to_all(value, axis, split_axis=0, concat_axis=0, tiled=True)  14.3 us
    pallas_call x3, Pallas kernels, terms(): pl.pallas_call(functools.partial(pair_kernel, bins, some, len(begun), len...  12.2 us
    pallas_call x1, Pallas kernels, per_device(): pl.pallas_call(functools.partial(forward_kernel, steps), grid=(steps,), o...  10.1 us
    pallas_call x2, Pallas kernels, pack(): pl.pallas_call(functools.partial(pack_kernel, parts, groups), out_shape=s...  6.7 us
    pallas_call x1, Pallas kernels, inverse(): pl.pallas_call(functools.partial(inverse_kernel, 1.0 / math.sqrt(bins)),...  6.69 us
    ppermute x8, waiting for transfers between devices, move(): return lax.ppermute(value, 'chan', [(i, i ^ tag) for i in range(groups)])  6.62 us
  transfers between devices with their start and end apart: 15, of which 6 were waited for; matrix products, arithmetic and copies ran while one was open for 8% of the time, Pallas kernels for 12%

profile of v1, /device:TPU:0, one launch (start us, length us, event | category | flops | bytes accessed | tf_op | source)
XLA Modules:
  0.0 125.2 jit_solution(16942423973157500444)
XLA Ops:
  1.8 3.7 %pack.2 = (f32[32,2048]{1,0:T(8,128)}, f32[32,2048]{1,0:T(8,128)}, f32[32,2048]{1,0:T(8,128)}, f32[32,2048]{1,0:T(8,128)}, f32[32,2048]{1,0:T(8,128)}, /*index=5*/f32[1,256]{1,0:T(1,128)}, s32[1,128]{1,0:T(1,128)}) custom-call(s32[1,128]{1,0:T(1,128)} %broadcast_xor_fusion.tag_ref, s32[1,128]{1,0:T(1,128)} %bitcast.83, s32[1,128]{1,0:T(1,128)} %bitcast.85, ...), custom_call_target="tpu_custom_call" | custom-call | flops 400000000 | bytes 3000000 | tf_op jit(solution)/shard_map/pack/pallas_call | solution.py:305
  6.2 0.7 reduce.9
  7.6 0.7 copy.37.rows_ref
  8.3 10.1 %forward.1 = (f32[128,2048]{1,0:T(8,128)}, f32[16,2048]{1,0:T(8,128)}) custom-call(bf16[128,4096]{1,0:T(8,128)(2,1)} %records_ref.1, f32[64,1024]{1,0:T(8,128)} %constant.135.clone.cos_a_ref, f32[64,1024]{1,0:T(8,128)} %constant.136.clone.sin_a_ref, f32[64,1024]{1,0:T(8,128)} %constant.137.clone.cos_b_ref, f32[64,1024]{1,0:T(8,128)} %constant.138.clone.sin_b_ref, ...), custom_call_target="tpu_custom_call" | custom-call | flops 8000000000 | bytes 4000000 | tf_op jit(solution)/shard_map/forward/pallas_call | solution.py:337
  18.4 0.9 copy.55
  19.3 0.7 select_maximum_fusion
  20.0 7.4 %all-to-all-start = ((f32[8,24,256]{2,1,0:T(8,128)}), f32[8,24,256]{2,1,0:T(8,128)S(1)}, u32[]{:S(2)}, u32[]{:S(2)}) async-start(f32[8,24,256]{2,1,0:T(8,128)} %select_maximum_fusion), calls=%async_computation | async-start | bytes 393216 | tf_op jit(solution)/shard_map/all_to_all | solution.py:254
  27.5 3.8 %collective-permute-start.1 = (f32[32,2048]{1,0:T(8,128)S(1)}, f32[32,2048]{1,0:T(8,128)S(1)}, u32[]{:S(2)}, u32[]{:S(2)}) collective-permute-start(f32[32,2048]{1,0:T(8,128)S(1)} %copy-done.16), channel_id=1, source_target_pairs={{0,24},{4,28},{8,16},{12,20},{16,8},{20,12},{24,0},{28,4},{1,25},{... | collective-permute-start | bytes 786440 | tf_op jit(solution)/shard_map/ppermute | solution.py:315
  31.3 1.5 %collective-permute-start.2 = (f32[32,2048]{1,0:T(8,128)S(1)}, f32[32,2048]{1,0:T(8,128)S(1)}, u32[]{:S(2)}, u32[]{:S(2)}) collective-permute-start(f32[32,2048]{1,0:T(8,128)S(1)} %copy-done.10), channel_id=1, source_target_pairs={{0,28},{4,24},{8,20},{12,16},{16,12},{20,8},{24,4},{28,0},{1,29},{... | collective-permute-start | bytes 786440 | tf_op jit(solution)/shard_map/ppermute | solution.py:315
  32.8 1.5 %collective-permute-start.4 = (f32[32,2048]{1,0:T(8,128)S(1)}, f32[32,2048]{1,0:T(8,128)S(1)}, u32[]{:S(2)}, u32[]{:S(2)}) collective-permute-start(f32[32,2048]{1,0:T(8,128)S(1)} %copy-done.8), channel_id=1, source_target_pairs={{0,12},{4,8},{8,4},{12,0},{16,28},{20,24},{24,20},{28,16},{1,13},{... | collective-permute-start | bytes 786440 | tf_op jit(solution)/shard_map/ppermute | solution.py:315
  34.3 1.9 %collective-permute-start.5 = (f32[32,2048]{1,0:T(8,128)S(1)}, f32[32,2048]{1,0:T(8,128)S(1)}, u32[]{:S(2)}, u32[]{:S(2)}) collective-permute-start(f32[32,2048]{1,0:T(8,128)S(1)} %copy-done.7), channel_id=1, source_target_pairs={{0,4},{4,0},{8,12},{12,8},{16,20},{20,16},{24,28},{28,24},{1,5},{5... | collective-permute-start | bytes 786440 | tf_op jit(solution)/shard_map/ppermute | solution.py:315
  36.9 3.0 %pack.3 = (f32[32,2048]{1,0:T(8,128)}, f32[32,2048]{1,0:T(8,128)}, f32[32,1280]{1,0:T(8,128)}, f32[32,768]{1,0:T(8,128)}) custom-call(s32[1,128]{1,0:T(1,128)} %broadcast_xor_fusion.tag_ref, s32[1,128]{1,0:T(1,128)} %bitcast.84, s32[1,128]{1,0:T(1,128)} %bitcast.86, s32[1,128]{1,0:T(1,128)} %bitcast.88, f32[128,2048]{1,0:T(8,128)} %observed_ref.3), custom_call_target="tpu_custom_call" | custom-call | flops 400000000 | bytes 3000000 | tf_op jit(solution)/shard_map/pack/pallas_call | solution.py:305
  39.9 7.5 %all-to-all-done = f32[8,24,256]{2,1,0:T(8,128)S(1)} async-done(((f32[8,24,256]{2,1,0:T(8,128)}), f32[8,24,256]{2,1,0:T(8,128)S(1)}, u32[]{:S(2)}, u32[]{:S(2)}) %all-to-all-start) | async-done | bytes 196640 | tf_op jit(solution)/shard_map/all_to_all | solution.py:254
  48.7 3.4 %all-to-all-start.1 = ((f32[8,16,256]{2,1,0:T(8,128)}), f32[8,16,256]{2,1,0:T(8,128)S(1)}, u32[]{:S(2)}, u32[]{:S(2)}) async-start(f32[8,16,256]{2,1,0:T(8,128)} %broadcast_in_dim.43), calls=%async_computation.1 | async-start | bytes 262144 | tf_op jit(solution)/shard_map/all_to_all | solution.py:254
  52.1 2.9 %collective-permute-start.6 = (f32[32,2048]{1,0:T(8,128)S(1)}, f32[32,2048]{1,0:T(8,128)S(1)}, u32[]{:S(2)}, u32[]{:S(2)}) collective-permute-start(f32[32,2048]{1,0:T(8,128)S(1)} %copy-done.17), channel_id=1, source_target_pairs={{0,16},{4,20},{8,24},{12,28},{16,0},{20,4},{24,8},{28,12},{1,17},{... | collective-permute-start | bytes 786440 | tf_op jit(solution)/shard_map/ppermute | solution.py:315
  56.2 13.7 %all-to-all-done.1 = f32[8,16,256]{2,1,0:T(8,128)S(1)} async-done(((f32[8,16,256]{2,1,0:T(8,128)}), f32[8,16,256]{2,1,0:T(8,128)S(1)}, u32[]{:S(2)}, u32[]{:S(2)}) %all-to-all-start.1) | async-done | bytes 131104 | tf_op jit(solution)/shard_map/all_to_all | solution.py:254
  71.1 3.5 %collective-permute-start.9 = (f32[32,768]{1,0:T(8,128)S(1)}, f32[32,768]{1,0:T(8,128)S(1)}, u32[]{:S(2)}, u32[]{:S(2)}) collective-permute-start(f32[32,768]{1,0:T(8,128)S(1)} %copy-done.21), channel_id=1, source_target_pairs={{0,20},{4,16},{8,28},{12,24},{16,4},{20,0},{24,12},{28,8},{1,21},{... | collective-permute-start | bytes 294920 | tf_op jit(solution)/shard_map/ppermute | solution.py:315
  74.6 6.6 %collective-permute-done.6.refs_6_ = f32[32,2048]{1,0:T(8,128)S(1)} collective-permute-done((f32[32,2048]{1,0:T(8,128)S(1)}, f32[32,2048]{1,0:T(8,128)S(1)}, u32[]{:S(2)}, u32[]{:S(2)}) %collective-permute-start.6) | collective-permute-done | bytes 262176 | tf_op jit(solution)/shard_map/ppermute | solution.py:315
  81.9 5.8 %pairs.3 = (f32[128,1280]{1,0:T(8,128)}, f32[128,768]{1,0:T(8,128)}, f32[224,1]{1,0:T(8,128)}) custom-call(s32[1,224]{1,0:T(1,128)} %bitcast.81, f32[128,2048]{1,0:T(8,128)} %get-tuple-element.24.white_ref, f32[16,2048]{1,0:T(8,128)} %bitcast.74, f32[32,2048]{1,0:T(8,128)} %get-tuple-element.26.refs_0_, f32[32,2048]{1,0:T(8,128)} %copy-done.11, ...), custom_call_target="tpu_custom_call" | custom-call | flops 2000000000 | bytes 5000000 | tf_op jit(solution)/shard_map/pairs/pallas_call | solution.py:374
  88.3 2.9 %pairs.5 = (f32[128,768]{1,0:T(8,128)}, f32[32,1]{1,0:T(8,128)}) custom-call(s32[1,32]{1,0:T(1,128)} %get-tuple-element.49.code_ref, f32[128,2048]{1,0:T(8,128)} %get-tuple-element.24.white_ref, f32[16,2048]{1,0:T(8,128)} %bitcast.75, f32[32,768]{1,0:T(8,128)} %copy-done.22, f32[128,768]{1,0:T(8,128)} %get-tuple-element.36.refs_1_), custom_call_target="tpu_custom_call" | custom-call | flops 2000000000 | bytes 5000000 | tf_op jit(solution)/shard_map/pairs/pallas_call | solution.py:374
  91.2 1.0 dynamic-slice_bitcast_fusion.1
  92.5 0.7 copy-done.20
  93.1 3.5 %pairs.4 = (f32[128,1280]{1,0:T(8,128)}, f32[32,1]{1,0:T(8,128)}) custom-call(s32[1,32]{1,0:T(1,128)} %get-tuple-element.49.code_ref, f32[128,2048]{1,0:T(8,128)} %get-tuple-element.24.white_ref, f32[16,2048]{1,0:T(8,128)} %bitcast.76, f32[32,1280]{1,0:T(8,128)} %copy-done.20, f32[128,1280]{1,0:T(8,128)} %get-tuple-element.33.refs_1_), custom_call_target="tpu_custom_call" | custom-call | flops 2000000000 | bytes 5000000 | tf_op jit(solution)/shard_map/pairs/pallas_call | solution.py:374
  96.6 0.9 add_reduce_fusion
  98.8 3.5 %all-to-all-start.2 = ((f32[8,1,32]{2,1,0:T(1,128)}), f32[8,1,32]{2,1,0:T(1,128)S(1)}, u32[]{:S(2)}, u32[]{:S(2)}) async-start(f32[8,1,32]{2,1,0:T(1,128)} %bitcast.29), calls=%async_computation.2 | async-start | bytes 8192 | tf_op jit(solution)/shard_map/all_to_all | solution.py:254
  102.3 1.1 dynamic-slice_bitcast_fusion
  103.9 4.5 %all-to-all-done.2 = f32[8,1,32]{2,1,0:T(1,128)S(1)} async-done(((f32[8,1,32]{2,1,0:T(1,128)}), f32[8,1,32]{2,1,0:T(1,128)S(1)}, u32[]{:S(2)}, u32[]{:S(2)}) %all-to-all-start.2) | async-done | bytes 1056 | tf_op jit(solution)/shard_map/all_to_all | solution.py:254
  108.4 0.7 reduce.10
  109.9 1.6 %collective-permute-start.11 = (f32[1,32,768]{2,1,0:T(8,128)S(1)}, f32[1,32,768]{2,1,0:T(8,128)S(1)}, u32[]{:S(2)}, u32[]{:S(2)}) collective-permute-start(f32[1,32,768]{2,1,0:T(8,128)S(1)} %constant_dynamic-slice_fusion), channel_id=1, source_target_pairs={{0,2},{1,3},{2,0},{3,1},{4,6},{5,7},{6,4},{7,5},{8,10},{9,11},{10,... | collective-permute-start | bytes 294920 | tf_op jit(solution)/shard_map/ppermute | solution.py:270
  112.1 3.5 %collective-permute-done.11 = f32[1,32,768]{2,1,0:T(8,128)S(1)} collective-permute-done((f32[1,32,768]{2,1,0:T(8,128)S(1)}, f32[1,32,768]{2,1,0:T(8,128)S(1)}, u32[]{:S(2)}, u32[]{:S(2)}) %collective-permute-start.11) | collective-permute-done | bytes 98336 | tf_op jit(solution)/shard_map/ppermute | solution.py:270
  116.3 1.6 %collective-permute-done.8 = f32[1,32,1280]{2,1,0:T(8,128)S(1)} collective-permute-done((f32[1,32,1280]{2,1,0:T(8,128)S(1)}, f32[1,32,1280]{2,1,0:T(8,128)S(1)}, u32[]{:S(2)}, u32[]{:S(2)}) %collective-permute-start.8) | collective-permute-done | bytes 163872 | tf_op jit(solution)/shard_map/ppermute | solution.py:270
  118.5 6.7 %inverse.1 = f32[32,4096]{1,0:T(8,128)} custom-call(bf16[128,48]{1,0:T(8,128)(2,1)} %constant.140.clone.mix_ref, f32[128,128]{1,0:T(8,128)} %constant.141.clone.turn_cos_ref, f32[128,128]{1,0:T(8,128)} %constant.142.clone.turn_sin_ref, bf16[32,768]{1,0:T(8,128)(2,1)} %constant.143.clone.last_ref, f32[32,1280]{1,0:T(8,128)} %add_bitcast_fusion.refs_0_, ...), custom_call_target="tpu_custom_call" | custom-call | flops 1000000000 | bytes 2000000 | tf_op jit(solution)/shard_map/inverse/pallas_call | solution.py:239
  (95 shorter events, 13.0 us)
Async XLA Ops:
  8.3 19.1 %copy-start.16 = (f32[32,2048]{1,0:T(8,128)S(1)}, f32[32,2048]{1,0:T(8,128)}, u32[]{:S(2)}) copy-start(f32[32,2048]{1,0:T(8,128)} %get-tuple-element.27) | copy-start | bytes 786436
  8.3 23.0 %copy-start.10 = (f32[32,2048]{1,0:T(8,128)S(1)}, f32[32,2048]{1,0:T(8,128)}, u32[]{:S(2)}) copy-start(f32[32,2048]{1,0:T(8,128)} %get-tuple-element.28) | copy-start | bytes 786436
  8.3 24.4 %copy-start.9 = (f32[32,2048]{1,0:T(8,128)S(1)}, f32[32,2048]{1,0:T(8,128)}, u32[]{:S(2)}) copy-start(f32[32,2048]{1,0:T(8,128)} %get-tuple-element.29) | copy-start | bytes 786436
  19.3 13.4 %copy-start.8 = (f32[32,2048]{1,0:T(8,128)S(1)}, f32[32,2048]{1,0:T(8,128)}, u32[]{:S(2)}) copy-start(f32[32,2048]{1,0:T(8,128)} %get-tuple-element.30) | copy-start | bytes 786436
  20.0 14.3 %copy-start.7 = (f32[32,2048]{1,0:T(8,128)S(1)}, f32[32,2048]{1,0:T(8,128)}, u32[]{:S(2)}) copy-start(f32[32,2048]{1,0:T(8,128)} %get-tuple-element.31) | copy-start | bytes 786436
  20.0 16.2 %copy-start = (s32[8]{0:T(128)S(1)}, s32[8]{0:T(128)}, u32[]{:S(2)}) copy-start(s32[8]{0:T(128)} %constant.139.clone) | copy-start | bytes 100
  20.0 27.4 %all-to-all-start = ((f32[8,24,256]{2,1,0:T(8,128)}), f32[8,24,256]{2,1,0:T(8,128)S(1)}, u32[]{:S(2)}, u32[]{:S(2)}) async-start(f32[8,24,256]{2,1,0:T(8,128)} %select_maximum_fusion), calls=%async_computation | async-start | bytes 393216 | tf_op jit(solution)/shard_map/all_to_all | solution.py:254
  27.5 24.6 %collective-permute-start.1 = (f32[32,2048]{1,0:T(8,128)S(1)}, f32[32,2048]{1,0:T(8,128)S(1)}, u32[]{:S(2)}, u32[]{:S(2)}) collective-permute-start(f32[32,2048]{1,0:T(8,128)S(1)} %copy-done.16), channel_id=1, source_target_pairs={{0,24},{4,28},{8,16},{12,20},{16,8},{20,12},{24,0},{28,4},{1,25},{... | collective-permute-start | bytes 786440 | tf_op jit(solution)/shard_map/ppermute | solution.py:315
  31.3 39.3 %collective-permute-start.2 = (f32[32,2048]{1,0:T(8,128)S(1)}, f32[32,2048]{1,0:T(8,128)S(1)}, u32[]{:S(2)}, u32[]{:S(2)}) collective-permute-start(f32[32,2048]{1,0:T(8,128)S(1)} %copy-done.10), channel_id=1, source_target_pairs={{0,28},{4,24},{8,20},{12,16},{16,12},{20,8},{24,4},{28,0},{1,29},{... | collective-permute-start | bytes 786440 | tf_op jit(solution)/shard_map/ppermute | solution.py:315
  32.7 38.3 %collective-permute-start.3 = (f32[32,2048]{1,0:T(8,128)S(1)}, f32[32,2048]{1,0:T(8,128)S(1)}, u32[]{:S(2)}, u32[]{:S(2)}) collective-permute-start(f32[32,2048]{1,0:T(8,128)S(1)} %copy-done.9), channel_id=1, source_target_pairs={{0,8},{4,12},{8,0},{12,4},{16,24},{20,28},{24,16},{28,20},{1,9},{5... | collective-permute-start | bytes 786440 | tf_op jit(solution)/shard_map/ppermute | solution.py:315
  32.8 41.8 %collective-permute-start.4 = (f32[32,2048]{1,0:T(8,128)S(1)}, f32[32,2048]{1,0:T(8,128)S(1)}, u32[]{:S(2)}, u32[]{:S(2)}) collective-permute-start(f32[32,2048]{1,0:T(8,128)S(1)} %copy-done.8), channel_id=1, source_target_pairs={{0,12},{4,8},{8,4},{12,0},{16,28},{20,24},{24,20},{28,16},{1,13},{... | collective-permute-start | bytes 786440 | tf_op jit(solution)/shard_map/ppermute | solution.py:315
  34.3 40.2 %collective-permute-start.5 = (f32[32,2048]{1,0:T(8,128)S(1)}, f32[32,2048]{1,0:T(8,128)S(1)}, u32[]{:S(2)}, u32[]{:S(2)}) collective-permute-start(f32[32,2048]{1,0:T(8,128)S(1)} %copy-done.7), channel_id=1, source_target_pairs={{0,4},{4,0},{8,12},{12,8},{16,20},{20,16},{24,28},{28,24},{1,5},{5... | collective-permute-start | bytes 786440 | tf_op jit(solution)/shard_map/ppermute | solution.py:315
  47.9 4.1 %copy-start.17 = (f32[32,2048]{1,0:T(8,128)S(1)}, f32[32,2048]{1,0:T(8,128)}, u32[]{:S(2)}) copy-start(f32[32,2048]{1,0:T(8,128)} %get-tuple-element.32) | copy-start | bytes 786436
  48.7 21.3 %all-to-all-start.1 = ((f32[8,16,256]{2,1,0:T(8,128)}), f32[8,16,256]{2,1,0:T(8,128)S(1)}, u32[]{:S(2)}, u32[]{:S(2)}) async-start(f32[8,16,256]{2,1,0:T(8,128)} %broadcast_in_dim.43), calls=%async_computation.1 | async-start | bytes 262144 | tf_op jit(solution)/shard_map/all_to_all | solution.py:254
  52.0 18.6 %copy-start.19 = (f32[32,1280]{1,0:T(8,128)S(1)}, f32[32,1280]{1,0:T(8,128)}, u32[]{:S(2)}) copy-start(f32[32,1280]{1,0:T(8,128)} %get-tuple-element.25) | copy-start | bytes 491524
  52.0 29.1 %copy-start.11 = (f32[32,2048]{1,0:T(8,128)}, f32[32,2048]{1,0:T(8,128)S(1)}, u32[]{:S(2)}) copy-start(f32[32,2048]{1,0:T(8,128)S(1)} %collective-permute-done.1.refs_1_) | copy-start | bytes 786436
  52.1 29.1 %collective-permute-start.6 = (f32[32,2048]{1,0:T(8,128)S(1)}, f32[32,2048]{1,0:T(8,128)S(1)}, u32[]{:S(2)}, u32[]{:S(2)}) collective-permute-start(f32[32,2048]{1,0:T(8,128)S(1)} %copy-done.17), channel_id=1, source_target_pairs={{0,16},{4,20},{8,24},{12,28},{16,0},{20,4},{24,8},{28,12},{1,17},{... | collective-permute-start | bytes 786440 | tf_op jit(solution)/shard_map/ppermute | solution.py:315
  70.6 10.6 %copy-start.12 = (f32[32,2048]{1,0:T(8,128)}, f32[32,2048]{1,0:T(8,128)S(1)}, u32[]{:S(2)}) copy-start(f32[32,2048]{1,0:T(8,128)S(1)} %collective-permute-done.2.refs_2_) | copy-start | bytes 786436
  70.6 21.9 %collective-permute-start = (f32[32,1280]{1,0:T(8,128)S(1)}, f32[32,1280]{1,0:T(8,128)S(1)}, u32[]{:S(2)}, u32[]{:S(2)}) collective-permute-start(f32[32,1280]{1,0:T(8,128)S(1)} %copy-done.19), channel_id=1, source_target_pairs={{0,20},{4,16},{8,28},{12,24},{16,4},{20,0},{24,12},{28,8},{1,21},{... | collective-permute-start | bytes 491528 | tf_op jit(solution)/shard_map/ppermute | solution.py:315
  71.0 10.1 %copy-start.13 = (f32[32,2048]{1,0:T(8,128)}, f32[32,2048]{1,0:T(8,128)S(1)}, u32[]{:S(2)}) copy-start(f32[32,2048]{1,0:T(8,128)S(1)} %collective-permute-done.3.refs_3_) | copy-start | bytes 786436
  71.1 16.6 %collective-permute-start.9 = (f32[32,768]{1,0:T(8,128)S(1)}, f32[32,768]{1,0:T(8,128)S(1)}, u32[]{:S(2)}, u32[]{:S(2)}) collective-permute-start(f32[32,768]{1,0:T(8,128)S(1)} %copy-done.21), channel_id=1, source_target_pairs={{0,20},{4,16},{8,28},{12,24},{16,4},{20,0},{24,12},{28,8},{1,21},{... | collective-permute-start | bytes 294920 | tf_op jit(solution)/shard_map/ppermute | solution.py:315
  74.5 6.6 %copy-start.14 = (f32[32,2048]{1,0:T(8,128)}, f32[32,2048]{1,0:T(8,128)S(1)}, u32[]{:S(2)}) copy-start(f32[32,2048]{1,0:T(8,128)S(1)} %collective-permute-done.4.refs_4_) | copy-start | bytes 786436
  74.5 6.6 %copy-start.15 = (f32[32,2048]{1,0:T(8,128)}, f32[32,2048]{1,0:T(8,128)S(1)}, u32[]{:S(2)}) copy-start(f32[32,2048]{1,0:T(8,128)S(1)} %collective-permute-done.5.refs_5_) | copy-start | bytes 786436
  92.2 17.7 %collective-permute-start.10 = (f32[2,32,768]{2,1,0:T(8,128)S(1)}, f32[2,32,768]{2,1,0:T(8,128)S(1)}, u32[]{:S(2)}, u32[]{:S(2)}) collective-permute-start(f32[2,32,768]{2,1,0:T(8,128)S(1)} %dynamic-slice_bitcast_fusion.1), channel_id=1, source_target_pairs={{0,1},{1,0},{2,3},{3,2},{4,5},{5,4},{6,7},{7,6},{8,9},{9,8},{10,11... | collective-permute-start | bytes 589832 | tf_op jit(solution)/shard_map/ppermute | solution.py:270
  93.1 3.5 %copy-start.4 = (f32[32,1]{1,0:T(8,128)S(1)}, f32[32,1]{1,0:T(8,128)}, u32[]{:S(2)}) copy-start(f32[32,1]{1,0:T(8,128)} %get-tuple-element.41) | copy-start | bytes 388
  93.1 16.1 %copy-start.6 = (s32[1,128]{1,0:T(1,128)S(1)}, s32[1,128]{1,0:T(1,128)}, u32[]{:S(2)}) copy-start(s32[1,128]{1,0:T(1,128)} %get-tuple-element.38) | copy-start | bytes 1540
  96.6 13.2 %copy-start.2 = (f32[128,768]{1,0:T(8,128)S(1)}, f32[128,768]{1,0:T(8,128)}, u32[]{:S(2)}) copy-start(f32[128,768]{1,0:T(8,128)} %get-tuple-element.37) | copy-start | bytes 1179652
  98.8 9.7 %all-to-all-start.2 = ((f32[8,1,32]{2,1,0:T(1,128)}), f32[8,1,32]{2,1,0:T(1,128)S(1)}, u32[]{:S(2)}, u32[]{:S(2)}) async-start(f32[8,1,32]{2,1,0:T(1,128)} %bitcast.29), calls=%async_computation.2 | async-start | bytes 8192 | tf_op jit(solution)/shard_map/all_to_all | solution.py:254
  102.3 9.2 %copy-start.1 = (f32[128,1280]{1,0:T(8,128)S(1)}, f32[128,1280]{1,0:T(8,128)}, u32[]{:S(2)}) copy-start(f32[128,1280]{1,0:T(8,128)} %get-tuple-element.34) | copy-start | bytes 1966084
  103.3 8.1 %collective-permute-start.7 = (f32[2,32,1280]{2,1,0:T(8,128)S(1)}, f32[2,32,1280]{2,1,0:T(8,128)S(1)}, u32[]{:S(2)}, u32[]{:S(2)}) collective-permute-start(f32[2,32,1280]{2,1,0:T(8,128)S(1)} %dynamic-slice_bitcast_fusion), channel_id=1, source_target_pairs={{0,1},{1,0},{2,3},{3,2},{4,5},{5,4},{6,7},{7,6},{8,9},{9,8},{10,11... | collective-permute-start | bytes 983048 | tf_op jit(solution)/shard_map/ppermute | solution.py:270
  109.9 5.7 %collective-permute-start.11 = (f32[1,32,768]{2,1,0:T(8,128)S(1)}, f32[1,32,768]{2,1,0:T(8,128)S(1)}, u32[]{:S(2)}, u32[]{:S(2)}) collective-permute-start(f32[1,32,768]{2,1,0:T(8,128)S(1)} %constant_dynamic-slice_fusion), channel_id=1, source_target_pairs={{0,2},{1,3},{2,0},{3,1},{4,6},{5,7},{6,4},{7,5},{8,10},{9,11},{10,... | collective-permute-start | bytes 294920 | tf_op jit(solution)/shard_map/ppermute | solution.py:270
  111.6 6.3 %collective-permute-start.8 = (f32[1,32,1280]{2,1,0:T(8,128)S(1)}, f32[1,32,1280]{2,1,0:T(8,128)S(1)}, u32[]{:S(2)}, u32[]{:S(2)}) collective-permute-start(f32[1,32,1280]{2,1,0:T(8,128)S(1)} %constant_dynamic-slice_fusion.1), channel_id=1, source_target_pairs={{0,2},{1,3},{2,0},{3,1},{4,6},{5,7},{6,4},{7,5},{8,10},{9,11},{10,... | collective-permute-start | bytes 491528 | tf_op jit(solution)/shard_map/ppermute | solution.py:270
  (8 other events, 6.2 us)

commit v2 on v1

v2 whole, which is shorter than its diff:
```python
import functools
import math

import jax
import jax.numpy as jnp
import numpy as np
from jax import lax
from jax.experimental import pallas as pl
from jax.experimental.pallas import tpu as pltpu
from jax.sharding import PartitionSpec as P


K0 = 64
LANES = 128
CUT = 6
GRANT = pltpu.CompilerParams(vmem_limit_bytes=12 * 1024 * 1024)
FIRST = (6,)
SECOND = (7,)
THIRD = (2, 3, 1)
LATE = (4,)
LAST = 5
EARLY = [0, *FIRST, *SECOND, *THIRD]
BASE = 64
F32 = jnp.float32
BF16 = jnp.bfloat16
VMEM = pl.BlockSpec(memory_space=pltpu.VMEM)
NT_DIMS = (((1,), (1,)), ((), ()))


def mm(a, b):
    return jnp.dot(a, b, preferred_element_type=F32)


def split2(x):
    hi = x.astype(BF16)
    return hi, (x - hi.astype(F32)).astype(BF16)


def split3(x):
    hi = x.astype(BF16)
    rest = x - hi.astype(F32)
    mid = rest.astype(BF16)
    return hi, mid, (rest - mid.astype(F32)).astype(BF16)


def phases(products, period):
    angles = (products % period) * (2.0 * math.pi / period)
    return np.cos(angles), np.sin(angles)


def pack_kernel(parts, groups, here_ref, group_ref, receiver_ref, source_ref, observed_ref, *outs):
    pairs = observed_ref.shape[0]
    bins = observed_ref.shape[1] // 2
    capacity = 2 * pairs // groups
    group_row = group_ref[...]
    hits = (
        lax.broadcasted_iota(jnp.int32, (max(groups, 8), pairs), 0) == group_row
    ).astype(F32)
    earlier = (
        lax.broadcasted_iota(jnp.int32, (pairs, pairs), 0)
        < lax.broadcasted_iota(jnp.int32, (pairs, pairs), 1)
    ).astype(F32)
    counts = mm(hits.astype(BF16), earlier.astype(BF16))
    rank = jnp.sum(hits * counts, axis=0, keepdims=True).astype(jnp.int32)

    def chosen(slot_row, start, stop):
        index = start + lax.broadcasted_iota(jnp.int32, (stop - start, pairs), 0)
        return (index == slot_row).astype(F32).astype(BF16)

    if len(outs) > len(parts):
        label_ref, slot_ref = outs[-2:]
        slot_row = group_row * capacity + rank
        slot_ref[...] = slot_row
        labels = jnp.concatenate(
            [receiver_ref[...] + 1, source_ref[...]] + [jnp.zeros((6, pairs), jnp.int32)], axis=0
        ).astype(F32).astype(BF16)
        sent = lax.dot_general(
            labels, chosen(slot_row, 0, groups * capacity), NT_DIMS, preferred_element_type=F32
        )
        code = jnp.broadcast_to(sent[0:1] * 256.0 + sent[1:2], (8, groups * capacity))
        label_ref[...] = jnp.zeros_like(label_ref)
        for group in range(groups):
            label_ref[group, :, :capacity] = code[:, group * capacity : (group + 1) * capacity]
    slot_row = (group_row ^ here_ref[0, 0]) * capacity + rank
    for span in dict.fromkeys(part[1] for part in parts):
        mine = [(tags, ref) for (tags, other), ref in zip(parts, outs) if other == span]
        rows = jnp.concatenate(
            [chosen(slot_row, low * capacity, high * capacity) for (low, high), _ in mine], axis=0
        )
        rows = jnp.concatenate([rows] * 3, axis=1)
        width = span[1] - span[0]
        tile = math.gcd(width, 256)
        for half in range(2):
            for at in range(0, width, tile):
                left = half * bins + span[0] + at
                values = mm(rows, jnp.concatenate(split3(observed_ref[:, left : left + tile]), axis=0))
                top = 0
                for (low, high), out_ref in mine:
                    count = (high - low) * capacity
                    out_ref[:, half * width + at : half * width + at + tile] = values[top : top + count]
                    top += count


def forward_kernel(
    steps, records_ref, cos_a_ref, sin_a_ref, cos_b_ref, sin_b_ref, rows_ref, label_ref,
    white_ref, picked_ref, table, total,
):
    step = pl.program_id(0)
    bins = cos_b_ref.shape[1]
    parts = table.shape[0] // BASE

    @pl.when(step == 0)
    def _():
        total[...] = jnp.zeros_like(total)

    for part in range(parts):
        row = step * parts + part
        cos_a = cos_a_ref[pl.ds(row, 1), :]
        sin_a = sin_a_ref[pl.ds(row, 1), :]
        cos_b = cos_b_ref[...]
        sin_b = sin_b_ref[...]
        rows = slice(part * BASE, (part + 1) * BASE)
        table[rows, :bins] = (cos_a * cos_b - sin_a * sin_b).astype(BF16)
        table[rows, bins:] = (sin_a * cos_b + cos_a * sin_b).astype(BF16)
    total[...] += mm(records_ref[...], table[...])

    @pl.when(step == steps - 1)
    def _():
        spectra = total[...]
        power = jnp.sum(spectra * spectra, axis=1, keepdims=True) / bins
        white = spectra / jnp.sqrt(power + 1e-06)
        white_ref[...] = white
        owners = rows_ref.shape[0]
        chosen = (
            lax.broadcasted_iota(jnp.int32, (owners, white.shape[0]), 1) == rows_ref[...]
        ).astype(F32).astype(BF16)
        picked = mm(jnp.concatenate([chosen] * 3, axis=1), jnp.concatenate(split3(white), axis=0))
        part = picked_ref.shape[2]
        for group in range(picked_ref.shape[0]):
            picked_ref[group, :owners, :] = picked[:, group * part : (group + 1) * part]
        picked_ref[:, owners:, :] = label_ref[...]


def spread_kernel(arrived_ref, out_ref):
    owners = out_ref.shape[1]
    summed = arrived_ref[0, :owners, :]
    for group in range(1, arrived_ref.shape[0]):
        summed = summed + arrived_ref[group, :owners, :]
    out_ref[...] = jnp.broadcast_to(summed[None], out_ref.shape)


def pair_kernel(
    bins, spans, tags, whole_block, starts, older, last_of, split, here_ref, arrived_ref, white_ref, sources_ref, *refs
):
    count = 1 if whole_block else len(tags)
    pieces = split
    refs = list(refs)
    blocks, begun = refs[:count], refs[count : count + starts]
    before = refs[count + starts : count + starts + len(older)]
    refs = refs[count + starts + len(older) :]
    outs, misfits = refs[: sum(pieces)], refs[sum(pieces) :]
    begin = spans[0][0]
    total = spans[-1][1] - begin
    rows = white_ref.shape[0]
    _, owners, part = sources_ref.shape
    capacity = misfits[0].shape[1]
    here, side = here_ref[0, 0], here_ref[0, 1]
    quarter = rows // 4
    gathers, picks = [], []
    for tag in tags:
        code = arrived_ref[tag if whole_block else here ^ tag, owners : owners + 8, :capacity]
        code = code[0:1, :].astype(jnp.int32)
        receiver = code // 256 - 1
        source = code % 256
        hit = (lax.broadcasted_iota(jnp.int32, (rows, capacity), 0) == receiver).astype(F32)
        gathers.append(hit.T)
        hit = (
            (lax.broadcasted_iota(jnp.int32, (LANES, capacity), 0) == source) & (receiver >= 0)
        ).astype(F32)
        picks.append(hit.T)
    gather = jnp.concatenate(gathers, axis=0)
    pick = jnp.concatenate(picks, axis=0).astype(BF16)
    place = lax.broadcasted_iota(jnp.int32, (rows, rows), 0)
    block = place // quarter
    block = (((block & 1) << 1) | (block >> 1)) ^ side
    wanted = block * quarter + place % quarter
    order = (lax.broadcasted_iota(jnp.int32, (rows, rows), 1) == wanted).astype(F32).astype(BF16)
    gather2 = gather.astype(BF16)
    scatter = lax.dot_general(order, gather2, NT_DIMS, preferred_element_type=F32).astype(BF16)
    gather2 = jnp.concatenate([gather2, gather2], axis=1)
    scatter2 = jnp.concatenate([scatter, scatter], axis=1)
    slots = gather.shape[0]
    tile = 2 * LANES if all((last - first) % (2 * LANES) == 0 for first, last in spans) else LANES

    def rows_of(left):
        hi, low = split2(white_ref[:, left : left + tile])
        return mm(gather2, jnp.concatenate([hi, low], axis=0))

    def sources_of(left):
        taken = min(tile, part)
        values = jnp.concatenate(
            [sources_ref[at // part, :, at % part : at % part + taken] for at in range(left, left + tile, taken)],
            axis=1,
        )
        values = jnp.concatenate([values, jnp.zeros((LANES - owners, tile), F32)], axis=0)
        hi, low = split2(values)
        return mm(jnp.concatenate([pick, pick], axis=1), jnp.concatenate([hi, low], axis=0))

    def summed(terms):
        hi, low = split2(terms)
        return mm(scatter2, jnp.concatenate([hi, low], axis=0))

    def seen(half, lo):
        values = []
        for block in blocks:
            left = half * bins + lo if block.shape[1] == 2 * bins else half * total + lo - begin
            values.append(block[:, left : left + tile])
        return jnp.concatenate(values, axis=0)

    misfit = jnp.zeros((slots, tile), F32)
    for number, (first, last) in enumerate(spans):
        width = last - first
        mine = outs[sum(pieces[:number]) : sum(pieces[: number + 1])]

        def put(left, value):
            if starts:
                value = value + begun[number][:, left : left + tile]
            size = rows // len(mine)
            for piece, ref in enumerate(mine):
                ref[:, left : left + tile] = value[piece * size : (piece + 1) * size]

        for at in range(0, width, tile):
            lo = first + at
            index = lo + lax.broadcasted_iota(jnp.int32, (1, tile), 1)
            weights = 0.5 - 0.5 * jnp.cos((index.astype(F32) + 0.5) * (2.0 * math.pi / bins))
            receiver_real, receiver_imag = rows_of(lo), rows_of(bins + lo)
            source_real, source_imag = sources_of(lo), sources_of(bins + lo)
            diff_real = source_real * receiver_real + source_imag * receiver_imag - seen(0, lo)
            diff_imag = source_real * receiver_imag - source_imag * receiver_real - seen(1, lo)
            residual_real = weights * diff_real
            residual_imag = weights * diff_imag
            misfit = misfit + (residual_real * diff_real + residual_imag * diff_imag)
            put(at, summed(residual_real * source_real - residual_imag * source_imag))
            put(width + at, summed(residual_real * source_imag + residual_imag * source_real))
    misfit = jnp.sum(misfit, axis=1, keepdims=True) / (2 * bins)
    index = lax.broadcasted_iota(jnp.int32, (slots, capacity), 0) % capacity
    spots = lax.broadcasted_iota(jnp.int32, (slots, capacity), 1)
    spread = jnp.where(index == spots, misfit, 0.0)
    found = [
        jnp.sum(spread[number * capacity : (number + 1) * capacity], axis=0, keepdims=True)
        for number in range(len(tags))
    ]
    (misfit_ref,) = misfits
    if not last_of:
        for number in range(len(tags)):
            misfit_ref[number : number + 1, :] = found[number]
        return
    for ref, names in zip(before, older):
        for number, tag in enumerate(names):
            value = ref[number : number + 1, :]
            if tag in tags:
                found[tags.index(tag)] = found[tags.index(tag)] + value
            else:
                misfit_ref[pl.ds(here ^ tag, 1), :] = value
    for number, tag in enumerate(tags):
        misfit_ref[pl.ds(tag if whole_block else here ^ tag, 1), :] = found[number]


def looked(returned, slot):
    groups, capacity = returned.shape
    pairs = slot.shape[1]
    group = (
        lax.broadcasted_iota(jnp.int32, (groups, pairs), 0) == slot // capacity
    ).astype(F32).astype(BF16)
    parts = split3(returned.T)
    values = mm(parts[0], group) + mm(parts[1], group) + mm(parts[2], group)
    rank = lax.broadcasted_iota(jnp.int32, (capacity, pairs), 0) == slot % capacity
    return jnp.sum(jnp.where(rank, values, 0.0), axis=0, keepdims=True)


def inverse_kernel(
    scale, sizes, mix_ref, turn_cos_ref, turn_sin_ref, last_ref, slot_ref, returned_ref, *refs
):
    chunks = refs[: sum(sizes)]
    out_ref, misfit_ref, held, wide = refs[-4:]
    misfit_ref[...] = looked(returned_ref[...], slot_ref[...])
    count = out_ref.shape[0]
    blocks = held.shape[1] // 2
    steps = mix_ref.shape[0] // 2
    turns = turn_cos_ref.shape[0]
    at = 0
    for number, size in enumerate(sizes):
        addends = chunks[sum(sizes[:number]) : sum(sizes[: number + 1])]
        width = addends[0].shape[1] // 2
        for block in range(width // LANES):
            for half in range(2):
                left = half * width + block * LANES
                value = addends[0][:count, left : left + LANES]
                for other in addends[1:]:
                    value = value + other[:count, left : left + LANES]
                held[:, half * blocks + at, :] = value
            at += 1
    mix = mix_ref[...]
    last = last_ref[...]
    turn_cos = turn_cos_ref[...]
    turn_sin = turn_sin_ref[...]
    for row in range(count):
        hi, low = split2(held[row])
        mixed = mm(mix, jnp.concatenate([hi, low, hi], axis=0))
        real = jnp.concatenate([mixed[:steps]] * (turns // steps), axis=0)
        imag = jnp.concatenate([mixed[steps:]] * (turns // steps), axis=0)
        turned = jnp.concatenate(
            [real * turn_cos - imag * turn_sin, real * turn_sin + imag * turn_cos], axis=1
        )
        hi, low = split2(turned)
        wide[row] = lax.dot_general(
            last, jnp.concatenate([hi, low, hi], axis=1), NT_DIMS, preferred_element_type=F32
        )
    for block in range(wide.shape[1]):
        out_ref[:, block * LANES : (block + 1) * LANES] = wide[:, block, :] * scale


def bf16_parts(values):
    hi = values.astype(jnp.bfloat16)
    return hi, (values - hi.astype(np.float64)).astype(jnp.bfloat16)


def inverse(slot, returned, spectra, count, time_len, bins):
    period = 2 * time_len
    blocks = bins // LANES
    steps = period // LANES
    turns = LANES
    outer = time_len // turns
    cos, sin = phases(np.arange(steps)[:, None] * np.arange(blocks)[None, :] * LANES, period)
    mix = np.concatenate(
        [np.concatenate([cos, -sin], axis=1), np.concatenate([sin, cos], axis=1)], axis=0
    )
    hi, low = bf16_parts(mix)
    mix = np.concatenate([hi, hi, low], axis=1)
    r = np.arange(LANES)[None, :]
    turn_cos, turn_sin = phases((K0 + r) * np.arange(turns)[:, None], period)
    cos, sin = phases((K0 + r) * np.arange(outer)[:, None] * turns, period)
    hi, low = bf16_parts(np.concatenate([cos, -sin], axis=1))
    last = np.concatenate([hi, hi, low], axis=1)
    chunks = [value for addends in spectra for value in addends]
    sizes = [len(addends) for addends in spectra]
    return pl.pallas_call(
        functools.partial(inverse_kernel, 1.0 / math.sqrt(bins), sizes),
        out_shape=[jax.ShapeDtypeStruct((count, time_len), F32), jax.ShapeDtypeStruct(slot.shape, F32)],
        in_specs=[VMEM] * (6 + len(chunks)),
        out_specs=[VMEM] * 2,
        scratch_shapes=[
            pltpu.VMEM((count, 2 * blocks, LANES), F32),
            pltpu.VMEM((count, outer, LANES), F32),
        ],
        compiler_params=GRANT,
        cost_estimate=pl.CostEstimate(flops=1_000_000_000, bytes_accessed=2_000_000, transcendentals=0),
        name="inverse",
    )(
        in_hbm(mix), in_hbm(np.float32(turn_cos)), in_hbm(np.float32(turn_sin)), in_hbm(last),
        slot, returned, *chunks,
    )


def in_hbm(value):
    return pltpu.with_memory_space_constraint(jnp.asarray(value), pltpu.HBM)


def exchange(value, axis):
    return lax.all_to_all(value, axis, split_axis=0, concat_axis=0, tiled=True)


def over_src(value, step):
    return lax.ppermute(value, "src", [(i, i ^ step) for i in range(4)])


def rows_in_two(kept, sent):
    half = kept.shape[0] // 2
    moved = over_src(sent, 1)
    return [kept, moved, over_src(kept[half:] + moved[half:], 2)]


def rows_in_one(own, *others):
    return [own] + [over_src(value, step) for value, step in zip(others, (2, 1, 3))]


def per_device(records, virtual_sources, pair_group, pair_receiver, pair_source, observed):
    row_count, time_len = records.shape
    pair_count = observed.shape[0]
    bins = observed.shape[1] // 2
    groups = lax.axis_size("chan")
    assert lax.axis_size("src") == 4
    capacity = 2 * pair_count // groups
    slots = groups * capacity
    owners = virtual_sources.shape[0]
    chan_index = lax.axis_index("chan")
    routed = groups == 8
    part = 2 * bins // groups
    cut = bins * CUT // 8
    spans = [(0, cut), (cut, bins)]
    full = (0, bins)
    here = jnp.stack([chan_index if routed else 0 * chan_index, lax.axis_index("src")]).reshape(1, 2)
    smem = pl.BlockSpec(memory_space=pltpu.SMEM)
    lists = (
        here,
        in_hbm(pair_group.reshape(1, pair_count)),
        in_hbm(pair_receiver.reshape(1, pair_count)),
        in_hbm(pair_source.reshape(1, pair_count)),
    )

    def pack(parts, labelled):
        shapes = [
            jax.ShapeDtypeStruct(((high - low) * capacity, 2 * (last - first)), F32)
            for (low, high), (first, last) in parts
        ]
        if labelled:
            shapes.append(jax.ShapeDtypeStruct((groups, 8, part), F32))
            shapes.append(jax.ShapeDtypeStruct((1, pair_count), jnp.int32))
        return pl.pallas_call(
            functools.partial(pack_kernel, parts, groups),
            out_shape=shapes,
            in_specs=[smem] + [VMEM] * 4,
            out_specs=[VMEM] * len(shapes),
            compiler_params=GRANT,
            cost_estimate=pl.CostEstimate(flops=400_000_000, bytes_accessed=3_000_000, transcendentals=0),
            name="pack",
        )(*lists, observed)

    def move(value, tag):
        return lax.ppermute(value, "chan", [(i, i ^ tag) for i in range(groups)])

    if routed:
        *sent, label, slot = pack([((tag, tag + 1), full) for tag in FIRST], True)
        blocks = {tag: move(value, tag) for tag, value in zip(FIRST, sent)}
        rest = [*SECOND, *THIRD, *LATE]
        *sent, last_a, last_b, blocks[0] = pack(
            [((tag, tag + 1), full) for tag in rest]
            + [((LAST, LAST + 1), span) for span in spans]
            + [((0, 1), full)],
            False,
        )
    else:
        own, label, slot = pack([((0, groups), full)], True)

    period = 2 * time_len
    k = K0 + np.arange(bins)[None, :]
    cos_a, sin_a = phases(k * BASE * np.arange(time_len // BASE)[:, None], period)
    cos_b, sin_b = phases(k * np.arange(BASE)[:, None], period)
    steps = 8
    block = time_len // steps
    whole = lambda *shape: pl.BlockSpec(shape, lambda i: (0,) * len(shape))
    whitened, picked = pl.pallas_call(
        functools.partial(forward_kernel, steps),
        grid=(steps,),
        out_shape=[
            jax.ShapeDtypeStruct((row_count, 2 * bins), F32),
            jax.ShapeDtypeStruct((groups, owners + 8, part), F32),
        ],
        in_specs=[
            pl.BlockSpec((row_count, block), lambda i: (0, i)),
            whole(*cos_a.shape), whole(*cos_a.shape), whole(*cos_b.shape), whole(*cos_b.shape),
            whole(owners, 1), whole(groups, 8, part),
        ],
        out_specs=[whole(row_count, 2 * bins), whole(groups, owners + 8, part)],
        scratch_shapes=[pltpu.VMEM((block, 2 * bins), BF16), pltpu.VMEM((row_count, 2 * bins), F32)],
        compiler_params=GRANT,
        cost_estimate=pl.CostEstimate(flops=8_000_000_000, bytes_accessed=4_000_000, transcendentals=0),
        name="forward",
    )(
        records, in_hbm(np.float32(cos_a)), in_hbm(np.float32(-sin_a)), in_hbm(np.float32(cos_b)),
        in_hbm(np.float32(-sin_b)), (virtual_sources - chan_index * row_count).reshape(owners, 1), label,
    )

    arrived = exchange(picked, "chan")
    summed = pl.pallas_call(
        spread_kernel,
        out_shape=jax.ShapeDtypeStruct((groups, owners, part), F32),
        in_specs=[VMEM],
        out_specs=VMEM,
        compiler_params=GRANT,
        cost_estimate=pl.CostEstimate(flops=100_000, bytes_accessed=300_000, transcendentals=0),
        name="spread",
    )(arrived)
    sources = exchange(summed, "chan")

    def terms(values, tags, some, split, begun, before, older=(), last_of=False):
        shapes = [
            jax.ShapeDtypeStruct((row_count // pieces, 2 * (last - first)), F32)
            for (first, last), pieces in zip(some, split)
            for _ in range(pieces)
        ] + [jax.ShapeDtypeStruct((groups if last_of else len(tags), capacity), F32)]
        return pl.pallas_call(
            functools.partial(
                pair_kernel, bins, some, tags, not routed, len(begun), older, last_of, split
            ),
            out_shape=shapes,
            in_specs=[smem] + [VMEM] * (3 + len(values) + len(begun) + len(before)),
            out_specs=[VMEM] * len(shapes),
            compiler_params=GRANT,
            cost_estimate=pl.CostEstimate(flops=2_000_000_000, bytes_accessed=5_000_000, transcendentals=0),
            name="pairs",
        )(here, arrived, whitened, sources, *values, *begun, *before)

    if routed:
        for tag, value in zip(rest, sent):
            blocks[tag] = move(value, tag)
        last_a = move(last_a, LAST)
        last_b = move(last_b, LAST)
        *begun, misfit = terms([blocks[tag] for tag in EARLY], EARLY, spans, (1, 1), [], [])
        older, before = [EARLY], [misfit]
        tags = [*LATE, LAST]
        late = [blocks[tag] for tag in LATE]
        *sums, misfit = terms([*late, last_a], tags, spans[:1], (2,), begun[:1], [])
        older.append(tags)
        before.append(misfit)
        spectra = [rows_in_two(*sums)]
        *sums, misfit = terms([*late, last_b], tags, spans[1:], (4,), begun[1:], before, older, True)
        spectra.append(rows_in_one(*sums))
    else:
        came = exchange(own.reshape(groups, capacity, -1), "chan").reshape(slots, -1)
        *sums, misfit = terms([came], list(range(groups)), spans, (2, 2), [], [], (), True)
        spectra = [rows_in_two(*sums[:2]), rows_in_two(*sums[2:])]

    returned = exchange(misfit, "chan")
    result, pair_misfit = inverse(slot, returned, spectra, row_count // 4, time_len, bins)
    return (result, pair_misfit.reshape(pair_count))


def solution(mesh):
    return jax.shard_map(
        per_device,
        mesh=mesh,
        in_specs=(
            P("chan", None),
            P("src"),
            P(("chan", "src"), None),
            P(("chan", "src")),
            P(("chan", "src")),
            P(("chan", "src"), None),
        ),
        out_specs=(P(("chan", "src"), None), P(("chan", "src"))),
        check_vma=False,
    )
```

time: 126 us -> 106 us (0.84)
  waiting for transfers between devices: 37.4 us -> 20.9 us
  Pallas kernels: 35.7 us -> 25.4 us
  starting transfers between devices: 32.7 us -> 43 us
  blocking collectives: 0 us -> 9.15 us
  local copies, waits for them, and re-layouts: 12.2 us -> 5.18 us
  other arithmetic: 6.37 us -> 0.84 us
    all_to_all x3 -> x2, waiting for transfers between devices: 25.7 us -> 9.27 us  [exchange(): return lax.all_to_all(value, axis, split_axis=0, concat_axis=0, tiled=True)]
    ppermute x8, starting transfers between devices: 15.6 us -> 28.4 us  [move(): return lax.ppermute(value, 'chan', [(i, i ^ tag) for i in range(groups)])]
    all_to_all x0 -> x1, blocking collectives: none -> 9.15 us  [exchange(): return lax.all_to_all(value, axis, split_axis=0, concat_axis=0, tiled=True)]
    pallas_call x4 -> x5, Pallas kernels: 18.9 us -> 12.3 us  [the longest x1 6.52 us: inverse(): pl.pallas_call(functools.partial(inverse_kernel, 1.0 / math.sqrt(bins), s...]
    all_to_all x3 -> x2, starting transfers between devices: 14.3 us -> 10.8 us  [exchange(): return lax.all_to_all(value, axis, split_axis=0, concat_axis=0, tiled=True)]
    ppermute x4 -> x5, waiting for transfers between devices: 5.08 us -> 1.64 us  [over_src(): return lax.ppermute(value, 'src', [(i, i ^ step) for i in range(4)])]
    pallas_call x2, Pallas kernels: 6.7 us -> 3.32 us  [pack(): pl.pallas_call(functools.partial(pack_kernel, parts, groups), out_shape=s...]
    ppermute x8, waiting for transfers between devices: 6.62 us -> 9.99 us  [move(): return lax.ppermute(value, 'chan', [(i, i ^ tag) for i in range(groups)])]
  transfers between devices with their start and end apart: 15 -> 15, of which waited for: 6 -> 5; matrix products, arithmetic and copies ran while one was open for 8% -> 0% of each run, Pallas kernels for 12% -> 6%
where the time goes in v2:
time: 106 us; the launch traced here: 105 us
  starting transfers between devices  43 us (41%)
  Pallas kernels  25.4 us (24%)
  waiting for transfers between devices  20.9 us (20%)
  blocking collectives  9.15 us (9%)
  local copies, waits for them, and re-layouts  5.18 us (5%)
    ppermute x8, starting transfers between devices, move(): return lax.ppermute(value, 'chan', [(i, i ^ tag) for i in range(groups)])  28.4 us
    all_to_all x2, starting transfers between devices, exchange(): return lax.all_to_all(value, axis, split_axis=0, concat_axis=0, tiled=True)  10.8 us
    ppermute x8, waiting for transfers between devices, move(): return lax.ppermute(value, 'chan', [(i, i ^ tag) for i in range(groups)])  9.99 us
    pallas_call x1, Pallas kernels, per_device(): pl.pallas_call(functools.partial(forward_kernel, steps), grid=(steps,), o...  9.71 us
    all_to_all x2, waiting for transfers between devices, exchange(): return lax.all_to_all(value, axis, split_axis=0, concat_axis=0, tiled=True)  9.27 us
    all_to_all x1, blocking collectives, exchange(): return lax.all_to_all(value, axis, split_axis=0, concat_axis=0, tiled=True)  9.15 us
    pallas_call x1, Pallas kernels, inverse(): pl.pallas_call(functools.partial(inverse_kernel, 1.0 / math.sqrt(bins), s...  6.52 us
    pallas_call x3, Pallas kernels, terms(): pl.pallas_call(functools.partial(pair_kernel, bins, some, tags, not route...  5.15 us
  transfers between devices with their start and end apart: 15, of which 5 were waited for; matrix products, arithmetic and copies ran while one was open for 0% of the time, Pallas kernels for 6%

profile of v2, /device:TPU:0, one launch (start us, length us, event | category | flops | bytes accessed | tf_op | source)
XLA Modules:
  0.0 105.2 jit_solution(10254483941214036632)
XLA Ops:
  0.6 0.7 subtract_bitcast_fusion
  1.4 0.1 copy.17.rows_ref
  1.6 1.2 %copy-done.1 = f32[128,2048]{1,0:T(8,128)S(1)} copy-done((f32[128,2048]{1,0:T(8,128)S(1)}, f32[128,2048]{1,0:T(8,128)}, u32[]{:S(2)}) %copy-start.1) | copy-done | bytes 1048600
  2.8 1.2 %pack.2 = (f32[32,2048]{1,0:T(8,128)S(1)}, f32[8,8,256]{2,1,0:T(8,128)S(1)}, s32[1,128]{1,0:T(1,128)S(1)}) custom-call(s32[1,2]{1,0:T(1,128)S(1)} %add_bitcast_fusion.here_ref, s32[1,128]{1,0:T(1,128)} %bitcast.16, s32[1,128]{1,0:T(1,128)} %bitcast.18, s32[1,128]{1,0:T(1,128)} %bitcast.20, f32[128,2048]{1,0:T(8,128)S(1)} %copy-done.1), custom_call_target="tpu_custom_call" | custom-call | flops 400000000 | bytes 3000000 | tf_op jit(solution)/shard_map/pack/pallas_call | solution.py:419
  4.0 9.7 %forward.1 = (f32[128,2048]{1,0:T(8,128)S(1)}, f32[8,24,256]{2,1,0:T(8,128)}) custom-call(bf16[128,4096]{1,0:T(8,128)(2,1)S(1)} %copy-done, f32[64,1024]{1,0:T(8,128)} %constant.27.clone.cos_a_ref, f32[64,1024]{1,0:T(8,128)} %constant.28.clone.sin_a_ref, f32[64,1024]{1,0:T(8,128)} %constant.29.clone.cos_b_ref, f32[64,1024]{1,0:T(8,128)} %constant.30.clone.sin_b_ref, ...), custom_call_target="tpu_custom_call" | custom-call | flops 8000000000 | bytes 4000000 | tf_op jit(solution)/shard_map/forward/pallas_call | solution.py:452
  13.7 1.0 copy-done.7
  14.7 7.3 %all-to-all-start = ((f32[8,24,256]{2,1,0:T(8,128)}), f32[8,24,256]{2,1,0:T(8,128)S(1)}, u32[]{:S(2)}, u32[]{:S(2)}) async-start(f32[8,24,256]{2,1,0:T(8,128)} %get-tuple-element.30), calls=%async_computation | async-start | bytes 393216 | tf_op jit(solution)/shard_map/all_to_all | solution.py:370
  22.0 3.8 %collective-permute-start.2 = (f32[32,2048]{1,0:T(8,128)S(1)}, f32[32,2048]{1,0:T(8,128)S(1)}, u32[]{:S(2)}, u32[]{:S(2)}) collective-permute-start(f32[32,2048]{1,0:T(8,128)S(1)} %get-tuple-element.35), channel_id=1, source_target_pairs={{0,24},{4,28},{8,16},{12,20},{16,8},{20,12},{24,0},{28,4},{1,25},{... | collective-permute-start | bytes 786440 | tf_op jit(solution)/shard_map/ppermute | solution.py:430
  25.8 2.1 %pack.3 = (f32[32,2048]{1,0:T(8,128)}, f32[32,2048]{1,0:T(8,128)S(1)}, f32[32,2048]{1,0:T(8,128)S(1)}, f32[32,2048]{1,0:T(8,128)S(1)}, f32[32,2048]{1,0:T(8,128)...) custom-call(s32[1,2]{1,0:T(1,128)S(1)} %add_bitcast_fusion.here_ref, ...), custom_call_target="tpu_custom_call" | custom-call | flops 400000000 | bytes 3000000 | tf_op jit(solution)/shard_map/pack/pallas_call | solution.py:419
  27.9 0.7 copy-done.3
  28.6 1.5 %collective-permute-start.3 = (f32[32,2048]{1,0:T(8,128)}, f32[32,2048]{1,0:T(8,128)S(1)}, u32[]{:S(2)}, u32[]{:S(2)}) collective-permute-start(f32[32,2048]{1,0:T(8,128)} %get-tuple-element.36), channel_id=1, source_target_pairs={{0,28},{4,24},{8,20},{12,16},{16,12},{20,8},{24,4},{28,0},{1,29},{... | collective-permute-start | bytes 786440 | tf_op jit(solution)/shard_map/ppermute | solution.py:430
  30.1 1.5 %collective-permute-start.5 = (f32[32,2048]{1,0:T(8,128)S(1)}, f32[32,2048]{1,0:T(8,128)S(1)}, u32[]{:S(2)}, u32[]{:S(2)}) collective-permute-start(f32[32,2048]{1,0:T(8,128)S(1)} %get-tuple-element.38), channel_id=1, source_target_pairs={{0,12},{4,8},{8,4},{12,0},{16,28},{20,24},{24,20},{28,16},{1,13},{... | collective-permute-start | bytes 786440 | tf_op jit(solution)/shard_map/ppermute | solution.py:430
  31.6 2.0 %collective-permute-start.6 = (f32[32,2048]{1,0:T(8,128)S(1)}, f32[32,2048]{1,0:T(8,128)S(1)}, u32[]{:S(2)}, u32[]{:S(2)}) collective-permute-start(f32[32,2048]{1,0:T(8,128)S(1)} %get-tuple-element.39), channel_id=1, source_target_pairs={{0,4},{4,0},{8,12},{12,8},{16,20},{20,16},{24,28},{28,24},{1,5},{5... | collective-permute-start | bytes 786440 | tf_op jit(solution)/shard_map/ppermute | solution.py:430
  33.6 8.4 %all-to-all-done.arrived_ref = f32[8,24,256]{2,1,0:T(8,128)S(1)} async-done(((f32[8,24,256]{2,1,0:T(8,128)}), f32[8,24,256]{2,1,0:T(8,128)S(1)}, u32[]{:S(2)}, u32[]{:S(2)}) %all-to-all-start) | async-done | bytes 196640 | tf_op jit(solution)/shard_map/all_to_all | solution.py:370
  42.0 0.7 spread.1
  42.6 3.5 %all-to-all-start.1 = ((f32[8,16,256]{2,1,0:T(8,128)}), f32[8,16,256]{2,1,0:T(8,128)S(1)}, u32[]{:S(2)}, u32[]{:S(2)}) async-start(f32[8,16,256]{2,1,0:T(8,128)} %spread.1), calls=%async_computation.1 | async-start | bytes 262144 | tf_op jit(solution)/shard_map/all_to_all | solution.py:370
  46.2 2.8 %collective-permute-start = (f32[32,2048]{1,0:T(8,128)S(1)}, f32[32,2048]{1,0:T(8,128)S(1)}, u32[]{:S(2)}, u32[]{:S(2)}) collective-permute-start(f32[32,2048]{1,0:T(8,128)S(1)} %get-tuple-element.32), channel_id=1, source_target_pairs={{0,16},{4,20},{8,24},{12,28},{16,0},{20,4},{24,8},{28,12},{1,17},{... | collective-permute-start | bytes 786440 | tf_op jit(solution)/shard_map/ppermute | solution.py:430
  49.0 16.7 %collective-permute-start.7 = (f32[32,1536]{1,0:T(8,128)S(1)}, f32[32,1536]{1,0:T(8,128)S(1)}, u32[]{:S(2)}, u32[]{:S(2)}) collective-permute-start(f32[32,1536]{1,0:T(8,128)S(1)} %copy-done.4), channel_id=1, source_target_pairs={{0,20},{4,16},{8,28},{12,24},{16,4},{20,0},{24,12},{28,8},{1,21},{... | collective-permute-start | bytes 589832 | tf_op jit(solution)/shard_map/ppermute | solution.py:430
  65.7 0.9 all-to-all-done.1.sources_ref
  66.6 0.9 copy-done.6
  67.6 1.2 %copy-done.8 = f32[128,2048]{1,0:T(8,128)S(1)} copy-done((f32[128,2048]{1,0:T(8,128)S(1)}, f32[128,2048]{1,0:T(8,128)}, u32[]{:S(2)}) %copy-start.8) | copy-done | bytes 1048600
  68.8 2.5 %pairs.3 = (f32[128,1536]{1,0:T(8,128)S(1)}, f32[128,512]{1,0:T(8,128)S(1)}, f32[6,32]{1,0:T(8,128)S(1)}) custom-call(s32[1,2]{1,0:T(1,128)S(1)} %add_bitcast_fusion.here_ref, f32[8,24,256]{2,1,0:T(8,128)S(1)} %all-to-all-done.arrived_ref, f32[128,2048]{1,0:T(8,128)S(1)} %copy-done.8, f32[8,16,256]{2,1,0:T(8,128)S(1)} %all-to-all-done.1.sources_ref, ...), custom_call_target="tpu_custom_call" | custom-call | flops 2000000000 | bytes 5000000 | tf_op jit(solution)/shard_map/pairs/pallas_call | solution.py:492
  71.3 7.0 %collective-permute-done.7.refs_1_ = f32[32,1536]{1,0:T(8,128)S(1)} collective-permute-done((f32[32,1536]{1,0:T(8,128)S(1)}, f32[32,1536]{1,0:T(8,128)S(1)}, u32[]{:S(2)}, u32[]{:S(2)}) %collective-permute-start.7) | collective-permute-done | bytes 196640 | tf_op jit(solution)/shard_map/ppermute | solution.py:430
  78.3 1.6 %pairs.4 = (f32[64,1536]{1,0:T(8,128)S(1)}, f32[64,1536]{1,0:T(8,128)S(1)}, f32[2,32]{1,0:T(2,128)S(1)}) custom-call(s32[1,2]{1,0:T(1,128)S(1)} %add_bitcast_fusion.here_ref, f32[8,24,256]{2,1,0:T(8,128)S(1)} %all-to-all-done.arrived_ref, f32[128,2048]{1,0:T(8,128)S(1)} %copy-done.8, f32[8,16,256]{2,1,0:T(8,128)S(1)} %all-to-all-done.1.sources_ref, ...), custom_call_target="tpu_custom_call" | custom-call | flops 2000000000 | bytes 5000000 | tf_op jit(solution)/shard_map/pairs/pallas_call | solution.py:492
  80.0 1.6 %collective-permute-done.8.refs_1_ = f32[64,1536]{1,0:T(8,128)S(1)} collective-permute-done((f32[64,1536]{1,0:T(8,128)S(1)}, f32[64,1536]{1,0:T(8,128)S(1)}, u32[]{:S(2)}, u32[]{:S(2)}) %collective-permute-start.8) | collective-permute-done | bytes 393248 | tf_op jit(solution)/shard_map/ppermute | solution.py:374
  81.7 1.6 %collective-permute-start.9 = (f32[32,1536]{1,0:T(8,128)S(1)}, f32[32,1536]{1,0:T(8,128)S(1)}, u32[]{:S(2)}, u32[]{:S(2)}) collective-permute-start(f32[32,1536]{1,0:T(8,128)S(1)} %slice_add_fusion), channel_id=1, source_target_pairs={{0,2},{1,3},{2,0},{3,1},{4,6},{5,7},{6,4},{7,5},{8,10},{9,11},{10,... | collective-permute-start | bytes 589832 | tf_op jit(solution)/shard_map/ppermute | solution.py:374
  83.2 3.0 %collective-permute-done.1.refs_1_ = f32[32,512]{1,0:T(8,128)S(1)} collective-permute-done((f32[32,512]{1,0:T(8,128)S(1)}, f32[32,512]{1,0:T(8,128)S(1)}, u32[]{:S(2)}, u32[]{:S(2)}) %collective-permute-start.1) | collective-permute-done | bytes 65568 | tf_op jit(solution)/shard_map/ppermute | solution.py:430
  86.2 1.1 %pairs.5 = (f32[32,512]{1,0:T(8,128)S(1)}, f32[32,512]{1,0:T(8,128)S(1)}, f32[32,512]{1,0:T(8,128)S(1)}, f32[32,512]{1,0:T(8,128)S(1)}, f32[8,32]{1,0:T(8,128)S(1)}) custom-call(s32[1,2]{1,0:T(1,128)S(1)} %add_bitcast_fusion.here_ref, f32[8,24,256]{2,1,0:T(8,128)S(1)} %all-to-all-done.arrived_ref, f32[128,2048]{1,0:T(8,128)S(1)} %copy-done.8, ...), custom_call_target="tpu_custom_call" | custom-call | flops 2000000000 | bytes 5000000 | tf_op jit(solution)/shard_map/pairs/pallas_call | solution.py:492
  87.3 1.6 %collective-permute-start.10 = (f32[32,512]{1,0:T(8,128)S(1)}, f32[32,512]{1,0:T(8,128)S(1)}, u32[]{:S(2)}, u32[]{:S(2)}) collective-permute-start(f32[32,512]{1,0:T(8,128)S(1)} %get-tuple-element.49), channel_id=1, source_target_pairs={{0,2},{1,3},{2,0},{3,1},{4,6},{5,7},{6,4},{7,5},{8,10},{9,11},{10,... | collective-permute-start | bytes 196616 | tf_op jit(solution)/shard_map/ppermute | solution.py:374
  88.9 0.6 collective-permute-start.12
  89.5 9.1 %all_to_all.21 = f32[8,1,32]{2,1,0:T(1,128)S(1)} all-to-all(f32[8,1,32]{2,1,0:T(1,128)S(1)} %bitcast.15), channel_id=1, replica_groups=mesh['chan'=8,'src'=4] {'chan'}, dimensions={0} | all-to-all | bytes 2048 | tf_op jit(solution)/shard_map/all_to_all | solution.py:370
  98.7 6.5 %inverse.1 = (f32[32,4096]{1,0:T(8,128)}, f32[1,128]{1,0:T(1,128)}) custom-call(bf16[128,48]{1,0:T(8,128)(2,1)} %constant.31.clone.mix_ref, f32[128,128]{1,0:T(8,128)} %constant.32.clone.turn_cos_ref, f32[128,128]{1,0:T(8,128)} %constant.33.clone.turn_sin_ref, bf16[32,768]{1,0:T(8,128)(2,1)} %constant.34.clone.last_ref, ...), custom_call_target="tpu_custom_call" | custom-call | flops 1000000000 | bytes 2000000 | tf_op jit(solution)/shard_map/inverse/pallas_call | solution.py:347
  (29 shorter events, 0.3 us)
Async XLA Ops:
  0.6 3.4 %copy-start = (bf16[128,4096]{1,0:T(8,128)(2,1)S(1)}, bf16[128,4096]{1,0:T(8,128)(2,1)}, u32[]{:S(2)}) copy-start(bf16[128,4096]{1,0:T(8,128)(2,1)} %records_ref.1) | copy-start | bytes 3145732
  1.6 1.2 %copy-start.1 = (f32[128,2048]{1,0:T(8,128)S(1)}, f32[128,2048]{1,0:T(8,128)}, u32[]{:S(2)}) copy-start(f32[128,2048]{1,0:T(8,128)} %observed_ref.3) | copy-start | bytes 3145732
  4.0 21.8 %copy-start.2 = (f32[128,2048]{1,0:T(8,128)S(1)}, f32[128,2048]{1,0:T(8,128)}, u32[]{:S(2)}) copy-start(f32[128,2048]{1,0:T(8,128)} %observed_ref.3) | copy-start | bytes 3145732
  13.7 1.0 copy-start.7
  14.7 27.2 %all-to-all-start = ((f32[8,24,256]{2,1,0:T(8,128)}), f32[8,24,256]{2,1,0:T(8,128)S(1)}, u32[]{:S(2)}, u32[]{:S(2)}) async-start(f32[8,24,256]{2,1,0:T(8,128)} %get-tuple-element.30), calls=%async_computation | async-start | bytes 393216 | tf_op jit(solution)/shard_map/all_to_all | solution.py:370
  22.0 24.1 %collective-permute-start.2 = (f32[32,2048]{1,0:T(8,128)S(1)}, f32[32,2048]{1,0:T(8,128)S(1)}, u32[]{:S(2)}, u32[]{:S(2)}) collective-permute-start(f32[32,2048]{1,0:T(8,128)S(1)} %get-tuple-element.35), channel_id=1, source_target_pairs={{0,24},{4,28},{8,16},{12,20},{16,8},{20,12},{24,0},{28,4},{1,25},{... | collective-permute-start | bytes 786440 | tf_op jit(solution)/shard_map/ppermute | solution.py:430
  27.9 0.7 copy-start.3
  28.6 14.0 %copy-start.5 = (f32[32,2048]{1,0:T(8,128)}, f32[32,2048]{1,0:T(8,128)S(1)}, u32[]{:S(2)}) copy-start(f32[32,2048]{1,0:T(8,128)S(1)} %get-tuple-element.34.refs_0_) | copy-start | bytes 786436
  28.6 20.4 %collective-permute-start.3 = (f32[32,2048]{1,0:T(8,128)}, f32[32,2048]{1,0:T(8,128)S(1)}, u32[]{:S(2)}, u32[]{:S(2)}) collective-permute-start(f32[32,2048]{1,0:T(8,128)} %get-tuple-element.36), channel_id=1, source_target_pairs={{0,28},{4,24},{8,20},{12,16},{16,12},{20,8},{24,4},{28,0},{1,29},{... | collective-permute-start | bytes 786440 | tf_op jit(solution)/shard_map/ppermute | solution.py:430
  30.1 35.7 %collective-permute-start.4 = (f32[32,2048]{1,0:T(8,128)S(1)}, f32[32,2048]{1,0:T(8,128)S(1)}, u32[]{:S(2)}, u32[]{:S(2)}) collective-permute-start(f32[32,2048]{1,0:T(8,128)S(1)} %get-tuple-element.37), channel_id=1, source_target_pairs={{0,8},{4,12},{8,0},{12,4},{16,24},{20,28},{24,16},{28,20},{1,9},{5... | collective-permute-start | bytes 786440 | tf_op jit(solution)/shard_map/ppermute | solution.py:430
  30.1 35.7 %collective-permute-start.5 = (f32[32,2048]{1,0:T(8,128)S(1)}, f32[32,2048]{1,0:T(8,128)S(1)}, u32[]{:S(2)}, u32[]{:S(2)}) collective-permute-start(f32[32,2048]{1,0:T(8,128)S(1)} %get-tuple-element.38), channel_id=1, source_target_pairs={{0,12},{4,8},{8,4},{12,0},{16,28},{20,24},{24,20},{28,16},{1,13},{... | collective-permute-start | bytes 786440 | tf_op jit(solution)/shard_map/ppermute | solution.py:430
  31.6 34.2 %collective-permute-start.6 = (f32[32,2048]{1,0:T(8,128)S(1)}, f32[32,2048]{1,0:T(8,128)S(1)}, u32[]{:S(2)}, u32[]{:S(2)}) collective-permute-start(f32[32,2048]{1,0:T(8,128)S(1)} %get-tuple-element.39), channel_id=1, source_target_pairs={{0,4},{4,0},{8,12},{12,8},{16,20},{20,16},{24,28},{28,24},{1,5},{5... | collective-permute-start | bytes 786440 | tf_op jit(solution)/shard_map/ppermute | solution.py:430
  42.6 6.4 %copy-start.4 = (f32[32,1536]{1,0:T(8,128)S(1)}, f32[32,1536]{1,0:T(8,128)}, u32[]{:S(2)}) copy-start(f32[32,1536]{1,0:T(8,128)} %copy-done.3) | copy-start | bytes 589828
  42.6 24.0 %all-to-all-start.1 = ((f32[8,16,256]{2,1,0:T(8,128)}), f32[8,16,256]{2,1,0:T(8,128)S(1)}, u32[]{:S(2)}, u32[]{:S(2)}) async-start(f32[8,16,256]{2,1,0:T(8,128)} %spread.1), calls=%async_computation.1 | async-start | bytes 262144 | tf_op jit(solution)/shard_map/all_to_all | solution.py:370
  46.2 32.1 %collective-permute-start = (f32[32,2048]{1,0:T(8,128)S(1)}, f32[32,2048]{1,0:T(8,128)S(1)}, u32[]{:S(2)}, u32[]{:S(2)}) collective-permute-start(f32[32,2048]{1,0:T(8,128)S(1)} %get-tuple-element.32), channel_id=1, source_target_pairs={{0,16},{4,20},{8,24},{12,28},{16,0},{20,4},{24,8},{28,12},{1,17},{... | collective-permute-start | bytes 786440 | tf_op jit(solution)/shard_map/ppermute | solution.py:430
  49.0 29.3 %collective-permute-start.7 = (f32[32,1536]{1,0:T(8,128)S(1)}, f32[32,1536]{1,0:T(8,128)S(1)}, u32[]{:S(2)}, u32[]{:S(2)}) collective-permute-start(f32[32,1536]{1,0:T(8,128)S(1)} %copy-done.4), channel_id=1, source_target_pairs={{0,20},{4,16},{8,28},{12,24},{16,4},{20,0},{24,12},{28,8},{1,21},{... | collective-permute-start | bytes 589832 | tf_op jit(solution)/shard_map/ppermute | solution.py:430
  66.6 1.0 copy-start.6
  67.6 1.2 %copy-start.8 = (f32[128,2048]{1,0:T(8,128)S(1)}, f32[128,2048]{1,0:T(8,128)}, u32[]{:S(2)}) copy-start(f32[128,2048]{1,0:T(8,128)} %copy-done.7) | copy-start | bytes 3145732
  79.9 1.8 %collective-permute-start.8 = (f32[64,1536]{1,0:T(8,128)S(1)}, f32[64,1536]{1,0:T(8,128)S(1)}, u32[]{:S(2)}, u32[]{:S(2)}) collective-permute-start(f32[64,1536]{1,0:T(8,128)S(1)} %get-tuple-element.47), channel_id=1, source_target_pairs={{0,1},{1,0},{2,3},{3,2},{4,5},{5,4},{6,7},{7,6},{8,9},{9,8},{10,11... | collective-permute-start | bytes 1179656 | tf_op jit(solution)/shard_map/ppermute | solution.py:374
  79.9 6.3 %collective-permute-start.1 = (f32[32,512]{1,0:T(8,128)S(1)}, f32[32,512]{1,0:T(8,128)S(1)}, u32[]{:S(2)}, u32[]{:S(2)}) collective-permute-start(f32[32,512]{1,0:T(8,128)S(1)} %get-tuple-element.33), channel_id=1, source_target_pairs={{0,20},{4,16},{8,28},{12,24},{16,4},{20,0},{24,12},{28,8},{1,21},{... | collective-permute-start | bytes 196616 | tf_op jit(solution)/shard_map/ppermute | solution.py:430
  81.7 17.0 %collective-permute-start.9 = (f32[32,1536]{1,0:T(8,128)S(1)}, f32[32,1536]{1,0:T(8,128)S(1)}, u32[]{:S(2)}, u32[]{:S(2)}) collective-permute-start(f32[32,1536]{1,0:T(8,128)S(1)} %slice_add_fusion), channel_id=1, source_target_pairs={{0,2},{1,3},{2,0},{3,1},{4,6},{5,7},{6,4},{7,5},{8,10},{9,11},{10,... | collective-permute-start | bytes 589832 | tf_op jit(solution)/shard_map/ppermute | solution.py:374
  87.3 11.4 %collective-permute-start.10 = (f32[32,512]{1,0:T(8,128)S(1)}, f32[32,512]{1,0:T(8,128)S(1)}, u32[]{:S(2)}, u32[]{:S(2)}) collective-permute-start(f32[32,512]{1,0:T(8,128)S(1)} %get-tuple-element.49), channel_id=1, source_target_pairs={{0,2},{1,3},{2,0},{3,1},{4,6},{5,7},{6,4},{7,5},{8,10},{9,11},{10,... | collective-permute-start | bytes 196616 | tf_op jit(solution)/shard_map/ppermute | solution.py:374
  88.9 9.8 %collective-permute-start.11 = (f32[32,512]{1,0:T(8,128)S(1)}, f32[32,512]{1,0:T(8,128)S(1)}, u32[]{:S(2)}, u32[]{:S(2)}) collective-permute-start(f32[32,512]{1,0:T(8,128)S(1)} %get-tuple-element.50), channel_id=1, source_target_pairs={{0,1},{1,0},{2,3},{3,2},{4,5},{5,4},{6,7},{7,6},{8,9},{9,8},{10,11... | collective-permute-start | bytes 196616 | tf_op jit(solution)/shard_map/ppermute | solution.py:374
  88.9 9.8 %collective-permute-start.12 = (f32[32,512]{1,0:T(8,128)S(1)}, f32[32,512]{1,0:T(8,128)S(1)}, u32[]{:S(2)}, u32[]{:S(2)}) collective-permute-start(f32[32,512]{1,0:T(8,128)S(1)} %get-tuple-element.51), channel_id=1, source_target_pairs={{0,3},{1,2},{2,1},{3,0},{4,7},{5,6},{6,5},{7,4},{8,11},{9,10},{10,... | collective-permute-start | bytes 196616 | tf_op jit(solution)/shard_map/ppermute | solution.py:374

commit v3 on v2

--- a/solution.py
+++ b/solution.py
@@ -12,13 +12,14 @@
 
 K0 = 64
 LANES = 128
-CUT = 6
+CUT = 5
+TOGETHER = 2
 GRANT = pltpu.CompilerParams(vmem_limit_bytes=12 * 1024 * 1024)
-FIRST = (6,)
-SECOND = (7,)
+FIRST = (5,)
+SECOND = (6,)
 THIRD = (2, 3, 1)
-LATE = (4,)
-LAST = 5
+LATE = (7,)
+LAST = 4
 EARLY = [0, *FIRST, *SECOND, *THIRD]
 BASE = 64
 F32 = jnp.float32
@@ -103,26 +104,20 @@
 
 def forward_kernel(
     steps, records_ref, cos_a_ref, sin_a_ref, cos_b_ref, sin_b_ref, rows_ref, label_ref,
-    white_ref, picked_ref, table, total,
+    white_ref, picked_ref, table_real, table_imag, total,
 ):
     step = pl.program_id(0)
-    bins = cos_b_ref.shape[1]
-    parts = table.shape[0] // BASE
-
-    @pl.when(step == 0)
-    def _():
-        total[...] = jnp.zeros_like(total)
-
-    for part in range(parts):
-        row = step * parts + part
-        cos_a = cos_a_ref[pl.ds(row, 1), :]
-        sin_a = sin_a_ref[pl.ds(row, 1), :]
-        cos_b = cos_b_ref[...]
-        sin_b = sin_b_ref[...]
-        rows = slice(part * BASE, (part + 1) * BASE)
-        table[rows, :bins] = (cos_a * cos_b - sin_a * sin_b).astype(BF16)
-        table[rows, bins:] = (sin_a * cos_b + cos_a * sin_b).astype(BF16)
-    total[...] += mm(records_ref[...], table[...])
+    width = cos_b_ref.shape[1]
+    bins = steps * width
+    cos_b, sin_b = cos_b_ref[...], sin_b_ref[...]
+    for row in range(cos_a_ref.shape[0]):
+        cos_a, sin_a = cos_a_ref[row : row + 1, :], sin_a_ref[row : row + 1, :]
+        rows = slice(row * BASE, (row + 1) * BASE)
+        table_real[rows, :] = (cos_a * cos_b - sin_a * sin_b).astype(BF16)
+        table_imag[rows, :] = (sin_a * cos_b + cos_a * sin_b).astype(BF16)
+    left = pl.multiple_of(step * width, width)
+    total[:, pl.ds(left, width)] = mm(records_ref[...], table_real[...])
+    total[:, pl.ds(bins + left, width)] = mm(records_ref[...], table_imag[...])
 
     @pl.when(step == steps - 1)
     def _():
@@ -266,28 +261,27 @@
         misfit_ref[pl.ds(tag if whole_block else here ^ tag, 1), :] = found[number]
 
 
-def looked(returned, slot):
-    groups, capacity = returned.shape
+def look_kernel(returned_ref, slot_ref, out_ref):
+    groups, capacity = returned_ref.shape
+    slot = slot_ref[...]
     pairs = slot.shape[1]
     group = (
         lax.broadcasted_iota(jnp.int32, (groups, pairs), 0) == slot // capacity
     ).astype(F32).astype(BF16)
-    parts = split3(returned.T)
+    parts = split3(returned_ref[...].T)
     values = mm(parts[0], group) + mm(parts[1], group) + mm(parts[2], group)
     rank = lax.broadcasted_iota(jnp.int32, (capacity, pairs), 0) == slot % capacity
-    return jnp.sum(jnp.where(rank, values, 0.0), axis=0, keepdims=True)
+    out_ref[...] = jnp.sum(jnp.where(rank, values, 0.0), axis=0, keepdims=True)
 
 
 def inverse_kernel(
-    scale, sizes, mix_ref, turn_cos_ref, turn_sin_ref, last_ref, slot_ref, returned_ref, *refs
+    scale, sizes, mix_ref, turn_cos_ref, turn_sin_ref, last_ref, *refs
 ):
     chunks = refs[: sum(sizes)]
-    out_ref, misfit_ref, held, wide = refs[-4:]
-    misfit_ref[...] = looked(returned_ref[...], slot_ref[...])
+    out_ref, held, wide = refs[-3:]
     count = out_ref.shape[0]
     blocks = held.shape[1] // 2
-    steps = mix_ref.shape[0] // 2
-    turns = turn_cos_ref.shape[0]
+    turns = turn_cos_ref.shape[1]
     at = 0
     for number, size in enumerate(sizes):
         addends = chunks[sum(sizes[:number]) : sum(sizes[: number + 1])]
@@ -304,18 +298,25 @@
     last = last_ref[...]
     turn_cos = turn_cos_ref[...]
     turn_sin = turn_sin_ref[...]
-    for row in range(count):
-        hi, low = split2(held[row])
-        mixed = mm(mix, jnp.concatenate([hi, low, hi], axis=0))
-        real = jnp.concatenate([mixed[:steps]] * (turns // steps), axis=0)
-        imag = jnp.concatenate([mixed[steps:]] * (turns // steps), axis=0)
-        turned = jnp.concatenate(
-            [real * turn_cos - imag * turn_sin, real * turn_sin + imag * turn_cos], axis=1
-        )
-        hi, low = split2(turned)
-        wide[row] = lax.dot_general(
-            last, jnp.concatenate([hi, low, hi], axis=1), NT_DIMS, preferred_element_type=F32
-        )
+    for row in range(0, count, TOGETHER):
+        some = range(row, row + TOGETHER)
+        hi, low = split2(jnp.concatenate([held[i].T for i in some], axis=0))
+        mixed = mm(jnp.concatenate([hi, low, hi], axis=1), mix)
+        his, lows = [], []
+        for i in range(TOGETHER):
+            real = mixed[i * LANES : (i + 1) * LANES, :turns]
+            imag = mixed[i * LANES : (i + 1) * LANES, turns:]
+            hi, low = split2(
+                jnp.concatenate(
+                    [real * turn_cos - imag * turn_sin, real * turn_sin + imag * turn_cos], axis=0
+                )
+            )
+            his.append(hi)
+            lows.append(low)
+        hi, low = jnp.concatenate(his, axis=1), jnp.concatenate(lows, axis=1)
+        values = mm(last, jnp.concatenate([hi, low, hi], axis=0))
+        for i, at in enumerate(some):
+            wide[at] = values[:, i * turns : (i + 1) * turns]
     for block in range(wide.shape[1]):
         out_ref[:, block * LANES : (block + 1) * LANES] = wide[:, block, :] * scale
 
@@ -325,7 +326,7 @@
     return hi, (values - hi.astype(np.float64)).astype(jnp.bfloat16)
 
 
-def inverse(slot, returned, spectra, count, time_len, bins):
+def inverse(spectra, count, time_len, bins):
     period = 2 * time_len
     blocks = bins // LANES
     steps = period // LANES
@@ -333,22 +334,24 @@
     outer = time_len // turns
     cos, sin = phases(np.arange(steps)[:, None] * np.arange(blocks)[None, :] * LANES, period)
     mix = np.concatenate(
-        [np.concatenate([cos, -sin], axis=1), np.concatenate([sin, cos], axis=1)], axis=0
-    )
+        [np.concatenate([cos, -sin], axis=1)] * (turns // steps)
+        + [np.concatenate([sin, cos], axis=1)] * (turns // steps),
+        axis=0,
+    ).T
     hi, low = bf16_parts(mix)
-    mix = np.concatenate([hi, hi, low], axis=1)
-    r = np.arange(LANES)[None, :]
-    turn_cos, turn_sin = phases((K0 + r) * np.arange(turns)[:, None], period)
-    cos, sin = phases((K0 + r) * np.arange(outer)[:, None] * turns, period)
+    mix = np.concatenate([hi, hi, low], axis=0)
+    r = np.arange(LANES)
+    turn_cos, turn_sin = phases((K0 + r)[:, None] * np.arange(turns)[None, :], period)
+    cos, sin = phases((K0 + r)[None, :] * np.arange(outer)[:, None] * turns, period)
     hi, low = bf16_parts(np.concatenate([cos, -sin], axis=1))
     last = np.concatenate([hi, hi, low], axis=1)
     chunks = [value for addends in spectra for value in addends]
     sizes = [len(addends) for addends in spectra]
     return pl.pallas_call(
         functools.partial(inverse_kernel, 1.0 / math.sqrt(bins), sizes),
-        out_shape=[jax.ShapeDtypeStruct((count, time_len), F32), jax.ShapeDtypeStruct(slot.shape, F32)],
-        in_specs=[VMEM] * (6 + len(chunks)),
-        out_specs=[VMEM] * 2,
+        out_shape=jax.ShapeDtypeStruct((count, time_len), F32),
+        in_specs=[VMEM] * (4 + len(chunks)),
+        out_specs=VMEM,
         scratch_shapes=[
             pltpu.VMEM((count, 2 * blocks, LANES), F32),
             pltpu.VMEM((count, outer, LANES), F32),
@@ -358,7 +361,7 @@
         name="inverse",
     )(
         in_hbm(mix), in_hbm(np.float32(turn_cos)), in_hbm(np.float32(turn_sin)), in_hbm(last),
-        slot, returned, *chunks,
+        *chunks,
     )
 
 
@@ -446,8 +449,8 @@
     k = K0 + np.arange(bins)[None, :]
     cos_a, sin_a = phases(k * BASE * np.arange(time_len // BASE)[:, None], period)
     cos_b, sin_b = phases(k * np.arange(BASE)[:, None], period)
-    steps = 8
-    block = time_len // steps
+    steps = 4
+    tile = bins // steps
     whole = lambda *shape: pl.BlockSpec(shape, lambda i: (0,) * len(shape))
     whitened, picked = pl.pallas_call(
         functools.partial(forward_kernel, steps),
@@ -457,12 +460,12 @@
             jax.ShapeDtypeStruct((groups, owners + 8, part), F32),
         ],
         in_specs=[
-            pl.BlockSpec((row_count, block), lambda i: (0, i)),
-            whole(*cos_a.shape), whole(*cos_a.shape), whole(*cos_b.shape), whole(*cos_b.shape),
+            whole(row_count, time_len),
+            *[pl.BlockSpec((value.shape[0], tile), lambda i: (0, i)) for value in (cos_a, cos_a, cos_b, cos_b)],
             whole(owners, 1), whole(groups, 8, part),
         ],
         out_specs=[whole(row_count, 2 * bins), whole(groups, owners + 8, part)],
-        scratch_shapes=[pltpu.VMEM((block, 2 * bins), BF16), pltpu.VMEM((row_count, 2 * bins), F32)],
+        scratch_shapes=[pltpu.VMEM((time_len, tile), BF16)] * 2 + [pltpu.VMEM((row_count, 2 * bins), F32)],
         compiler_params=GRANT,
         cost_estimate=pl.CostEstimate(flops=8_000_000_000, bytes_accessed=4_000_000, transcendentals=0),
         name="forward",
@@ -522,7 +525,16 @@
         spectra = [rows_in_two(*sums[:2]), rows_in_two(*sums[2:])]
 
     returned = exchange(misfit, "chan")
-    result, pair_misfit = inverse(slot, returned, spectra, row_count // 4, time_len, bins)
+    result = inverse(spectra, row_count // 4, time_len, bins)
+    pair_misfit = pl.pallas_call(
+        look_kernel,
+        out_shape=jax.ShapeDtypeStruct((1, pair_count), F32),
+        in_specs=[VMEM] * 2,
+        out_specs=VMEM,
+        compiler_params=GRANT,
+        cost_estimate=pl.CostEstimate(flops=100_000, bytes_accessed=3000, transcendentals=0),
+        name="look",
+    )(returned, slot)
     return (result, pair_misfit.reshape(pair_count))
 
 

time: 106 us -> 100 us (0.943)
  starting transfers between devices: 43 us -> 36.5 us
  Pallas kernels: 25.4 us -> 23.3 us
  blocking collectives: 9.15 us -> 11.1 us
    ppermute x8, starting transfers between devices: 28.4 us -> 22 us  [move(): return lax.ppermute(value, 'chan', [(i, i ^ tag) for i in range(groups)])]
    pallas_call x1, Pallas kernels: 9.71 us -> 7.21 us  [per_device(): pl.pallas_call(functools.partial(forward_kernel, steps), grid=(steps,), o...]
    all_to_all x1, blocking collectives: 9.15 us -> 11.1 us  [exchange(): return lax.all_to_all(value, axis, split_axis=0, concat_axis=0, tiled=True)]
    pallas_call x1, Pallas kernels: 6.52 us -> 4.84 us  [inverse(): pl.pallas_call(functools.partial(inverse_kernel, 1.0 / math.sqrt(bins), s...]
    pallas_call x3, Pallas kernels: 5.15 us -> 6.58 us  [terms(): pl.pallas_call(functools.partial(pair_kernel, bins, some, tags, not route...]
    all_to_all x2, waiting for transfers between devices: 9.27 us -> 10.4 us  [exchange(): return lax.all_to_all(value, axis, split_axis=0, concat_axis=0, tiled=True)]
    unnamed x18 -> x20, local copies, waits for them, and re-layouts: 5.09 us -> 5.1 us
  transfers between devices with their start and end apart: 15 -> 15, of which waited for: 5 -> 6; matrix products, arithmetic and copies ran while one was open for 0% -> 0% of each run, Pallas kernels for 6% -> 8%
where the time goes in v3:
time: 100 us; the launch traced here: 99.5 us
  starting transfers between devices  36.5 us (36%)
  Pallas kernels  23.3 us (23%)
  waiting for transfers between devices  21.8 us (22%)
  blocking collectives  11.1 us (11%)
  local copies, waits for them, and re-layouts  5.19 us (5%)
    ppermute x8, starting transfers between devices, move(): return lax.ppermute(value, 'chan', [(i, i ^ tag) for i in range(groups)])  22 us
    all_to_all x1, blocking collectives, exchange(): return lax.all_to_all(value, axis, split_axis=0, concat_axis=0, tiled=True)  11.1 us
    all_to_all x2, starting transfers between devices, exchange(): return lax.all_to_all(value, axis, split_axis=0, concat_axis=0, tiled=True)  10.7 us
    all_to_all x2, waiting for transfers between devices, exchange(): return lax.all_to_all(value, axis, split_axis=0, concat_axis=0, tiled=True)  10.4 us
    ppermute x8, waiting for transfers between devices, move(): return lax.ppermute(value, 'chan', [(i, i ^ tag) for i in range(groups)])  9.89 us
    pallas_call x1, Pallas kernels, per_device(): pl.pallas_call(functools.partial(forward_kernel, steps), grid=(steps,), o...  7.21 us
    pallas_call x3, Pallas kernels, terms(): pl.pallas_call(functools.partial(pair_kernel, bins, some, tags, not route...  6.58 us
    unnamed x20, local copies, waits for them, and re-layouts  5.1 us
  transfers between devices with their start and end apart: 15, of which 6 were waited for; matrix products, arithmetic and copies ran while one was open for 0% of the time, Pallas kernels for 8%

profile of v3, /device:TPU:0, one launch (start us, length us, event | category | flops | bytes accessed | tf_op | source)
XLA Modules:
  0.0 99.5 jit_solution(18293619212919490807)
XLA Ops:
  0.6 0.7 subtract_bitcast_fusion
  1.6 1.2 %copy-done.1 = f32[128,2048]{1,0:T(8,128)S(1)} copy-done((f32[128,2048]{1,0:T(8,128)S(1)}, f32[128,2048]{1,0:T(8,128)}, u32[]{:S(2)}) %copy-start.1) | copy-done | bytes 1048600
  2.8 1.2 %pack.2 = (f32[32,2048]{1,0:T(8,128)S(1)}, f32[8,8,256]{2,1,0:T(8,128)S(1)}, s32[1,128]{1,0:T(1,128)S(1)}) custom-call(s32[1,2]{1,0:T(1,128)S(1)} %add_bitcast_fusion.here_ref, s32[1,128]{1,0:T(1,128)} %bitcast.17, s32[1,128]{1,0:T(1,128)} %bitcast.19, s32[1,128]{1,0:T(1,128)} %bitcast.21, f32[128,2048]{1,0:T(8,128)S(1)} %copy-done.1), custom_call_target="tpu_custom_call" | custom-call | flops 400000000 | bytes 3000000 | tf_op jit(solution)/shard_map/pack/pallas_call | solution.py:422
  4.0 7.2 %forward.1 = (f32[128,2048]{1,0:T(8,128)S(1)}, f32[8,24,256]{2,1,0:T(8,128)}) custom-call(bf16[128,4096]{1,0:T(8,128)(2,1)S(1)} %copy-done, f32[64,1024]{1,0:T(8,128)} %constant.27.clone.cos_a_ref, f32[64,1024]{1,0:T(8,128)} %constant.28.clone.sin_a_ref, f32[64,1024]{1,0:T(8,128)} %constant.29.clone.cos_b_ref, f32[64,1024]{1,0:T(8,128)} %constant.30.clone.sin_b_ref, ...), custom_call_target="tpu_custom_call" | custom-call | flops 8000000000 | bytes 4000000 | tf_op jit(solution)/shard_map/forward/pallas_call | solution.py:455
  11.3 1.0 copy-done.8
  12.2 7.3 %all-to-all-start = ((f32[8,24,256]{2,1,0:T(8,128)}), f32[8,24,256]{2,1,0:T(8,128)S(1)}, u32[]{:S(2)}, u32[]{:S(2)}) async-start(f32[8,24,256]{2,1,0:T(8,128)} %get-tuple-element.27), calls=%async_computation | async-start | bytes 393216 | tf_op jit(solution)/shard_map/all_to_all | solution.py:373
  19.5 3.8 %collective-permute-start.2 = (f32[32,2048]{1,0:T(8,128)S(1)}, f32[32,2048]{1,0:T(8,128)S(1)}, u32[]{:S(2)}, u32[]{:S(2)}) collective-permute-start(f32[32,2048]{1,0:T(8,128)S(1)} %get-tuple-element.32), channel_id=1, source_target_pairs={{0,20},{4,16},{8,28},{12,24},{16,4},{20,0},{24,12},{28,8},{1,21},{... | collective-permute-start | bytes 786440 | tf_op jit(solution)/shard_map/ppermute | solution.py:433
  23.3 2.1 %pack.3 = (f32[32,2048]{1,0:T(8,128)}, f32[32,2048]{1,0:T(8,128)S(1)}, f32[32,2048]{1,0:T(8,128)S(1)}, f32[32,2048]{1,0:T(8,128)S(1)}, f32[32,2048]{1,0:T(8,128)...) custom-call(s32[1,2]{1,0:T(1,128)S(1)} %add_bitcast_fusion.here_ref, ...), custom_call_target="tpu_custom_call" | custom-call | flops 400000000 | bytes 3000000 | tf_op jit(solution)/shard_map/pack/pallas_call | solution.py:422
  25.4 0.7 copy-done.6
  26.1 1.5 %collective-permute-start.3 = (f32[32,2048]{1,0:T(8,128)}, f32[32,2048]{1,0:T(8,128)S(1)}, u32[]{:S(2)}, u32[]{:S(2)}) collective-permute-start(f32[32,2048]{1,0:T(8,128)} %get-tuple-element.33), channel_id=1, source_target_pairs={{0,24},{4,28},{8,16},{12,20},{16,8},{20,12},{24,0},{28,4},{1,25},{... | collective-permute-start | bytes 786440 | tf_op jit(solution)/shard_map/ppermute | solution.py:433
  27.6 2.0 %collective-permute-start.5 = (f32[32,2048]{1,0:T(8,128)S(1)}, f32[32,2048]{1,0:T(8,128)S(1)}, u32[]{:S(2)}, u32[]{:S(2)}) collective-permute-start(f32[32,2048]{1,0:T(8,128)S(1)} %get-tuple-element.35), channel_id=1, source_target_pairs={{0,12},{4,8},{8,4},{12,0},{16,28},{20,24},{24,20},{28,16},{1,13},{... | collective-permute-start | bytes 786440 | tf_op jit(solution)/shard_map/ppermute | solution.py:433
  29.6 1.5 %collective-permute-start.6 = (f32[32,2048]{1,0:T(8,128)S(1)}, f32[32,2048]{1,0:T(8,128)S(1)}, u32[]{:S(2)}, u32[]{:S(2)}) collective-permute-start(f32[32,2048]{1,0:T(8,128)S(1)} %get-tuple-element.36), channel_id=1, source_target_pairs={{0,4},{4,0},{8,12},{12,8},{16,20},{20,16},{24,28},{28,24},{1,5},{5... | collective-permute-start | bytes 786440 | tf_op jit(solution)/shard_map/ppermute | solution.py:433
  31.1 8.5 %all-to-all-done.arrived_ref = f32[8,24,256]{2,1,0:T(8,128)S(1)} async-done(((f32[8,24,256]{2,1,0:T(8,128)}), f32[8,24,256]{2,1,0:T(8,128)S(1)}, u32[]{:S(2)}, u32[]{:S(2)}) %all-to-all-start) | async-done | bytes 196640 | tf_op jit(solution)/shard_map/all_to_all | solution.py:373
  39.6 0.7 spread.1
  40.2 3.4 %all-to-all-start.1 = ((f32[8,16,256]{2,1,0:T(8,128)}), f32[8,16,256]{2,1,0:T(8,128)S(1)}, u32[]{:S(2)}, u32[]{:S(2)}) async-start(f32[8,16,256]{2,1,0:T(8,128)} %spread.1), calls=%async_computation.1 | async-start | bytes 262144 | tf_op jit(solution)/shard_map/all_to_all | solution.py:373
  43.6 2.3 %collective-permute-done.2.refs_1_ = f32[32,2048]{1,0:T(8,128)S(1)} collective-permute-done((f32[32,2048]{1,0:T(8,128)S(1)}, f32[32,2048]{1,0:T(8,128)S(1)}, u32[]{:S(2)}, u32[]{:S(2)}) %collective-permute-start.2) | collective-permute-done | bytes 262176 | tf_op jit(solution)/shard_map/ppermute | solution.py:433
  45.9 2.3 %collective-permute-start = (f32[32,2048]{1,0:T(8,128)S(1)}, f32[32,2048]{1,0:T(8,128)S(1)}, u32[]{:S(2)}, u32[]{:S(2)}) collective-permute-start(f32[32,2048]{1,0:T(8,128)S(1)} %get-tuple-element.29), channel_id=1, source_target_pairs={{0,28},{4,24},{8,20},{12,16},{16,12},{20,8},{24,4},{28,0},{1,29},{... | collective-permute-start | bytes 786440 | tf_op jit(solution)/shard_map/ppermute | solution.py:433
  48.3 10.8 %collective-permute-start.1 = (f32[32,1280]{1,0:T(8,128)}, f32[32,1280]{1,0:T(8,128)S(1)}, u32[]{:S(2)}, u32[]{:S(2)}) collective-permute-start(f32[32,1280]{1,0:T(8,128)} %copy-done.3), channel_id=1, source_target_pairs={{0,16},{4,20},{8,24},{12,28},{16,0},{20,4},{24,8},{28,12},{1,17},{... | collective-permute-start | bytes 491528 | tf_op jit(solution)/shard_map/ppermute | solution.py:433
  59.1 1.9 %all-to-all-done.1.sources_ref = f32[8,16,256]{2,1,0:T(8,128)S(1)} async-done(((f32[8,16,256]{2,1,0:T(8,128)}), f32[8,16,256]{2,1,0:T(8,128)S(1)}, u32[]{:S(2)}, u32[]{:S(2)}) %all-to-all-start.1) | async-done | bytes 131104 | tf_op jit(solution)/shard_map/all_to_all | solution.py:373
  61.0 0.9 copy-done.7
  61.9 1.2 %copy-done.9 = f32[128,2048]{1,0:T(8,128)S(1)} copy-done((f32[128,2048]{1,0:T(8,128)S(1)}, f32[128,2048]{1,0:T(8,128)}, u32[]{:S(2)}) %copy-start.9) | copy-done | bytes 1048600
  63.2 3.4 %pairs.3 = (f32[128,1280]{1,0:T(8,128)S(1)}, f32[128,768]{1,0:T(8,128)S(1)}, f32[6,32]{1,0:T(8,128)S(1)}) custom-call(s32[1,2]{1,0:T(1,128)S(1)} %add_bitcast_fusion.here_ref, f32[8,24,256]{2,1,0:T(8,128)S(1)} %all-to-all-done.arrived_ref, f32[128,2048]{1,0:T(8,128)S(1)} %copy-done.9, f32[8,16,256]{2,1,0:T(8,128)S(1)} %all-to-all-done.1.sources_ref, ...), custom_call_target="tpu_custom_call" | custom-call | flops 2000000000 | bytes 5000000 | tf_op jit(solution)/shard_map/pairs/pallas_call | solution.py:495
  66.5 4.1 %collective-permute-done.1.refs_1_ = f32[32,1280]{1,0:T(8,128)S(1)} collective-permute-done((f32[32,1280]{1,0:T(8,128)}, f32[32,1280]{1,0:T(8,128)S(1)}, u32[]{:S(2)}, u32[]{:S(2)}) %collective-permute-start.1) | collective-permute-done | bytes 163872 | tf_op jit(solution)/shard_map/ppermute | solution.py:433
  70.6 1.8 %pairs.4 = (f32[64,1280]{1,0:T(8,128)S(1)}, f32[64,1280]{1,0:T(8,128)S(1)}, f32[2,32]{1,0:T(2,128)S(1)}) custom-call(s32[1,2]{1,0:T(1,128)S(1)} %add_bitcast_fusion.here_ref, f32[8,24,256]{2,1,0:T(8,128)S(1)} %all-to-all-done.arrived_ref, f32[128,2048]{1,0:T(8,128)S(1)} %copy-done.9, f32[8,16,256]{2,1,0:T(8,128)S(1)} %all-to-all-done.1.sources_ref, ...), custom_call_target="tpu_custom_call" | custom-call | flops 2000000000 | bytes 5000000 | tf_op jit(solution)/shard_map/pairs/pallas_call | solution.py:495
  72.6 1.5 %collective-permute-done.7.refs_1_ = f32[64,1280]{1,0:T(8,128)S(1)} collective-permute-done((f32[64,1280]{1,0:T(8,128)S(1)}, f32[64,1280]{1,0:T(8,128)S(1)}, u32[]{:S(2)}, u32[]{:S(2)}) %collective-permute-start.7) | collective-permute-done | bytes 327712 | tf_op jit(solution)/shard_map/ppermute | solution.py:377
  74.1 1.6 %collective-permute-start.8 = (f32[32,1280]{1,0:T(8,128)S(1)}, f32[32,1280]{1,0:T(8,128)S(1)}, u32[]{:S(2)}, u32[]{:S(2)}) collective-permute-start(f32[32,1280]{1,0:T(8,128)S(1)} %slice_add_fusion), channel_id=1, source_target_pairs={{0,2},{1,3},{2,0},{3,1},{4,6},{5,7},{6,4},{7,5},{8,10},{9,11},{10,... | collective-permute-start | bytes 491528 | tf_op jit(solution)/shard_map/ppermute | solution.py:377
  75.7 3.5 %collective-permute-done.9.refs_1_ = f32[32,768]{1,0:T(8,128)S(1)} collective-permute-done((f32[32,768]{1,0:T(8,128)S(1)}, f32[32,768]{1,0:T(8,128)S(1)}, u32[]{:S(2)}, u32[]{:S(2)}) %collective-permute-start.9) | collective-permute-done | bytes 98336 | tf_op jit(solution)/shard_map/ppermute | solution.py:433
  79.2 1.4 %pairs.5 = (f32[32,768]{1,0:T(8,128)S(1)}, f32[32,768]{1,0:T(8,128)S(1)}, f32[32,768]{1,0:T(8,128)S(1)}, f32[32,768]{1,0:T(8,128)S(1)}, f32[8,32]{1,0:T(8,128)S(1)}) custom-call(s32[1,2]{1,0:T(1,128)S(1)} %add_bitcast_fusion.here_ref, f32[8,24,256]{2,1,0:T(8,128)S(1)} %all-to-all-done.arrived_ref, f32[128,2048]{1,0:T(8,128)S(1)} %copy-done.9, ...), custom_call_target="tpu_custom_call" | custom-call | flops 2000000000 | bytes 5000000 | tf_op jit(solution)/shard_map/pairs/pallas_call | solution.py:495
  80.6 1.6 %collective-permute-start.10 = (f32[32,768]{1,0:T(8,128)S(1)}, f32[32,768]{1,0:T(8,128)S(1)}, u32[]{:S(2)}, u32[]{:S(2)}) collective-permute-start(f32[32,768]{1,0:T(8,128)S(1)} %get-tuple-element.45), channel_id=1, source_target_pairs={{0,2},{1,3},{2,0},{3,1},{4,6},{5,7},{6,4},{7,5},{8,10},{9,11},{10,... | collective-permute-start | bytes 294920 | tf_op jit(solution)/shard_map/ppermute | solution.py:377
  82.8 11.1 %all_to_all.21 = f32[8,1,32]{2,1,0:T(1,128)S(1)} all-to-all(f32[8,1,32]{2,1,0:T(1,128)S(1)} %bitcast.15), channel_id=1, replica_groups=mesh['chan'=8,'src'=4] {'chan'}, dimensions={0} | all-to-all | bytes 2048 | tf_op jit(solution)/shard_map/all_to_all | solution.py:373
  93.9 0.7 look.1
  94.7 4.8 %inverse.1 = f32[32,4096]{1,0:T(8,128)} custom-call(bf16[48,256]{1,0:T(8,128)(2,1)} %constant.31.clone.mix_ref, f32[128,128]{1,0:T(8,128)} %constant.32.clone.turn_cos_ref, f32[128,128]{1,0:T(8,128)} %constant.33.clone.turn_sin_ref, bf16[32,768]{1,0:T(8,128)(2,1)} %constant.34.clone.last_ref, f32[64,1280]{1,0:T(8,128)S(1)} %get-tuple-element.38.refs_0_, ...), custom_call_target="tpu_custom_call" | custom-call | flops 1000000000 | bytes 2000000 | tf_op jit(solution)/shard_map/inverse/pallas_call | solution.py:350
  (32 shorter events, 1.0 us)
Async XLA Ops:
  0.6 3.4 %copy-start = (bf16[128,4096]{1,0:T(8,128)(2,1)S(1)}, bf16[128,4096]{1,0:T(8,128)(2,1)}, u32[]{:S(2)}) copy-start(bf16[128,4096]{1,0:T(8,128)(2,1)} %records_ref.1) | copy-start | bytes 3145732
  1.6 1.2 %copy-start.1 = (f32[128,2048]{1,0:T(8,128)S(1)}, f32[128,2048]{1,0:T(8,128)}, u32[]{:S(2)}) copy-start(f32[128,2048]{1,0:T(8,128)} %observed_ref.3) | copy-start | bytes 3145732
  4.0 19.3 %copy-start.2 = (f32[128,2048]{1,0:T(8,128)S(1)}, f32[128,2048]{1,0:T(8,128)}, u32[]{:S(2)}) copy-start(f32[128,2048]{1,0:T(8,128)} %observed_ref.3) | copy-start | bytes 3145732
  11.3 1.0 copy-start.8
  12.2 27.3 %all-to-all-start = ((f32[8,24,256]{2,1,0:T(8,128)}), f32[8,24,256]{2,1,0:T(8,128)S(1)}, u32[]{:S(2)}, u32[]{:S(2)}) async-start(f32[8,24,256]{2,1,0:T(8,128)} %get-tuple-element.27), calls=%async_computation | async-start | bytes 393216 | tf_op jit(solution)/shard_map/all_to_all | solution.py:373
  19.5 26.4 %collective-permute-start.2 = (f32[32,2048]{1,0:T(8,128)S(1)}, f32[32,2048]{1,0:T(8,128)S(1)}, u32[]{:S(2)}, u32[]{:S(2)}) collective-permute-start(f32[32,2048]{1,0:T(8,128)S(1)} %get-tuple-element.32), channel_id=1, source_target_pairs={{0,20},{4,16},{8,28},{12,24},{16,4},{20,0},{24,12},{28,8},{1,21},{... | collective-permute-start | bytes 786440 | tf_op jit(solution)/shard_map/ppermute | solution.py:433
  25.4 0.7 copy-start.6
  26.1 14.1 %copy-start.3 = (f32[32,1280]{1,0:T(8,128)}, f32[32,1280]{1,0:T(8,128)S(1)}, u32[]{:S(2)}) copy-start(f32[32,1280]{1,0:T(8,128)S(1)} %get-tuple-element.30) | copy-start | bytes 491524
  26.1 14.1 %copy-start.4 = (f32[32,768]{1,0:T(8,128)}, f32[32,768]{1,0:T(8,128)S(1)}, u32[]{:S(2)}) copy-start(f32[32,768]{1,0:T(8,128)S(1)} %get-tuple-element.40) | copy-start | bytes 294916
  26.1 22.2 %collective-permute-start.3 = (f32[32,2048]{1,0:T(8,128)}, f32[32,2048]{1,0:T(8,128)S(1)}, u32[]{:S(2)}, u32[]{:S(2)}) collective-permute-start(f32[32,2048]{1,0:T(8,128)} %get-tuple-element.33), channel_id=1, source_target_pairs={{0,24},{4,28},{8,16},{12,20},{16,8},{20,12},{24,0},{28,4},{1,25},{... | collective-permute-start | bytes 786440 | tf_op jit(solution)/shard_map/ppermute | solution.py:433
  27.6 31.5 %collective-permute-start.4 = (f32[32,2048]{1,0:T(8,128)S(1)}, f32[32,2048]{1,0:T(8,128)S(1)}, u32[]{:S(2)}, u32[]{:S(2)}) collective-permute-start(f32[32,2048]{1,0:T(8,128)S(1)} %get-tuple-element.34), channel_id=1, source_target_pairs={{0,8},{4,12},{8,0},{12,4},{16,24},{20,28},{24,16},{28,20},{1,9},{5... | collective-permute-start | bytes 786440 | tf_op jit(solution)/shard_map/ppermute | solution.py:433
  27.6 31.5 %collective-permute-start.5 = (f32[32,2048]{1,0:T(8,128)S(1)}, f32[32,2048]{1,0:T(8,128)S(1)}, u32[]{:S(2)}, u32[]{:S(2)}) collective-permute-start(f32[32,2048]{1,0:T(8,128)S(1)} %get-tuple-element.35), channel_id=1, source_target_pairs={{0,12},{4,8},{8,4},{12,0},{16,28},{20,24},{24,20},{28,16},{1,13},{... | collective-permute-start | bytes 786440 | tf_op jit(solution)/shard_map/ppermute | solution.py:433
  29.6 29.5 %collective-permute-start.6 = (f32[32,2048]{1,0:T(8,128)S(1)}, f32[32,2048]{1,0:T(8,128)S(1)}, u32[]{:S(2)}, u32[]{:S(2)}) collective-permute-start(f32[32,2048]{1,0:T(8,128)S(1)} %get-tuple-element.36), channel_id=1, source_target_pairs={{0,4},{4,0},{8,12},{12,8},{16,20},{20,16},{24,28},{28,24},{1,5},{5... | collective-permute-start | bytes 786440 | tf_op jit(solution)/shard_map/ppermute | solution.py:433
  40.2 20.7 %all-to-all-start.1 = ((f32[8,16,256]{2,1,0:T(8,128)}), f32[8,16,256]{2,1,0:T(8,128)S(1)}, u32[]{:S(2)}, u32[]{:S(2)}) async-start(f32[8,16,256]{2,1,0:T(8,128)} %spread.1), calls=%async_computation.1 | async-start | bytes 262144 | tf_op jit(solution)/shard_map/all_to_all | solution.py:373
  45.9 24.7 %collective-permute-start = (f32[32,2048]{1,0:T(8,128)S(1)}, f32[32,2048]{1,0:T(8,128)S(1)}, u32[]{:S(2)}, u32[]{:S(2)}) collective-permute-start(f32[32,2048]{1,0:T(8,128)S(1)} %get-tuple-element.29), channel_id=1, source_target_pairs={{0,28},{4,24},{8,20},{12,16},{16,12},{20,8},{24,4},{28,0},{1,29},{... | collective-permute-start | bytes 786440 | tf_op jit(solution)/shard_map/ppermute | solution.py:433
  48.3 22.3 %collective-permute-start.1 = (f32[32,1280]{1,0:T(8,128)}, f32[32,1280]{1,0:T(8,128)S(1)}, u32[]{:S(2)}, u32[]{:S(2)}) collective-permute-start(f32[32,1280]{1,0:T(8,128)} %copy-done.3), channel_id=1, source_target_pairs={{0,16},{4,20},{8,24},{12,28},{16,0},{20,4},{24,8},{28,12},{1,17},{... | collective-permute-start | bytes 491528 | tf_op jit(solution)/shard_map/ppermute | solution.py:433
  61.0 1.0 copy-start.7
  61.9 1.2 %copy-start.9 = (f32[128,2048]{1,0:T(8,128)S(1)}, f32[128,2048]{1,0:T(8,128)}, u32[]{:S(2)}) copy-start(f32[128,2048]{1,0:T(8,128)} %copy-done.8) | copy-start | bytes 3145732
  70.6 1.9 %copy-start.5 = (f32[32,768]{1,0:T(8,128)S(1)}, f32[32,768]{1,0:T(8,128)}, u32[]{:S(2)}) copy-start(f32[32,768]{1,0:T(8,128)} %copy-done.4) | copy-start | bytes 294916
  72.4 1.7 %collective-permute-start.7 = (f32[64,1280]{1,0:T(8,128)S(1)}, f32[64,1280]{1,0:T(8,128)S(1)}, u32[]{:S(2)}, u32[]{:S(2)}) collective-permute-start(f32[64,1280]{1,0:T(8,128)S(1)} %get-tuple-element.39), channel_id=1, source_target_pairs={{0,1},{1,0},{2,3},{3,2},{4,5},{5,4},{6,7},{7,6},{8,9},{9,8},{10,11... | collective-permute-start | bytes 983048 | tf_op jit(solution)/shard_map/ppermute | solution.py:377
  72.5 6.7 %collective-permute-start.9 = (f32[32,768]{1,0:T(8,128)S(1)}, f32[32,768]{1,0:T(8,128)S(1)}, u32[]{:S(2)}, u32[]{:S(2)}) collective-permute-start(f32[32,768]{1,0:T(8,128)S(1)} %copy-done.5), channel_id=1, source_target_pairs={{0,16},{4,20},{8,24},{12,28},{16,0},{20,4},{24,8},{28,12},{1,17},{... | collective-permute-start | bytes 294920 | tf_op jit(solution)/shard_map/ppermute | solution.py:433
  74.1 20.5 %collective-permute-start.8 = (f32[32,1280]{1,0:T(8,128)S(1)}, f32[32,1280]{1,0:T(8,128)S(1)}, u32[]{:S(2)}, u32[]{:S(2)}) collective-permute-start(f32[32,1280]{1,0:T(8,128)S(1)} %slice_add_fusion), channel_id=1, source_target_pairs={{0,2},{1,3},{2,0},{3,1},{4,6},{5,7},{6,4},{7,5},{8,10},{9,11},{10,... | collective-permute-start | bytes 491528 | tf_op jit(solution)/shard_map/ppermute | solution.py:377
  80.6 14.0 %collective-permute-start.10 = (f32[32,768]{1,0:T(8,128)S(1)}, f32[32,768]{1,0:T(8,128)S(1)}, u32[]{:S(2)}, u32[]{:S(2)}) collective-permute-start(f32[32,768]{1,0:T(8,128)S(1)} %get-tuple-element.45), channel_id=1, source_target_pairs={{0,2},{1,3},{2,0},{3,1},{4,6},{5,7},{6,4},{7,5},{8,10},{9,11},{10,... | collective-permute-start | bytes 294920 | tf_op jit(solution)/shard_map/ppermute | solution.py:377
  82.2 12.4 %collective-permute-start.11 = (f32[32,768]{1,0:T(8,128)S(1)}, f32[32,768]{1,0:T(8,128)S(1)}, u32[]{:S(2)}, u32[]{:S(2)}) collective-permute-start(f32[32,768]{1,0:T(8,128)S(1)} %get-tuple-element.46), channel_id=1, source_target_pairs={{0,1},{1,0},{2,3},{3,2},{4,5},{5,4},{6,7},{7,6},{8,9},{9,8},{10,11... | collective-permute-start | bytes 294920 | tf_op jit(solution)/shard_map/ppermute | solution.py:377
  82.2 12.4 %collective-permute-start.12 = (f32[32,768]{1,0:T(8,128)S(1)}, f32[32,768]{1,0:T(8,128)S(1)}, u32[]{:S(2)}, u32[]{:S(2)}) collective-permute-start(f32[32,768]{1,0:T(8,128)S(1)} %get-tuple-element.47), channel_id=1, source_target_pairs={{0,3},{1,2},{2,1},{3,0},{4,7},{5,6},{6,5},{7,4},{8,11},{9,10},{10,... | collective-permute-start | bytes 294920 | tf_op jit(solution)/shard_map/ppermute | solution.py:377

commit v4 on v3

--- a/solution.py
+++ b/solution.py
@@ -12,8 +12,8 @@
 
 K0 = 64
 LANES = 128
-CUT = 5
-TOGETHER = 2
+CUT = 4
+TOGETHER = 4
 GRANT = pltpu.CompilerParams(vmem_limit_bytes=12 * 1024 * 1024)
 FIRST = (5,)
 SECOND = (6,)
@@ -134,6 +134,11 @@
         for group in range(picked_ref.shape[0]):
             picked_ref[group, :owners, :] = picked[:, group * part : (group + 1) * part]
         picked_ref[:, owners:, :] = label_ref[...]
+
+
+def stage_kernel(*refs):
+    for source, target in zip(refs[: len(refs) // 2], refs[len(refs) // 2 :]):
+        target[...] = source[...]
 
 
 def spread_kernel(arrived_ref, out_ref):
@@ -185,14 +190,13 @@
     gather2 = jnp.concatenate([gather2, gather2], axis=1)
     scatter2 = jnp.concatenate([scatter, scatter], axis=1)
     slots = gather.shape[0]
-    tile = 2 * LANES if all((last - first) % (2 * LANES) == 0 for first, last in spans) else LANES
-
-    def rows_of(left):
+
+    def rows_of(left, tile):
         hi, low = split2(white_ref[:, left : left + tile])
         return mm(gather2, jnp.concatenate([hi, low], axis=0))
 
-    def sources_of(left):
-        taken = min(tile, part)
+    def sources_of(left, tile):
+        taken = min(LANES, part)
         values = jnp.concatenate(
             [sources_ref[at // part, :, at % part : at % part + taken] for at in range(left, left + tile, taken)],
             axis=1,
@@ -205,38 +209,41 @@
         hi, low = split2(terms)
         return mm(scatter2, jnp.concatenate([hi, low], axis=0))
 
-    def seen(half, lo):
+    def seen(half, lo, tile):
         values = []
         for block in blocks:
             left = half * bins + lo if block.shape[1] == 2 * bins else half * total + lo - begin
             values.append(block[:, left : left + tile])
         return jnp.concatenate(values, axis=0)
 
-    misfit = jnp.zeros((slots, tile), F32)
+    misfit = jnp.zeros((slots, LANES), F32)
     for number, (first, last) in enumerate(spans):
         width = last - first
         mine = outs[sum(pieces[:number]) : sum(pieces[: number + 1])]
 
-        def put(left, value):
+        def put(left, tile, value):
             if starts:
                 value = value + begun[number][:, left : left + tile]
             size = rows // len(mine)
             for piece, ref in enumerate(mine):
                 ref[:, left : left + tile] = value[piece * size : (piece + 1) * size]
 
-        for at in range(0, width, tile):
+        for at in range(0, width, 2 * LANES):
+            tile = min(2 * LANES, width - at)
             lo = first + at
             index = lo + lax.broadcasted_iota(jnp.int32, (1, tile), 1)
             weights = 0.5 - 0.5 * jnp.cos((index.astype(F32) + 0.5) * (2.0 * math.pi / bins))
-            receiver_real, receiver_imag = rows_of(lo), rows_of(bins + lo)
-            source_real, source_imag = sources_of(lo), sources_of(bins + lo)
-            diff_real = source_real * receiver_real + source_imag * receiver_imag - seen(0, lo)
-            diff_imag = source_real * receiver_imag - source_imag * receiver_real - seen(1, lo)
+            receiver_real, receiver_imag = rows_of(lo, tile), rows_of(bins + lo, tile)
+            source_real, source_imag = sources_of(lo, tile), sources_of(bins + lo, tile)
+            diff_real = source_real * receiver_real + source_imag * receiver_imag - seen(0, lo, tile)
+            diff_imag = source_real * receiver_imag - source_imag * receiver_real - seen(1, lo, tile)
             residual_real = weights * diff_real
             residual_imag = weights * diff_imag
-            misfit = misfit + (residual_real * diff_real + residual_imag * diff_imag)
-            put(at, summed(residual_real * source_real - residual_imag * source_imag))
-            put(width + at, summed(residual_real * source_imag + residual_imag * source_real))
+            weighted = residual_real * diff_real + residual_imag * diff_imag
+            for lane in range(0, tile, LANES):
+                misfit = misfit + weighted[:, lane : lane + LANES]
+            put(at, tile, summed(residual_real * source_real - residual_imag * source_imag))
+            put(width + at, tile, summed(residual_real * source_imag + residual_imag * source_real))
     misfit = jnp.sum(misfit, axis=1, keepdims=True) / (2 * bins)
     index = lax.broadcasted_iota(jnp.int32, (slots, capacity), 0) % capacity
     spots = lax.broadcasted_iota(jnp.int32, (slots, capacity), 1)
@@ -281,7 +288,6 @@
     out_ref, held, wide = refs[-3:]
     count = out_ref.shape[0]
     blocks = held.shape[1] // 2
-    turns = turn_cos_ref.shape[1]
     at = 0
     for number, size in enumerate(sizes):
         addends = chunks[sum(sizes[:number]) : sum(sizes[: number + 1])]
@@ -298,14 +304,21 @@
     last = last_ref[...]
     turn_cos = turn_cos_ref[...]
     turn_sin = turn_sin_ref[...]
+    outer = last.shape[0] // 2
+    first_row = lax.broadcasted_iota(jnp.int32, (outer, LANES), 1) < LANES // 2
     for row in range(0, count, TOGETHER):
-        some = range(row, row + TOGETHER)
-        hi, low = split2(jnp.concatenate([held[i].T for i in some], axis=0))
-        mixed = mm(jnp.concatenate([hi, low, hi], axis=1), mix)
+        sides = []
+        for pair in range(row, row + TOGETHER, 2):
+            parts = []
+            for i in (pair, pair + 1):
+                hi, low = split2(held[i].T)
+                parts += [hi, low, hi]
+            sides.append(jnp.concatenate(parts, axis=1))
+        mixed = mm(jnp.concatenate(sides, axis=0), mix)
         his, lows = [], []
-        for i in range(TOGETHER):
-            real = mixed[i * LANES : (i + 1) * LANES, :turns]
-            imag = mixed[i * LANES : (i + 1) * LANES, turns:]
+        for i in range(TOGETHER // 2):
+            real = mixed[i * LANES : (i + 1) * LANES, :LANES]
+            imag = mixed[i * LANES : (i + 1) * LANES, LANES:]
             hi, low = split2(
                 jnp.concatenate(
                     [real * turn_cos - imag * turn_sin, real * turn_sin + imag * turn_cos], axis=0
@@ -315,8 +328,12 @@
             lows.append(low)
         hi, low = jnp.concatenate(his, axis=1), jnp.concatenate(lows, axis=1)
         values = mm(last, jnp.concatenate([hi, low, hi], axis=0))
-        for i, at in enumerate(some):
-            wide[at] = values[:, i * turns : (i + 1) * turns]
+        for i in range(TOGETHER // 2):
+            even = values[:outer, i * LANES : (i + 1) * LANES]
+            odd = values[outer:, i * LANES : (i + 1) * LANES]
+            at = row + 2 * i
+            wide[at] = jnp.where(first_row, even, pltpu.roll(odd, LANES // 2, 1))
+            wide[at + 1] = jnp.where(first_row, pltpu.roll(even, LANES // 2, 1), odd)
     for block in range(wide.shape[1]):
         out_ref[:, block * LANES : (block + 1) * LANES] = wide[:, block, :] * scale
 
@@ -326,25 +343,31 @@
     return hi, (values - hi.astype(np.float64)).astype(jnp.bfloat16)
 
 
-def inverse(spectra, count, time_len, bins):
+def inverse_tables(time_len, bins):
     period = 2 * time_len
     blocks = bins // LANES
     steps = period // LANES
-    turns = LANES
-    outer = time_len // turns
-    cos, sin = phases(np.arange(steps)[:, None] * np.arange(blocks)[None, :] * LANES, period)
-    mix = np.concatenate(
-        [np.concatenate([cos, -sin], axis=1)] * (turns // steps)
-        + [np.concatenate([sin, cos], axis=1)] * (turns // steps),
-        axis=0,
-    ).T
-    hi, low = bf16_parts(mix)
-    mix = np.concatenate([hi, hi, low], axis=0)
-    r = np.arange(LANES)
-    turn_cos, turn_sin = phases((K0 + r)[:, None] * np.arange(turns)[None, :], period)
-    cos, sin = phases((K0 + r)[None, :] * np.arange(outer)[:, None] * turns, period)
+    assert 2 * steps == LANES
+    outer = time_len // steps
+    b, r = np.arange(steps), np.arange(LANES)
+    cos, sin = phases(b[None, :] * np.arange(blocks)[:, None] * LANES, period)
+    columns = []
+    for part in (np.concatenate([cos, -sin]), np.concatenate([sin, cos])):
+        hi, low = bf16_parts(part)
+        columns.append(np.concatenate([hi, hi, low]))
+    real, imag = columns
+    none = np.zeros_like(real)
+    mix = np.block([[real, none, imag, none], [none, real, none, imag]]).astype(real.dtype)
+    turn_cos, turn_sin = phases((K0 + r)[:, None] * np.tile(b, 2)[None, :], period)
+    a = np.concatenate([np.arange(0, outer, 2), np.arange(1, outer, 2)])
+    cos, sin = phases((K0 + r)[None, :] * a[:, None] * steps, period)
     hi, low = bf16_parts(np.concatenate([cos, -sin], axis=1))
     last = np.concatenate([hi, hi, low], axis=1)
+    return mix, np.float32(turn_cos), np.float32(turn_sin), last
+
+
+def inverse(tables, spectra, count, time_len, bins):
+    blocks = bins // LANES
     chunks = [value for addends in spectra for value in addends]
     sizes = [len(addends) for addends in spectra]
     return pl.pallas_call(
@@ -354,13 +377,13 @@
         out_specs=VMEM,
         scratch_shapes=[
             pltpu.VMEM((count, 2 * blocks, LANES), F32),
-            pltpu.VMEM((count, outer, LANES), F32),
+            pltpu.VMEM((count, time_len // LANES, LANES), F32),
         ],
         compiler_params=GRANT,
         cost_estimate=pl.CostEstimate(flops=1_000_000_000, bytes_accessed=2_000_000, transcendentals=0),
         name="inverse",
     )(
-        in_hbm(mix), in_hbm(np.float32(turn_cos)), in_hbm(np.float32(turn_sin)), in_hbm(last),
+        *tables,
         *chunks,
     )
 
@@ -456,7 +479,7 @@
         functools.partial(forward_kernel, steps),
         grid=(steps,),
         out_shape=[
-            jax.ShapeDtypeStruct((row_count, 2 * bins), F32),
+            pltpu.HBM((row_count, 2 * bins), F32),
             jax.ShapeDtypeStruct((groups, owners + 8, part), F32),
         ],
         in_specs=[
@@ -503,6 +526,17 @@
             cost_estimate=pl.CostEstimate(flops=2_000_000_000, bytes_accessed=5_000_000, transcendentals=0),
             name="pairs",
         )(here, arrived, whitened, sources, *values, *begun, *before)
+
+    tables = inverse_tables(time_len, bins)
+    tables = pl.pallas_call(
+        stage_kernel,
+        out_shape=[jax.ShapeDtypeStruct(table.shape, table.dtype) for table in tables],
+        in_specs=[VMEM] * 4,
+        out_specs=[VMEM] * 4,
+        compiler_params=GRANT,
+        cost_estimate=pl.CostEstimate(flops=1000, bytes_accessed=1_000_000, transcendentals=0),
+        name="stage",
+    )(*[in_hbm(table) for table in tables])
 
     if routed:
         for tag, value in zip(rest, sent):
@@ -525,7 +559,7 @@
         spectra = [rows_in_two(*sums[:2]), rows_in_two(*sums[2:])]
 
     returned = exchange(misfit, "chan")
-    result = inverse(spectra, row_count // 4, time_len, bins)
+    result = inverse(tables, spectra, row_count // 4, time_len, bins)
     pair_misfit = pl.pallas_call(
         look_kernel,
         out_shape=jax.ShapeDtypeStruct((1, pair_count), F32),

time: 100 us -> 95.5 us (0.955)
  blocking collectives: 11.1 us -> 0 us
  waiting for transfers between devices: 21.8 us -> 31.2 us
  starting transfers between devices: 36.5 us -> 34.8 us
    all_to_all x1 -> x0, blocking collectives: 11.1 us -> none  [exchange(): return lax.all_to_all(value, axis, split_axis=0, concat_axis=0, tiled=True)]
    all_to_all x2 -> x3, waiting for transfers between devices: 10.4 us -> 20.2 us  [exchange(): return lax.all_to_all(value, axis, split_axis=0, concat_axis=0, tiled=True)]
    ppermute x8, starting transfers between devices: 22 us -> 16.9 us  [move(): return lax.ppermute(value, 'chan', [(i, i ^ tag) for i in range(groups)])]
    all_to_all x2 -> x3, starting transfers between devices: 10.7 us -> 14.1 us  [exchange(): return lax.all_to_all(value, axis, split_axis=0, concat_axis=0, tiled=True)]
    ppermute x5, waiting for transfers between devices: 1.54 us -> 0.01 us  [over_src(): return lax.ppermute(value, 'src', [(i, i ^ step) for i in range(4)])]
    pallas_call x1, Pallas kernels: 4.84 us -> 3.49 us  [inverse(): pl.pallas_call(functools.partial(inverse_kernel, 1.0 / math.sqrt(bins), s...]
    ppermute x8, waiting for transfers between devices: 9.89 us -> 11 us  [move(): return lax.ppermute(value, 'chan', [(i, i ^ tag) for i in range(groups)])]
    pallas_call x0 -> x1, Pallas kernels: none -> 1.02 us  [per_device(): pl.pallas_call(stage_kernel, out_shape=[jax.ShapeDtypeStruct(table.shape,...]
  transfers between devices with their start and end apart: 15 -> 16, of which waited for: 6 -> 6; matrix products, arithmetic and copies ran while one was open for 0% -> 0% of each run, Pallas kernels for 8% -> 11%
where the time goes in v4:
time: 95.5 us; the launch traced here: 94.9 us
  starting transfers between devices  34.8 us (36%)
  waiting for transfers between devices  31.2 us (33%)
  Pallas kernels  22.5 us (24%)
  local copies, waits for them, and re-layouts  4.85 us (5%)
    all_to_all x3, waiting for transfers between devices, exchange(): return lax.all_to_all(value, axis, split_axis=0, concat_axis=0, tiled=True)  20.2 us
    ppermute x8, starting transfers between devices, move(): return lax.ppermute(value, 'chan', [(i, i ^ tag) for i in range(groups)])  16.9 us
    all_to_all x3, starting transfers between devices, exchange(): return lax.all_to_all(value, axis, split_axis=0, concat_axis=0, tiled=True)  14.1 us
    ppermute x8, waiting for transfers between devices, move(): return lax.ppermute(value, 'chan', [(i, i ^ tag) for i in range(groups)])  11 us
    pallas_call x1, Pallas kernels, per_device(): pl.pallas_call(functools.partial(forward_kernel, steps), grid=(steps,), o...  7.62 us
    pallas_call x3, Pallas kernels, terms(): pl.pallas_call(functools.partial(pair_kernel, bins, some, tags, not route...  5.67 us
    unnamed x18, local copies, waits for them, and re-layouts  4.76 us
    ppermute x5, starting transfers between devices, over_src(): return lax.ppermute(value, 'src', [(i, i ^ step) for i in range(4)])  3.8 us
  transfers between devices with their start and end apart: 16, of which 6 were waited for; matrix products, arithmetic and copies ran while one was open for 0% of the time, Pallas kernels for 11%

profile of v4, /device:TPU:0, one launch (start us, length us, event | category | flops | bytes accessed | tf_op | source)
XLA Modules:
  0.0 94.9 jit_solution(10674395563738715416)
XLA Ops:
  0.6 0.7 subtract_bitcast_fusion
  1.6 1.2 %copy-done.1 = f32[128,2048]{1,0:T(8,128)S(1)} copy-done((f32[128,2048]{1,0:T(8,128)S(1)}, f32[128,2048]{1,0:T(8,128)}, u32[]{:S(2)}) %copy-start.1) | copy-done | bytes 1048600
  2.8 1.2 %pack.2 = (f32[32,2048]{1,0:T(8,128)S(1)}, f32[8,8,256]{2,1,0:T(8,128)S(1)}, s32[1,128]{1,0:T(1,128)S(1)}) custom-call(s32[1,2]{1,0:T(1,128)S(1)} %add_bitcast_fusion.here_ref, s32[1,128]{1,0:T(1,128)} %bitcast.16, s32[1,128]{1,0:T(1,128)} %bitcast.18, s32[1,128]{1,0:T(1,128)} %bitcast.20, f32[128,2048]{1,0:T(8,128)S(1)} %copy-done.1), custom_call_target="tpu_custom_call" | custom-call | flops 400000000 | bytes 3000000 | tf_op jit(solution)/shard_map/pack/pallas_call | solution.py:445
  4.0 7.6 %forward.1 = (f32[128,2048]{1,0:T(8,128)}, f32[8,24,256]{2,1,0:T(8,128)}) custom-call(bf16[128,4096]{1,0:T(8,128)(2,1)S(1)} %copy-done, f32[64,1024]{1,0:T(8,128)} %constant.27.clone.cos_a_ref, f32[64,1024]{1,0:T(8,128)} %constant.28.clone.sin_a_ref, f32[64,1024]{1,0:T(8,128)} %constant.29.clone.cos_b_ref, f32[64,1024]{1,0:T(8,128)} %constant.30.clone.sin_b_ref, ...), custom_call_target="tpu_custom_call" | custom-call | flops 8000000000 | bytes 4000000 | tf_op jit(solution)/shard_map/forward/pallas_call | solution.py:478
  11.7 7.3 %all-to-all-start = ((f32[8,24,256]{2,1,0:T(8,128)}), f32[8,24,256]{2,1,0:T(8,128)S(1)}, u32[]{:S(2)}, u32[]{:S(2)}) async-start(f32[8,24,256]{2,1,0:T(8,128)} %get-tuple-element.35), calls=%async_computation | async-start | bytes 393216 | tf_op jit(solution)/shard_map/all_to_all | solution.py:396
  18.9 2.1 %pack.3 = (f32[32,2048]{1,0:T(8,128)S(1)}, f32[32,2048]{1,0:T(8,128)}, f32[32,2048]{1,0:T(8,128)S(1)}, f32[32,2048]{1,0:T(8,128)S(1)}, f32[32,2048]{1,0:T(8,128)...) custom-call(s32[1,2]{1,0:T(1,128)S(1)} %add_bitcast_fusion.here_ref, ...), custom_call_target="tpu_custom_call" | custom-call | flops 400000000 | bytes 3000000 | tf_op jit(solution)/shard_map/pack/pallas_call | solution.py:445
  21.0 0.6 copy-done.3
  21.7 0.7 copy-done.6
  22.4 3.8 %collective-permute-start.3 = (f32[32,2048]{1,0:T(8,128)S(1)}, f32[32,2048]{1,0:T(8,128)S(1)}, u32[]{:S(2)}, u32[]{:S(2)}) collective-permute-start(f32[32,2048]{1,0:T(8,128)S(1)} %get-tuple-element.41), channel_id=1, source_target_pairs={{0,24},{4,28},{8,16},{12,20},{16,8},{20,12},{24,0},{28,4},{1,25},{... | collective-permute-start | bytes 786440 | tf_op jit(solution)/shard_map/ppermute | solution.py:456
  26.2 2.9 %collective-permute-start.5 = (f32[32,2048]{1,0:T(8,128)S(1)}, f32[32,2048]{1,0:T(8,128)S(1)}, u32[]{:S(2)}, u32[]{:S(2)}) collective-permute-start(f32[32,2048]{1,0:T(8,128)S(1)} %get-tuple-element.43), channel_id=1, source_target_pairs={{0,12},{4,8},{8,4},{12,0},{16,28},{20,24},{24,20},{28,16},{1,13},{... | collective-permute-start | bytes 786440 | tf_op jit(solution)/shard_map/ppermute | solution.py:456
  30.2 1.3 %all-to-all-done.arrived_ref = f32[8,24,256]{2,1,0:T(8,128)S(1)} async-done(((f32[8,24,256]{2,1,0:T(8,128)}), f32[8,24,256]{2,1,0:T(8,128)S(1)}, u32[]{:S(2)}, u32[]{:S(2)}) %all-to-all-start) | async-done | bytes 196640 | tf_op jit(solution)/shard_map/all_to_all | solution.py:396
  31.5 0.7 spread.1
  32.2 3.5 %all-to-all-start.1 = ((f32[8,16,256]{2,1,0:T(8,128)}), f32[8,16,256]{2,1,0:T(8,128)S(1)}, u32[]{:S(2)}, u32[]{:S(2)}) async-start(f32[8,16,256]{2,1,0:T(8,128)} %spread.1), calls=%async_computation.1 | async-start | bytes 262144 | tf_op jit(solution)/shard_map/all_to_all | solution.py:396
  35.7 4.7 %collective-permute-start = (f32[32,2048]{1,0:T(8,128)S(1)}, f32[32,2048]{1,0:T(8,128)S(1)}, u32[]{:S(2)}, u32[]{:S(2)}) collective-permute-start(f32[32,2048]{1,0:T(8,128)S(1)} %get-tuple-element.37), channel_id=1, source_target_pairs={{0,28},{4,24},{8,20},{12,16},{16,12},{20,8},{24,4},{28,0},{1,29},{... | collective-permute-start | bytes 786440 | tf_op jit(solution)/shard_map/ppermute | solution.py:456
  40.4 4.4 %collective-permute-start.1 = (f32[32,1024]{1,0:T(8,128)}, f32[32,1024]{1,0:T(8,128)S(1)}, u32[]{:S(2)}, u32[]{:S(2)}) collective-permute-start(f32[32,1024]{1,0:T(8,128)} %copy-done.5), channel_id=1, source_target_pairs={{0,16},{4,20},{8,24},{12,28},{16,0},{20,4},{24,8},{28,12},{1,17},{... | collective-permute-start | bytes 393224 | tf_op jit(solution)/shard_map/ppermute | solution.py:456
  44.8 6.1 %collective-permute-done.5.refs_4_ = f32[32,2048]{1,0:T(8,128)S(1)} collective-permute-done((f32[32,2048]{1,0:T(8,128)S(1)}, f32[32,2048]{1,0:T(8,128)S(1)}, u32[]{:S(2)}, u32[]{:S(2)}) %collective-permute-start.5) | collective-permute-done | bytes 262176 | tf_op jit(solution)/shard_map/ppermute | solution.py:456
  50.9 13.6 %all-to-all-done.1.sources_ref = f32[8,16,256]{2,1,0:T(8,128)S(1)} async-done(((f32[8,16,256]{2,1,0:T(8,128)}), f32[8,16,256]{2,1,0:T(8,128)S(1)}, u32[]{:S(2)}, u32[]{:S(2)}) %all-to-all-start.1) | async-done | bytes 131104 | tf_op jit(solution)/shard_map/all_to_all | solution.py:396
  64.5 0.9 copy-done.7
  65.4 1.2 %copy-done.8 = f32[128,2048]{1,0:T(8,128)S(1)} copy-done((f32[128,2048]{1,0:T(8,128)S(1)}, f32[128,2048]{1,0:T(8,128)}, u32[]{:S(2)}) %copy-start.8) | copy-done | bytes 1048600
  66.7 2.5 %pairs.3 = (f32[128,1024]{1,0:T(8,128)S(1)}, f32[128,1024]{1,0:T(8,128)S(1)}, f32[6,32]{1,0:T(8,128)S(1)}) custom-call(s32[1,2]{1,0:T(1,128)S(1)} %add_bitcast_fusion.here_ref, f32[8,24,256]{2,1,0:T(8,128)S(1)} %all-to-all-done.arrived_ref, f32[128,2048]{1,0:T(8,128)S(1)} %copy-done.8, f32[8,16,256]{2,1,0:T(8,128)S(1)} %all-to-all-done.1.sources_ref, ...), custom_call_target="tpu_custom_call" | custom-call | flops 2000000000 | bytes 5000000 | tf_op jit(solution)/shard_map/pairs/pallas_call | solution.py:518
  69.2 3.7 %collective-permute-done.1.refs_1_ = f32[32,1024]{1,0:T(8,128)S(1)} collective-permute-done((f32[32,1024]{1,0:T(8,128)}, f32[32,1024]{1,0:T(8,128)S(1)}, u32[]{:S(2)}, u32[]{:S(2)}) %collective-permute-start.1) | collective-permute-done | bytes 131104 | tf_op jit(solution)/shard_map/ppermute | solution.py:456
  72.9 1.3 %pairs.4 = (f32[64,1024]{1,0:T(8,128)S(1)}, f32[64,1024]{1,0:T(8,128)S(1)}, f32[2,32]{1,0:T(2,128)S(1)}) custom-call(s32[1,2]{1,0:T(1,128)S(1)} %add_bitcast_fusion.here_ref, f32[8,24,256]{2,1,0:T(8,128)S(1)} %all-to-all-done.arrived_ref, f32[128,2048]{1,0:T(8,128)S(1)} %copy-done.8, f32[8,16,256]{2,1,0:T(8,128)S(1)} %all-to-all-done.1.sources_ref, ...), custom_call_target="tpu_custom_call" | custom-call | flops 2000000000 | bytes 5000000 | tf_op jit(solution)/shard_map/pairs/pallas_call | solution.py:518
  74.3 1.1 %collective-permute-done.9.refs_1_ = f32[32,1024]{1,0:T(8,128)S(1)} collective-permute-done((f32[32,1024]{1,0:T(8,128)S(1)}, f32[32,1024]{1,0:T(8,128)S(1)}, u32[]{:S(2)}, u32[]{:S(2)}) %collective-permute-start.9) | collective-permute-done | bytes 131104 | tf_op jit(solution)/shard_map/ppermute | solution.py:456
  75.5 1.8 %pairs.5 = (f32[32,1024]{1,0:T(8,128)S(1)}, f32[32,1024]{1,0:T(8,128)S(1)}, f32[32,1024]{1,0:T(8,128)S(1)}, f32[32,1024]{1,0:T(8,128)S(1)}, f32[8,32]{1,0:T(8,128)}) custom-call(s32[1,2]{1,0:T(1,128)S(1)} %add_bitcast_fusion.here_ref, f32[8,24,256]{2,1,0:T(8,128)S(1)} %all-to-all-done.arrived_ref, f32[128,2048]{1,0:T(8,128)S(1)} %copy-done.8, ...), custom_call_target="tpu_custom_call" | custom-call | flops 2000000000 | bytes 5000000 | tf_op jit(solution)/shard_map/pairs/pallas_call | solution.py:518
  77.3 1.5 %collective-permute-start.10 = (f32[32,1024]{1,0:T(8,128)S(1)}, f32[32,1024]{1,0:T(8,128)S(1)}, u32[]{:S(2)}, u32[]{:S(2)}) collective-permute-start(f32[32,1024]{1,0:T(8,128)S(1)} %get-tuple-element.53), channel_id=1, source_target_pairs={{0,2},{1,3},{2,0},{3,1},{4,6},{5,7},{6,4},{7,5},{8,10},{9,11},{10,... | collective-permute-start | bytes 393224 | tf_op jit(solution)/shard_map/ppermute | solution.py:400
  78.8 0.6 collective-permute-start.12
  79.5 1.6 %collective-permute-start.8 = (f32[32,1024]{1,0:T(8,128)S(1)}, f32[32,1024]{1,0:T(8,128)S(1)}, u32[]{:S(2)}, u32[]{:S(2)}) collective-permute-start(f32[32,1024]{1,0:T(8,128)S(1)} %slice_add_fusion), channel_id=1, source_target_pairs={{0,2},{1,3},{2,0},{3,1},{4,6},{5,7},{6,4},{7,5},{8,10},{9,11},{10,... | collective-permute-start | bytes 393224 | tf_op jit(solution)/shard_map/ppermute | solution.py:400
  81.0 3.3 %all-to-all-start.2 = ((f32[8,1,32]{2,1,0:T(1,128)}), f32[8,1,32]{2,1,0:T(1,128)S(1)}, u32[]{:S(2)}, u32[]{:S(2)}) async-start(f32[8,1,32]{2,1,0:T(1,128)} %bitcast.8), calls=%async_computation.2 | async-start | bytes 8192 | tf_op jit(solution)/shard_map/all_to_all | solution.py:396
  84.4 1.0 %stage.1 = (bf16[96,256]{1,0:T(8,128)(2,1)S(1)}, f32[128,128]{1,0:T(8,128)S(1)}, f32[128,128]{1,0:T(8,128)S(1)}, bf16[64,768]{1,0:T(8,128)(2,1)S(1)}) custom-call(bf16[96,256]{1,0:T(8,128)(2,1)} %constant.31.clone.refs_0_, f32[128,128]{1,0:T(8,128)} %constant.32.clone.refs_1_, f32[128,128]{1,0:T(8,128)} %constant.33.clone.refs_2_, ...), custom_call_target="tpu_custom_call" | custom-call | flops 1000 | bytes 1000000 | tf_op jit(solution)/shard_map/stage/pallas_call | solution.py:531
  85.4 5.3 %all-to-all-done.2 = f32[8,1,32]{2,1,0:T(1,128)S(1)} async-done(((f32[8,1,32]{2,1,0:T(1,128)}), f32[8,1,32]{2,1,0:T(1,128)S(1)}, u32[]{:S(2)}, u32[]{:S(2)}) %all-to-all-start.2) | async-done | bytes 1056 | tf_op jit(solution)/shard_map/all_to_all | solution.py:396
  90.7 0.7 look.1
  91.5 3.5 %inverse.1 = f32[32,4096]{1,0:T(8,128)} custom-call(bf16[96,256]{1,0:T(8,128)(2,1)S(1)} %get-tuple-element.30.mix_ref, f32[128,128]{1,0:T(8,128)S(1)} %get-tuple-element.31.turn_cos_ref, f32[128,128]{1,0:T(8,128)S(1)} %get-tuple-element.32.turn_sin_ref, bf16[64,768]{1,0:T(8,128)(2,1)S(1)} %get-tuple-element.33.last_ref, ...), custom_call_target="tpu_custom_call" | custom-call | flops 1000000000 | bytes 2000000 | tf_op jit(solution)/shard_map/inverse/pallas_call | solution.py:373
  (32 shorter events, 1.4 us)
Async XLA Ops:
  0.6 3.4 %copy-start = (bf16[128,4096]{1,0:T(8,128)(2,1)S(1)}, bf16[128,4096]{1,0:T(8,128)(2,1)}, u32[]{:S(2)}) copy-start(bf16[128,4096]{1,0:T(8,128)(2,1)} %records_ref.1) | copy-start | bytes 3145732
  1.6 1.2 %copy-start.1 = (f32[128,2048]{1,0:T(8,128)S(1)}, f32[128,2048]{1,0:T(8,128)}, u32[]{:S(2)}) copy-start(f32[128,2048]{1,0:T(8,128)} %observed_ref.3) | copy-start | bytes 3145732
  4.0 14.9 %copy-start.2 = (f32[128,2048]{1,0:T(8,128)S(1)}, f32[128,2048]{1,0:T(8,128)}, u32[]{:S(2)}) copy-start(f32[128,2048]{1,0:T(8,128)} %observed_ref.3) | copy-start | bytes 3145732
  11.7 19.8 %all-to-all-start = ((f32[8,24,256]{2,1,0:T(8,128)}), f32[8,24,256]{2,1,0:T(8,128)S(1)}, u32[]{:S(2)}, u32[]{:S(2)}) async-start(f32[8,24,256]{2,1,0:T(8,128)} %get-tuple-element.35), calls=%async_computation | async-start | bytes 393216 | tf_op jit(solution)/shard_map/all_to_all | solution.py:396
  21.0 0.6 copy-start.3
  21.7 0.7 copy-start.6
  22.4 9.8 %copy-start.5 = (f32[32,1024]{1,0:T(8,128)}, f32[32,1024]{1,0:T(8,128)S(1)}, u32[]{:S(2)}) copy-start(f32[32,1024]{1,0:T(8,128)S(1)} %get-tuple-element.38) | copy-start | bytes 393220
  22.4 13.3 %collective-permute-start.3 = (f32[32,2048]{1,0:T(8,128)S(1)}, f32[32,2048]{1,0:T(8,128)S(1)}, u32[]{:S(2)}, u32[]{:S(2)}) collective-permute-start(f32[32,2048]{1,0:T(8,128)S(1)} %get-tuple-element.41), channel_id=1, source_target_pairs={{0,24},{4,28},{8,16},{12,20},{16,8},{20,12},{24,0},{28,4},{1,25},{... | collective-permute-start | bytes 786440 | tf_op jit(solution)/shard_map/ppermute | solution.py:456
  26.2 14.2 %collective-permute-start.4 = (f32[32,2048]{1,0:T(8,128)}, f32[32,2048]{1,0:T(8,128)S(1)}, u32[]{:S(2)}, u32[]{:S(2)}) collective-permute-start(f32[32,2048]{1,0:T(8,128)} %get-tuple-element.42), channel_id=1, source_target_pairs={{0,8},{4,12},{8,0},{12,4},{16,24},{20,28},{24,16},{28,20},{1,9},{5... | collective-permute-start | bytes 786440 | tf_op jit(solution)/shard_map/ppermute | solution.py:456
  26.2 24.7 %collective-permute-start.5 = (f32[32,2048]{1,0:T(8,128)S(1)}, f32[32,2048]{1,0:T(8,128)S(1)}, u32[]{:S(2)}, u32[]{:S(2)}) collective-permute-start(f32[32,2048]{1,0:T(8,128)S(1)} %get-tuple-element.43), channel_id=1, source_target_pairs={{0,12},{4,8},{8,4},{12,0},{16,28},{20,24},{24,20},{28,16},{1,13},{... | collective-permute-start | bytes 786440 | tf_op jit(solution)/shard_map/ppermute | solution.py:456
  29.1 21.8 %collective-permute-start.6 = (f32[32,2048]{1,0:T(8,128)S(1)}, f32[32,2048]{1,0:T(8,128)S(1)}, u32[]{:S(2)}, u32[]{:S(2)}) collective-permute-start(f32[32,2048]{1,0:T(8,128)S(1)} %get-tuple-element.44), channel_id=1, source_target_pairs={{0,4},{4,0},{8,12},{12,8},{16,20},{20,16},{24,28},{28,24},{1,5},{5... | collective-permute-start | bytes 786440 | tf_op jit(solution)/shard_map/ppermute | solution.py:456
  29.7 21.2 %collective-permute-start.2 = (f32[32,2048]{1,0:T(8,128)S(1)}, f32[32,2048]{1,0:T(8,128)S(1)}, u32[]{:S(2)}, u32[]{:S(2)}) collective-permute-start(f32[32,2048]{1,0:T(8,128)S(1)} %get-tuple-element.40), channel_id=1, source_target_pairs={{0,20},{4,16},{8,28},{12,24},{16,4},{20,0},{24,12},{28,8},{1,21},{... | collective-permute-start | bytes 786440 | tf_op jit(solution)/shard_map/ppermute | solution.py:456
  32.2 18.7 %copy-start.4 = (f32[32,1024]{1,0:T(8,128)S(1)}, f32[32,1024]{1,0:T(8,128)}, u32[]{:S(2)}) copy-start(f32[32,1024]{1,0:T(8,128)} %copy-done.3) | copy-start | bytes 393220
  32.2 32.3 %all-to-all-start.1 = ((f32[8,16,256]{2,1,0:T(8,128)}), f32[8,16,256]{2,1,0:T(8,128)S(1)}, u32[]{:S(2)}, u32[]{:S(2)}) async-start(f32[8,16,256]{2,1,0:T(8,128)} %spread.1), calls=%async_computation.1 | async-start | bytes 262144 | tf_op jit(solution)/shard_map/all_to_all | solution.py:396
  35.7 37.2 %collective-permute-start = (f32[32,2048]{1,0:T(8,128)S(1)}, f32[32,2048]{1,0:T(8,128)S(1)}, u32[]{:S(2)}, u32[]{:S(2)}) collective-permute-start(f32[32,2048]{1,0:T(8,128)S(1)} %get-tuple-element.37), channel_id=1, source_target_pairs={{0,28},{4,24},{8,20},{12,16},{16,12},{20,8},{24,4},{28,0},{1,29},{... | collective-permute-start | bytes 786440 | tf_op jit(solution)/shard_map/ppermute | solution.py:456
  40.4 32.6 %collective-permute-start.1 = (f32[32,1024]{1,0:T(8,128)}, f32[32,1024]{1,0:T(8,128)S(1)}, u32[]{:S(2)}, u32[]{:S(2)}) collective-permute-start(f32[32,1024]{1,0:T(8,128)} %copy-done.5), channel_id=1, source_target_pairs={{0,16},{4,20},{8,24},{12,28},{16,0},{20,4},{24,8},{28,12},{1,17},{... | collective-permute-start | bytes 393224 | tf_op jit(solution)/shard_map/ppermute | solution.py:456
  50.9 24.6 %collective-permute-start.9 = (f32[32,1024]{1,0:T(8,128)S(1)}, f32[32,1024]{1,0:T(8,128)S(1)}, u32[]{:S(2)}, u32[]{:S(2)}) collective-permute-start(f32[32,1024]{1,0:T(8,128)S(1)} %copy-done.4), channel_id=1, source_target_pairs={{0,16},{4,20},{8,24},{12,28},{16,0},{20,4},{24,8},{28,12},{1,17},{... | collective-permute-start | bytes 393224 | tf_op jit(solution)/shard_map/ppermute | solution.py:456
  64.5 1.0 %copy-start.7 = (f32[32,2048]{1,0:T(8,128)S(1)}, f32[32,2048]{1,0:T(8,128)}, u32[]{:S(2)}) copy-start(f32[32,2048]{1,0:T(8,128)} %copy-done.6) | copy-start | bytes 786436
  65.4 1.2 %copy-start.8 = (f32[128,2048]{1,0:T(8,128)S(1)}, f32[128,2048]{1,0:T(8,128)}, u32[]{:S(2)}) copy-start(f32[128,2048]{1,0:T(8,128)} %get-tuple-element.36.white_ref) | copy-start | bytes 3145732
  74.2 5.2 %collective-permute-start.7 = (f32[64,1024]{1,0:T(8,128)S(1)}, f32[64,1024]{1,0:T(8,128)S(1)}, u32[]{:S(2)}, u32[]{:S(2)}) collective-permute-start(f32[64,1024]{1,0:T(8,128)S(1)} %get-tuple-element.47), channel_id=1, source_target_pairs={{0,1},{1,0},{2,3},{3,2},{4,5},{5,4},{6,7},{7,6},{8,9},{9,8},{10,11... | collective-permute-start | bytes 786440 | tf_op jit(solution)/shard_map/ppermute | solution.py:400
  77.3 14.1 %collective-permute-start.10 = (f32[32,1024]{1,0:T(8,128)S(1)}, f32[32,1024]{1,0:T(8,128)S(1)}, u32[]{:S(2)}, u32[]{:S(2)}) collective-permute-start(f32[32,1024]{1,0:T(8,128)S(1)} %get-tuple-element.53), channel_id=1, source_target_pairs={{0,2},{1,3},{2,0},{3,1},{4,6},{5,7},{6,4},{7,5},{8,10},{9,11},{10,... | collective-permute-start | bytes 393224 | tf_op jit(solution)/shard_map/ppermute | solution.py:400
  78.8 12.6 %collective-permute-start.11 = (f32[32,1024]{1,0:T(8,128)S(1)}, f32[32,1024]{1,0:T(8,128)S(1)}, u32[]{:S(2)}, u32[]{:S(2)}) collective-permute-start(f32[32,1024]{1,0:T(8,128)S(1)} %get-tuple-element.54), channel_id=1, source_target_pairs={{0,1},{1,0},{2,3},{3,2},{4,5},{5,4},{6,7},{7,6},{8,9},{9,8},{10,11... | collective-permute-start | bytes 393224 | tf_op jit(solution)/shard_map/ppermute | solution.py:400
  78.8 12.6 %collective-permute-start.12 = (f32[32,1024]{1,0:T(8,128)S(1)}, f32[32,1024]{1,0:T(8,128)S(1)}, u32[]{:S(2)}, u32[]{:S(2)}) collective-permute-start(f32[32,1024]{1,0:T(8,128)S(1)} %get-tuple-element.55), channel_id=1, source_target_pairs={{0,3},{1,2},{2,1},{3,0},{4,7},{5,6},{6,5},{7,4},{8,11},{9,10},{10,... | collective-permute-start | bytes 393224 | tf_op jit(solution)/shard_map/ppermute | solution.py:400
  79.5 12.0 %collective-permute-start.8 = (f32[32,1024]{1,0:T(8,128)S(1)}, f32[32,1024]{1,0:T(8,128)S(1)}, u32[]{:S(2)}, u32[]{:S(2)}) collective-permute-start(f32[32,1024]{1,0:T(8,128)S(1)} %slice_add_fusion), channel_id=1, source_target_pairs={{0,2},{1,3},{2,0},{3,1},{4,6},{5,7},{6,4},{7,5},{8,10},{9,11},{10,... | collective-permute-start | bytes 393224 | tf_op jit(solution)/shard_map/ppermute | solution.py:400
  81.0 9.7 %all-to-all-start.2 = ((f32[8,1,32]{2,1,0:T(1,128)}), f32[8,1,32]{2,1,0:T(1,128)S(1)}, u32[]{:S(2)}, u32[]{:S(2)}) async-start(f32[8,1,32]{2,1,0:T(1,128)} %bitcast.8), calls=%async_computation.2 | async-start | bytes 8192 | tf_op jit(solution)/shard_map/all_to_all | solution.py:396
